TPU v7x, 32 devices: a whole 2x2x4 slice. The times are simulated.
32 devices in a mesh: dp: 16 (over z, y, x), seq: 2 (over core).
Axes of the slice: x: 2, y: 2, z: 4, core: 2. Of those that a mesh axis runs over, the one named last changes fastest.
Arguments:
- hidden_in: bfloat16 [2, 16, 512, 768], P(None, 'dp', 'seq'), may hold values from -6 to 6
- cotangent: bfloat16 [2, 16, 512, 768], P(None, 'dp', 'seq'), may hold values from -6 to 6
- attention_keep: int32 [2, 16, 12, 512, 128], P(None, 'dp', None, 'seq'), may hold values from 0 to 4095
- output_keep: int32 [2, 16, 512, 192], P(None, 'dp', 'seq'), may hold values from 0 to 4095
- feed_keep: int32 [2, 16, 512, 192], P(None, 'dp', 'seq'), may hold values from 0 to 4095
- qkv_weight: bfloat16 [768, 2304], P(('dp', 'seq')), may hold values from -0.21875 to 0.21875
- qkv_bias: bfloat16 [1536], P(('dp', 'seq')), may hold values from -3 to 3
- out_weight: bfloat16 [768, 768], P(('dp', 'seq')), may hold values from -3 to 3
- out_bias: bfloat16 [768], P(('dp', 'seq')), may hold values from -3 to 3
- first_gain: bfloat16 [768], P(('dp', 'seq')), may hold values from 0.099609375 to 1.8984375
- first_shift: bfloat16 [768], P(('dp', 'seq')), may hold values from -3 to 3
- up_weight: bfloat16 [768, 3072], P(('dp', 'seq')), may hold values from -0.21875 to 0.21875
- up_bias: bfloat16 [3072], P(('dp', 'seq')), may hold values from -3 to 3
- down_weight: bfloat16 [3072, 768], P(('dp', 'seq')), may hold values from -0.109375 to 0.109375
- down_bias: bfloat16 [768], P(('dp', 'seq')), may hold values from -3 to 3
- second_gain: bfloat16 [768], P(('dp', 'seq')), may hold values from 0.099609375 to 1.8984375
- second_shift: bfloat16 [768], P(('dp', 'seq')), may hold values from -3 to 3
Outputs:
- layer_out: bfloat16 [2, 16, 512, 768], P(None, 'dp', 'seq')
- grad_input: bfloat16 [2, 16, 512, 768], P(None, 'dp', 'seq')
- grad_qkv_weight: float32 [768, 2304], P(('dp', 'seq'))
- grad_qkv_bias: float32 [1536], P(('dp', 'seq'))
- grad_out_weight: float32 [768, 768], P(('dp', 'seq'))
- grad_out_bias: float32 [768], P(('dp', 'seq'))
- grad_first_gain: float32 [768], P(('dp', 'seq'))
- grad_first_shift: float32 [768], P(('dp', 'seq'))
- grad_up_weight: float32 [768, 3072], P(('dp', 'seq'))
- grad_up_bias: float32 [3072], P(('dp', 'seq'))
- grad_down_weight: float32 [3072, 768], P(('dp', 'seq'))
- grad_down_bias: float32 [768], P(('dp', 'seq'))
- grad_second_gain: float32 [768], P(('dp', 'seq'))
- grad_second_shift: float32 [768], P(('dp', 'seq'))
Inputs may be any that keep to these rules, and one draw needn't show every extreme that they name: `attention_keep`: each word packs four 3-bit values, lowest bits first. `output_keep`: each word packs four 3-bit values, lowest bits first. `feed_keep`: each word packs four 3-bit values, lowest bits first.
All inputs are finite; a program needn't handle non-finite values.
Results may differ from a plain program's by a relative error of at most 0.015.
Values may be sent and summed in bfloat16 or wider, within the bound.
No kernel may reach another device: no remote copies, remote signals or barrier semaphores. Data moves between devices by JAX's collectives and lax.ppermute only.
A program may use at most 192 MiB of HBM per device.

v0:
```python
import functools

import jax
import jax.numpy as jnp
from jax import lax
from jax.experimental import pallas as pl
from jax.experimental.pallas import tpu as pltpu
from jax.sharding import Mesh
from jax.sharding import PartitionSpec as P

H = 12
epsilon = 1e-12
keep_scale = 8.0 / 7.0
root_half = 0.7071067811865476
inverse_root_tau = 0.3989422804014327
every = ("z", "y", "x", "seq")
f32 = jnp.float32
bf16 = jnp.bfloat16


def unpack_keep(packed_words):
    shifts = jnp.arange(4, dtype=jnp.int32) * 3
    nibble = jnp.right_shift(packed_words[..., None], shifts) & 7
    keep_value = (nibble >= 1).astype(jnp.float32) * keep_scale
    return keep_value.reshape(packed_words.shape[:-1] + (packed_words.shape[-1] * 4,))


def normalize(values, norm_gain, norm_shift):
    centred = values - jnp.mean(values, axis=-1, keepdims=True)
    inverse = lax.rsqrt(jnp.mean(centred * centred, axis=-1, keepdims=True) + epsilon)
    scaled = centred * inverse
    return (scaled * norm_gain + norm_shift, scaled, inverse)


def norm_back(upstream, scaled, inverse, norm_gain):
    weighted = upstream * norm_gain
    centre_term = jnp.mean(weighted, axis=-1, keepdims=True)
    slope_term = jnp.mean(weighted * scaled, axis=-1, keepdims=True)
    return inverse * (weighted - centre_term - scaled * slope_term)


def gelu_slope(inner_sum):
    normal_cdf = 0.5 * (1.0 + lax.erf(inner_sum * root_half))
    density = jnp.exp(-0.5 * inner_sum * inner_sum) * inverse_root_tau
    return normal_cdf + inner_sum * density


def matmul(left_side, right_side):
    return jnp.dot(left_side, right_side, preferred_element_type=jnp.float32)


def plain_local(
    hidden_in,
    cotangent,
    attention_keep,
    output_keep,
    feed_keep,
    qkv_weight,
    qkv_bias,
    out_weight,
    out_bias,
    first_gain,
    first_shift,
    up_weight,
    up_bias,
    down_weight,
    down_bias,
    second_gain,
    second_shift,
):
    model_width = hidden_in.shape[-1]
    sequence_count = hidden_in.shape[1]
    local_tokens = hidden_in.shape[2]
    token_rows = sequence_count * local_tokens
    head_count = H
    head_size = model_width // head_count
    held_params = (
        lax.all_gather(qkv_weight, every, axis=0, tiled=True),
        lax.all_gather(qkv_bias, every, axis=0, tiled=True),
        lax.all_gather(out_weight, every, axis=0, tiled=True),
        lax.all_gather(out_bias, every, axis=0, tiled=True),
        lax.all_gather(first_gain, every, axis=0, tiled=True),
        lax.all_gather(first_shift, every, axis=0, tiled=True),
        lax.all_gather(up_weight, every, axis=0, tiled=True),
        lax.all_gather(up_bias, every, axis=0, tiled=True),
        lax.all_gather(down_weight, every, axis=0, tiled=True),
        lax.all_gather(down_bias, every, axis=0, tiled=True),
        lax.all_gather(second_gain, every, axis=0, tiled=True),
        lax.all_gather(second_shift, every, axis=0, tiled=True),
    )
    totals = None
    outputs = []
    inputs_grad = []
    for micro_step in range(hidden_in.shape[0]):
        (
            full_qkv_w,
            full_qkv_b,
            full_out_w,
            full_out_b,
            full_gain_one,
            full_shift_one,
            full_up_w,
            full_up_b,
            full_down_w,
            full_down_b,
            full_gain_two,
            full_shift_two,
        ) = held_params
        rows_in = hidden_in[micro_step].reshape(token_rows, model_width)
        qkv_float = full_qkv_b.astype(jnp.float32)
        bias_full = jnp.concatenate(
            [
                qkv_float[:model_width],
                jnp.zeros((model_width,), jnp.float32),
                qkv_float[model_width:],
            ]
        )
        projected = (matmul(rows_in, full_qkv_w) + bias_full).astype(jnp.bfloat16)
        queries = projected[:, :model_width].reshape(
            sequence_count, local_tokens, head_count, head_size
        )
        keys_local = projected[:, model_width : 2 * model_width].reshape(
            sequence_count, local_tokens, model_width
        )
        values_local = projected[:, 2 * model_width :].reshape(
            sequence_count, local_tokens, model_width
        )
        keys_all, values_all = (
            lax.all_gather(keys_local, "seq", axis=1, tiled=True),
            lax.all_gather(values_local, "seq", axis=1, tiled=True),
        )
        keys_heads = keys_all.reshape(sequence_count, -1, head_count, head_size)
        values_heads = values_all.reshape(sequence_count, -1, head_count, head_size)
        scores = (
            jnp.einsum("sqhd,skhd->shqk", queries, keys_heads, preferred_element_type=jnp.float32)
            * 0.125
        )
        row_peak = jnp.max(scores, axis=-1, keepdims=True)
        exponent = jnp.exp(scores - row_peak)
        row_total = jnp.sum(exponent, axis=-1, keepdims=True)
        log_total = row_peak + jnp.log(row_total)
        softmax_weights = exponent / row_total
        keep_attention = unpack_keep(attention_keep[micro_step])
        dropped = (softmax_weights * keep_attention).astype(jnp.bfloat16)
        context = jnp.einsum(
            "shqk,skhd->sqhd", dropped, values_heads, preferred_element_type=jnp.float32
        )
        context = context.reshape(token_rows, model_width).astype(jnp.bfloat16)
        attended = matmul(context, full_out_w) + full_out_b.astype(jnp.float32)
        keep_output = unpack_keep(output_keep[micro_step]).reshape(token_rows, model_width)
        first_sum = rows_in.astype(jnp.float32) + attended * keep_output
        gain_one = full_gain_one.astype(jnp.float32)
        normed, scaled_one, inverse_one = normalize(
            first_sum, gain_one, full_shift_one.astype(jnp.float32)
        )
        normed_low = normed.astype(jnp.bfloat16)
        inner_sum = matmul(normed_low, full_up_w) + full_up_b.astype(jnp.float32)
        activated = jax.nn.gelu(inner_sum, approximate=False).astype(jnp.bfloat16)
        outer_sum = matmul(activated, full_down_w) + full_down_b.astype(jnp.float32)
        keep_feed = unpack_keep(feed_keep[micro_step]).reshape(token_rows, model_width)
        second_sum = normed + outer_sum * keep_feed
        gain_two = full_gain_two.astype(jnp.float32)
        result, scaled_two, inverse_two = normalize(
            second_sum, gain_two, full_shift_two.astype(jnp.float32)
        )
        outputs.append(
            result.astype(jnp.bfloat16).reshape(sequence_count, local_tokens, model_width)
        )
        (
            back_qkv_w,
            back_qkv_b,
            back_out_w,
            back_out_b,
            back_gain_one,
            back_shift_one,
            back_up_w,
            back_up_b,
            back_down_w,
            back_down_b,
            back_gain_two,
            back_shift_two,
        ) = held_params
        upstream = cotangent[micro_step].reshape(token_rows, model_width).astype(jnp.float32)
        g_second = norm_back(upstream, scaled_two, inverse_two, back_gain_two.astype(jnp.float32))
        grad_gain_two = jnp.sum(upstream * scaled_two, axis=0)
        grad_shift_two = jnp.sum(upstream, axis=0)
        g_outer = (g_second * keep_feed).astype(jnp.bfloat16)
        grad_down_b = jnp.sum(g_outer.astype(jnp.float32), axis=0)
        grad_down_w = matmul(activated.T, g_outer)
        g_inner = (matmul(g_outer, back_down_w.T) * gelu_slope(inner_sum)).astype(jnp.bfloat16)
        grad_up_b = jnp.sum(g_inner.astype(jnp.float32), axis=0)
        grad_up_w = matmul(normed_low.T, g_inner)
        g_normed = g_second + matmul(g_inner, back_up_w.T)
        g_first = norm_back(g_normed, scaled_one, inverse_one, back_gain_one.astype(jnp.float32))
        grad_gain_one = jnp.sum(g_normed * scaled_one, axis=0)
        grad_shift_one = jnp.sum(g_normed, axis=0)
        g_attended = (g_first * keep_output).astype(jnp.bfloat16)
        grad_out_b = jnp.sum(g_attended.astype(jnp.float32), axis=0)
        grad_out_w = matmul(context.T, g_attended)
        g_context = matmul(g_attended, back_out_w.T).astype(jnp.bfloat16)
        g_context = g_context.reshape(sequence_count, local_tokens, head_count, head_size)
        keys_again, values_again = (
            lax.all_gather(keys_local, "seq", axis=1, tiled=True),
            lax.all_gather(values_local, "seq", axis=1, tiled=True),
        )
        keys_heads = keys_again.reshape(sequence_count, -1, head_count, head_size)
        values_heads = values_again.reshape(sequence_count, -1, head_count, head_size)
        scores_again = (
            jnp.einsum("sqhd,skhd->shqk", queries, keys_heads, preferred_element_type=jnp.float32)
            * 0.125
        )
        weights_again = jnp.exp(scores_again - log_total)
        dropped_again = (weights_again * keep_attention).astype(jnp.bfloat16)
        g_values_all = jnp.einsum(
            "shqk,sqhd->skhd", dropped_again, g_context, preferred_element_type=jnp.float32
        )
        g_dropped = jnp.einsum(
            "sqhd,skhd->shqk", g_context, values_heads, preferred_element_type=jnp.float32
        )
        g_weights = g_dropped * keep_attention
        row_delta = jnp.sum(g_weights * weights_again, axis=-1, keepdims=True)
        g_scores = (weights_again * (g_weights - row_delta)).astype(jnp.bfloat16)
        g_queries = (
            jnp.einsum("shqk,skhd->sqhd", g_scores, keys_heads, preferred_element_type=jnp.float32)
            * 0.125
        )
        g_keys_all = (
            jnp.einsum("shqk,sqhd->skhd", g_scores, queries, preferred_element_type=jnp.float32)
            * 0.125
        )
        g_keys, g_values = (
            lax.psum_scatter(
                g_keys_all.reshape(sequence_count, -1, model_width).astype(jnp.bfloat16),
                "seq",
                scatter_dimension=1,
                tiled=True,
            ).astype(jnp.float32),
            lax.psum_scatter(
                g_values_all.reshape(sequence_count, -1, model_width).astype(jnp.bfloat16),
                "seq",
                scatter_dimension=1,
                tiled=True,
            ).astype(jnp.float32),
        )
        g_projected = jnp.concatenate(
            [
                g_queries.reshape(token_rows, model_width),
                g_keys.reshape(token_rows, model_width),
                g_values.reshape(token_rows, model_width),
            ],
            axis=1,
        ).astype(jnp.bfloat16)
        g_projected_float = g_projected.astype(jnp.float32)
        grad_qkv_b = jnp.concatenate(
            [
                jnp.sum(g_projected_float[:, :model_width], axis=0),
                jnp.sum(g_projected_float[:, 2 * model_width :], axis=0),
            ]
        )
        grad_qkv_w = matmul(rows_in.T, g_projected)
        input_grad = g_first + matmul(g_projected, back_qkv_w.T)
        inputs_grad.append(
            input_grad.astype(jnp.bfloat16).reshape(sequence_count, local_tokens, model_width)
        )
        grads_now = (
            grad_qkv_w,
            grad_qkv_b,
            grad_out_w,
            grad_out_b,
            grad_gain_one,
            grad_shift_one,
            grad_up_w,
            grad_up_b,
            grad_down_w,
            grad_down_b,
            grad_gain_two,
            grad_shift_two,
        )
        if totals is None:
            totals = grads_now
        else:
            totals = tuple((before + added for before, added in zip(totals, grads_now)))
    summed = (
        lax.psum_scatter(totals[0], every, scatter_dimension=0, tiled=True),
        lax.psum_scatter(totals[1], every, scatter_dimension=0, tiled=True),
        lax.psum_scatter(totals[2], every, scatter_dimension=0, tiled=True),
        lax.psum_scatter(totals[3], every, scatter_dimension=0, tiled=True),
        lax.psum_scatter(totals[4], every, scatter_dimension=0, tiled=True),
        lax.psum_scatter(totals[5], every, scatter_dimension=0, tiled=True),
        lax.psum_scatter(totals[6], every, scatter_dimension=0, tiled=True),
        lax.psum_scatter(totals[7], every, scatter_dimension=0, tiled=True),
        lax.psum_scatter(totals[8], every, scatter_dimension=0, tiled=True),
        lax.psum_scatter(totals[9], every, scatter_dimension=0, tiled=True),
        lax.psum_scatter(totals[10], every, scatter_dimension=0, tiled=True),
        lax.psum_scatter(totals[11], every, scatter_dimension=0, tiled=True),
    )
    return (
        jnp.stack(outputs, axis=0),
        jnp.stack(inputs_grad, axis=0),
        summed[0],
        summed[1],
        summed[2],
        summed[3],
        summed[4],
        summed[5],
        summed[6],
        summed[7],
        summed[8],
        summed[9],
        summed[10],
        summed[11],
    )


ANY = pl.BlockSpec(memory_space=pl.ANY)
WHOLE = pl.BlockSpec(memory_space=pltpu.VMEM)
MIB = 2**20
PARTS = (2, 1)
GROUP = 2


def dot_t(left_side, right_side):
    return lax.dot_general(left_side, right_side, (((1,), (1,)), ((), ())), preferred_element_type=f32)


def t_dot(left_side, right_side):
    return lax.dot_general(left_side, right_side, (((0,), (0,)), ((), ())), preferred_element_type=f32)


def iota(shape, axis):
    return lax.broadcasted_iota(jnp.int32, shape, axis)


def pp(value, axis, step=1):
    size = lax.axis_size(axis)
    return lax.ppermute(value, axis, [(i, i ^ step) for i in range(size)])


def pick(value, axis, index):
    return lax.dynamic_index_in_dim(value, index, axis, keepdims=False)


def after(value, *earlier):
    return lax.optimization_barrier((value,) + earlier)[0]


def hold(values, *earlier):
    return lax.optimization_barrier(tuple(values) + earlier)[: len(values)]


def add_up(terms):
    total = terms[0].astype(f32)
    for term in terms[1:]:
        total = total + term.astype(f32)
    return total


def divide(plan, cut):
    parts = []
    for start, rows, out, row, column in plan:
        ends = [start, cut, start + rows] if start < cut < start + rows else [start, start + rows]
        for first, last in zip(ends, ends[1:]):
            parts.append((first, last - first, out, row + first - start, column))
    return parts


def whole(number, first, array):
    return (number, first, array, 0, array.shape[1])


def at_core(piece):
    number, first, array, row, rows = piece
    return (number + 4, first, pp(array, "seq"), row, rows)


class Weights:
    def __init__(self, pieces, plan, shapes):
        arrays = []
        self.spans = []
        for number, first, array, row, rows in pieces:
            place = next((i for i, held in enumerate(arrays) if held is array), len(arrays))
            if place == len(arrays):
                arrays.append(array)
            self.spans.append((number, first, place, row, rows))
        self.operands = [pltpu.with_memory_space_constraint(array, pltpu.HBM) for array in arrays]
        self.plan, self.shapes = plan, shapes
        self.specs = [pl.BlockSpec(memory_space=pltpu.HBM)] * len(arrays)
        self.scratch = [pltpu.VMEM((4, 2, 2, 2, rows, columns), bf16) for rows, columns in shapes]
        self.scratch.append(pltpu.SemaphoreType.DMA((8 * len(plan),)))

    def copies(self, ids, sources, places, sems):
        found = [[] for _ in self.shapes]
        count = 0
        for start, rows, out, row, column in self.plan:
            for number, first, place, source_row, held in self.spans:
                if first <= start and start + rows <= first + held:
                    c = ids[0] ^ (number >> 2)
                    y = ids[1] ^ ((number >> 1) & 1)
                    x = ids[2] ^ (number & 1)
                    source = sources[place]
                    src = source.at[:, pl.ds(source_row + start - first, rows), :]
                    dst = places[out].at[:, y, x, c, pl.ds(row, rows), pl.ds(column, source.shape[2])]
                    found[out].append(pltpu.make_async_copy(src, dst, sems.at[count]))
                    count += 1
        return found

    def matrix(self, places, out):
        rows, columns = self.shapes[out]
        return places[out].reshape(32 * rows, columns)


def begin(copies):
    for group in copies:
        for copy in group:
            copy.start()


def finish(group):
    for copy in group:
        copy.wait()


def spread(block, row, count, per):
    values = block[:, row, : -(-per // 128) * 128].astype(bf16)
    lanes = values.shape[1]
    select = (iota((lanes, count), 1) % per == iota((lanes, count), 0)).astype(bf16)
    wide = jnp.dot(values, select, preferred_element_type=f32)
    return jnp.sum(jnp.where(iota(wide.shape, 1) // per == iota(wide.shape, 0), wide, 0.0), axis=0, keepdims=True)


def unspread(vectors, pers, block, first=0):
    block[:, first:] = jnp.zeros((32, 8 - first, block.shape[2]), f32)
    for row, (vector, per) in enumerate(zip(vectors, pers), first):
        count = vector.shape[1]
        lanes = -(-per // 128) * 128
        shape = (32, count)
        wide = jnp.where(iota(shape, 1) // per == iota(shape, 0), vector, 0.0).astype(bf16)
        select = (iota((count, lanes), 0) % per == iota((count, lanes), 1)).astype(bf16)
        block[:, row, :lanes] = jnp.dot(wide, select, preferred_element_type=f32)


def layer_norm(values):
    centred = values - jnp.mean(values, axis=-1, keepdims=True)
    inverse = lax.rsqrt(jnp.mean(centred * centred, axis=-1, keepdims=True) + epsilon)
    return centred * inverse, inverse


def turn_matrix(tokens):
    place = iota((tokens, tokens), 0)
    quarter = tokens // 4
    return (iota((tokens, tokens), 1) == 4 * (place % quarter) + place // quarter).astype(bf16)


def call(body, name, grid, operands, specs, outs, out_specs, scratch, room, load, aliases=None):
    return pl.pallas_call(
        body,
        grid_spec=pltpu.PrefetchScalarGridSpec(
            num_scalar_prefetch=1, grid=grid, in_specs=specs, out_specs=out_specs, scratch_shapes=scratch
        ),
        out_shape=outs,
        compiler_params=pltpu.CompilerParams(vmem_limit_bytes=room * MIB),
        cost_estimate=pl.CostEstimate(flops=1024, bytes_accessed=load * MIB // 16, transcendentals=0),
        input_output_aliases=aliases or {},
        name=name,
    )(*operands)


def shaped(shape, dtype):
    return jax.ShapeDtypeStruct(shape, dtype)


def rows_spec(rows, columns):
    return pl.BlockSpec((rows, columns), lambda i, ids: (i, 0))


def fixed_spec(shape):
    return pl.BlockSpec(shape, lambda i, ids: (0,) * len(shape))


def prepare_body(ids, hidden, output_words, feed_words, turned, keep_output, keep_feed):
    tokens, width = hidden.shape
    turned[...] = jnp.dot(turn_matrix(tokens), hidden[...], preferred_element_type=f32).astype(bf16)
    quarter = width // 4
    for words, keep in ((output_words, keep_output), (feed_words, keep_feed)):
        packed = words[0, 0]
        total = jnp.zeros((tokens, width), f32)
        for i in range(4):
            bit = ((packed & (7 << (3 * i))) != 0).astype(f32).astype(bf16)
            place = (iota((quarter, width), 1) == 4 * iota((quarter, width), 0) + i).astype(bf16)
            total = total + t_dot(bit, place)
        keep[...] = total.astype(bf16)


def prepare(ids, hidden, output_words, feed_words, tokens):
    rows, width = hidden.shape
    wide = rows_spec(tokens, width)
    narrow = pl.BlockSpec((1, 1, width // 4, tokens), lambda i, ids: (i, 0, 0, 0))
    return call(
        prepare_body,
        "prepare",
        (rows // tokens,),
        (ids, hidden, output_words, feed_words),
        [wide, narrow, narrow],
        [shaped((rows, width), bf16)] * 3,
        [wide] * 3,
        [],
        12,
        6,
    )


def project_body(weights, per, ids, *refs):
    count = len(weights.operands)
    sources, (hidden, turned, queries), rest = refs[:count], refs[count : count + 3], refs[count + 3 :]
    micro, tokens, width = queries.shape
    places, sems = rest[len(rest) - 1 - len(weights.shapes) : -1], rest[-1]
    near = iter(rest[: len(rest) - 1 - len(weights.shapes)])
    copies = weights.copies(ids, sources, places, sems)
    begin(copies)
    finish(copies[3])
    block = weights.matrix(places, 3)[:, :128].astype(f32).reshape(32, 8, 128)
    bias = spread(block, 0, 2 * width, per)
    for n in range(3):
        finish(copies[n])
    for m in range(micro):
        natural, other = hidden[m * tokens : (m + 1) * tokens, :], turned[m * tokens : (m + 1) * tokens, :]
        q = jnp.dot(natural, weights.matrix(places, 0)[...], preferred_element_type=f32) + bias[:, :width]
        queries[m] = q.astype(bf16)
        k = jnp.dot(other, weights.matrix(places, 1)[...], preferred_element_type=f32).astype(bf16)
        v = jnp.dot(other, weights.matrix(places, 2)[...], preferred_element_type=f32) + bias[:, width:]
        for value in (k, v.astype(bf16)):
            rows = tokens // PARTS[m]
            for part in range(PARTS[m]):
                next(near)[...] = value[part * rows : (part + 1) * rows]


def project(ids, weights, hidden, turned, micro, per):
    rows, width = hidden.shape
    return call(
        functools.partial(project_body, weights, per),
        "project",
        (1,),
        (ids, *weights.operands, hidden, turned),
        weights.specs + [WHOLE] * 2,
        [shaped((micro, rows // micro, width), bf16)]
        + [shaped((rows // micro // PARTS[m], width), bf16) for m in range(micro) for _ in range(2 * PARTS[m])],
        [WHOLE] * (1 + 2 * sum(PARTS)),
        weights.scratch,
        16,
        10,
    )


def lane_half(shape):
    return iota(shape, len(shape) - 1) < 64


def by_head(pair):
    left, zero = lane_half(pair.shape), jnp.zeros_like(pair)
    return jnp.concatenate([jnp.where(left, pair, zero), jnp.where(left, zero, pair)], axis=0)


def join_keys(core, near, far, buffer, lanes):
    quarter = buffer.shape[0] // 8
    parts = len(near)
    for i in range(4):
        here = pl.multiple_of((2 * i + core) * quarter, quarter)
        there = pl.multiple_of((2 * i + 1 - core) * quarter, quarter)
        at = (i * parts % 4) // parts * quarter
        buffer[pl.ds(here, quarter), :] = near[i * parts // 4][at : at + quarter, lanes]
        buffer[pl.ds(there, quarter), :] = far[i * parts // 4][at : at + quarter, lanes]


def group_lanes():
    return [slice(j * 128, (j + 1) * 128) for j in range(GROUP)]


def attention_body(parts, ids, q, *refs):
    ours, words = refs[: 4 * parts], refs[4 * parts]
    context, signed, keys, values = refs[-4:]
    core = ids[0]
    tokens = q.shape[1]
    for j, lanes in enumerate(group_lanes()):
        join_keys(core, ours[:parts], ours[2 * parts : 3 * parts], keys.at[j], lanes)
        join_keys(core, ours[parts : 2 * parts], ours[3 * parts :], values.at[j], lanes)
    scores = [dot_t(by_head(q[0, :, lanes]) * 0.125, keys[j]) for j, lanes in enumerate(group_lanes())]
    for j, lanes in enumerate(group_lanes()):
        blocks = [scores[j][:, i * 128 : (i + 1) * 128] for i in range(4)]
        peak = jnp.maximum(jnp.maximum(blocks[0], blocks[1]), jnp.maximum(blocks[2], blocks[3]))
        peak = jnp.max(peak, axis=1, keepdims=True)
        blocks = [jnp.exp(block - peak) for block in blocks]
        total = jnp.sum((blocks[0] + blocks[1]) + (blocks[2] + blocks[3]), axis=1, keepdims=True)
        scale = 1.0 / total
        word = words[0, 2 * j : 2 * j + 2].reshape(2 * tokens, 128)
        dropped = []
        for i in range(4):
            weight = blocks[i] * scale
            keep = (word & (7 << (3 * i))) != 0
            weight = jnp.where(keep, weight, -weight).astype(bf16)
            signed[0, j, i] = weight
            dropped.append(jnp.maximum(weight, jnp.zeros_like(weight)))
        out = jnp.dot(jnp.concatenate(dropped, axis=1), values[j], preferred_element_type=f32) * keep_scale
        context[0, :, lanes] = jnp.where(lane_half((tokens, 128)), out[:tokens], out[tokens:]).astype(bf16)


def attention(ids, m, queries, near, far, words, earlier=()):
    micro, tokens, width = queries.shape
    pairs = width // 128
    part = pl.BlockSpec((1, tokens, 128 * GROUP), lambda p, ids: (m, 0, p))
    flat = pl.BlockSpec((tokens // PARTS[m], 128 * GROUP), lambda p, ids: (0, p))
    operands = (ids, queries, *near[m], *far[m], words)
    return call(
        functools.partial(attention_body, PARTS[m]),
        "attention",
        (pairs // GROUP,),
        operands + tuple(earlier),
        [part] + [flat] * (4 * PARTS[m])
        + [pl.BlockSpec((1, 2 * GROUP, tokens, 128), lambda p, ids: (m, p, 0, 0))]
        + [ANY] * len(earlier),
        [shaped((micro, tokens, width), bf16), shaped((micro, pairs, 4, 2 * tokens, 128), bf16)],
        [part, pl.BlockSpec((1, GROUP, 4, 2 * tokens, 128), lambda p, ids: (m, p, 0, 0, 0))],
        [pltpu.VMEM((GROUP, 2 * tokens, 128), bf16)] * 2,
        16,
        14,
        {len(operands) + i: i for i in range(len(earlier))},
    )


def attention_back_body(parts, ids, q, *refs):
    ours, signed, upstream, refs = refs[: 4 * parts], refs[4 * parts], refs[4 * parts + 1], refs[4 * parts + 2 :]
    g_q, *grads, keys, values, sums = refs
    g_near, g_far = grads[:2], grads[2:]
    core = ids[0]
    tokens = q.shape[1]
    for j, lanes in enumerate(group_lanes()):
        join_keys(core, ours[:parts], ours[2 * parts : 3 * parts], keys.at[j], lanes)
        join_keys(core, ours[parts : 2 * parts], ours[3 * parts :], values.at[j], lanes)
    aboves = [by_head(upstream[:, lanes]) for lanes in group_lanes()]
    g_droppeds = [dot_t(aboves[j], values[j]) for j in range(GROUP)]
    for j, lanes in enumerate(group_lanes()):
        weights, kept, g_weights = [], [], []
        delta = None
        for i in range(4):
            both_signs = signed[0, j, i].astype(f32)
            weight = jnp.abs(both_signs)
            g_weight = jnp.where(both_signs > 0.0, g_droppeds[j][:, i * 128 : (i + 1) * 128], 0.0)
            term = g_weight * weight
            delta = term if delta is None else delta + term
            weights.append(weight)
            g_weights.append(g_weight)
            kept.append(jnp.maximum(both_signs, 0.0).astype(bf16))
        delta = jnp.sum(delta, axis=1, keepdims=True)
        g_scores = jnp.concatenate(
            [(weights[i] * (g_weights[i] - delta)).astype(bf16) for i in range(4)], axis=1
        )
        dropped = jnp.concatenate(kept, axis=1)
        out = jnp.dot(g_scores, keys[j], preferred_element_type=f32)
        out = jnp.where(lane_half((tokens, 128)), out[:tokens], out[tokens:])
        g_q[:, lanes] = (out * (0.125 * keep_scale)).astype(bf16)
        quarter = keys.shape[1] // 8
        sums[j, 0] = t_dot(g_scores, by_head(q[0, :, lanes])) * (0.125 * keep_scale)
        sums[j, 1] = t_dot(dropped, aboves[j]) * keep_scale
        for kind in range(2):
            for i in range(4):
                here = pl.multiple_of((2 * i + core) * quarter, quarter)
                there = pl.multiple_of((2 * i + 1 - core) * quarter, quarter)
                rows = slice(i * quarter, (i + 1) * quarter)
                g_near[kind][rows, lanes] = sums[j, kind, pl.ds(here, quarter), :]
                g_far[kind][rows, lanes] = sums[j, kind, pl.ds(there, quarter), :].astype(bf16)


def attention_back(ids, m, queries, near, far, signed, upstream):
    micro, tokens, width = queries.shape
    pairs = width // 128
    part = pl.BlockSpec((1, tokens, 128 * GROUP), lambda p, ids: (m, 0, p))
    flat = pl.BlockSpec((tokens // PARTS[m], 128 * GROUP), lambda p, ids: (0, p))
    both = pl.BlockSpec((tokens, 128 * GROUP), lambda p, ids: (0, p))
    operands = (ids, queries, *near[m], *far[m], signed, upstream)
    return call(
        functools.partial(attention_back_body, PARTS[m]),
        "attention_back",
        (pairs // GROUP,),
        operands,
        [part] + [flat] * (4 * PARTS[m])
        + [pl.BlockSpec((1, GROUP, 4, 2 * tokens, 128), lambda p, ids: (m, p, 0, 0, 0))]
        + [pl.BlockSpec((tokens, 128 * GROUP), lambda p, ids: (m, p))],
        [
            shaped((tokens, width), bf16),
            shaped((tokens, width), f32),
            shaped((tokens, width), f32),
            shaped((tokens, width), bf16),
            shaped((tokens, width), bf16),
        ],
        [both] * 5,
        [pltpu.VMEM((GROUP, 2 * tokens, 128), bf16)] * 2 + [pltpu.VMEM((GROUP, 2, 2 * tokens, 128), f32)],
        24,
        20,
    )


def up_body(weights, pers, tokens, ids, *refs):
    count = len(weights.operands)
    sources = refs[:count]
    context, hidden, keep, vectors, scaled, inverse, activated, slope = refs[count : count + 8]
    places, (sems, lows) = refs[count + 8 : -2], refs[-2:]
    copies = weights.copies(ids, sources, places, sems)
    rows, width = scaled.shape
    wide = activated.shape[1]
    begin([copies[0], copies[2], copies[1]])
    finish(copies[2])
    block = weights.matrix(places, 2)[:, :128].astype(f32).reshape(32, 8, 128)
    for row, per in enumerate(pers):
        vectors[row : row + 1, : 32 * per] = spread(block, row, 32 * per, per)
    finish(copies[0])

    def rows_part(m, carry):
        at = pl.ds(pl.multiple_of(m * tokens, tokens), tokens)
        attended = jnp.dot(context[at], weights.matrix(places, 0)[...], preferred_element_type=f32)
        attended = attended + vectors[0:1, :width]
        first_sum = hidden[at].astype(f32) + attended * (keep[at].astype(f32) * keep_scale)
        normal, scale = layer_norm(first_sum)
        scaled[at] = normal
        inverse[at] = jnp.broadcast_to(scale, (tokens, 128))
        lows[at] = (normal * vectors[1:2, :width] + vectors[2:3, :width]).astype(bf16)
        return carry

    lax.fori_loop(0, rows // tokens, rows_part, 0)
    finish(copies[1])
    up = weights.matrix(places, 1)
    step = 512

    def part(n, carry):
        at = pl.ds(pl.multiple_of(n * step, step), step)
        inner = jnp.dot(lows[...], up[:, at], preferred_element_type=f32) + vectors[3:4, at]
        cdf = 0.5 * (1.0 + lax.erf(inner * root_half))
        density = jnp.exp(-0.5 * inner * inner) * inverse_root_tau
        activated[:, at] = (inner * cdf).astype(bf16)
        slope[:, at] = (cdf + inner * density).astype(bf16)
        return carry

    lax.fori_loop(0, wide // step, part, 0)


def feed_up(ids, weights, pers, context, hidden, keep, tokens, wide):
    rows, width = hidden.shape
    return call(
        functools.partial(up_body, weights, pers, tokens),
        "feed_up",
        (1,),
        (ids, *weights.operands, context, hidden, keep),
        weights.specs + [WHOLE] * 3,
        [
            shaped((8, wide), f32),
            shaped((rows, width), f32),
            shaped((rows, 128), f32),
            shaped((rows, wide), bf16),
            shaped((rows, wide), bf16),
        ],
        [WHOLE] * 5,
        weights.scratch + [pltpu.VMEM((rows, width), bf16)],
        28,
        24,
    )


def hand_out(core, total, rows, own, send, first, at):
    def one(n, carry):
        here = pl.multiple_of((2 * n + core) * rows, 8)
        there = pl.multiple_of((2 * n + 1 - core) * rows, 8)
        own[first + n, at : at + rows, :] = total[pl.ds(here, rows), :].astype(bf16)
        send[first + n, at : at + rows, :] = total[pl.ds(there, rows), :].astype(bf16)
        return carry

    lax.fori_loop(0, total.shape[0] // (2 * rows), one, 0)


def down_body(weights, tokens, ids, *refs):
    count = len(weights.operands)
    sources, refs = refs[:count], refs[count:]
    activated, slope, scaled, keep, cotangent, vectors = refs[:6]
    layer_out, g_second_out, g_inner, own, send, sums = refs[6:12]
    place, sems, total, g_outers = refs[12:]
    copies = weights.copies(ids, sources, (place,), sems)
    rows, width = scaled.shape
    wide = activated.shape[1]
    begin(copies)
    sums[...] = jnp.zeros_like(sums)
    finish(copies[0])
    down = weights.matrix((place,), 0)
    gain = vectors[5:6, :width]

    def rows_part(m, carry):
        at = pl.ds(pl.multiple_of(m * tokens, tokens), tokens)
        outer = jnp.dot(activated[at], down[...], preferred_element_type=f32) + vectors[4:5, :width]
        factor = keep[at].astype(f32) * keep_scale
        normed = scaled[at] * vectors[1:2, :width] + vectors[2:3, :width]
        normal, scale = layer_norm(normed + outer * factor)
        layer_out[at] = (normal * gain + vectors[6:7, :width]).astype(bf16)
        above = cotangent[at].astype(f32)
        weighted = above * gain
        g_second = scale * (
            weighted
            - jnp.mean(weighted, axis=-1, keepdims=True)
            - normal * jnp.mean(weighted * normal, axis=-1, keepdims=True)
        )
        g_second_out[at] = g_second
        g_outer = (g_second * factor).astype(bf16)
        g_outers[at] = g_outer
        sums[0:1, :width] += jnp.sum(g_outer.astype(f32), axis=0, keepdims=True)
        sums[1:2, :width] += jnp.sum(above * normal, axis=0, keepdims=True)
        sums[2:3, :width] += jnp.sum(above, axis=0, keepdims=True)
        return carry

    lax.fori_loop(0, rows // tokens, rows_part, 0)
    step = 512

    def part(n, carry):
        at = pl.ds(pl.multiple_of(n * step, step), step)
        g_in = (dot_t(g_outers[...], down[at, :]) * slope[:, at].astype(f32)).astype(bf16)
        g_inner[:, at] = g_in
        sums[3:4, at] = jnp.sum(g_in.astype(f32), axis=0, keepdims=True)
        return carry

    lax.fori_loop(0, wide // step, part, 0)

    def grads(n, carry):
        at = pl.ds(pl.multiple_of(n * width, width), width)
        total[...] = t_dot(activated[:, at], g_outers[...])
        hand_out(ids[0], total, wide // 32, own, send, n * (16 * width // wide), 0)
        return carry

    lax.fori_loop(0, wide // width, grads, 0)


def feed_down(ids, weights, activated, slope, scaled, keep, cotangent, vectors, tokens):
    rows, width = scaled.shape
    wide = activated.shape[1]
    halves = (16, wide // 32, width)
    return call(
        functools.partial(down_body, weights, tokens),
        "feed_down",
        (1,),
        (ids, *weights.operands, activated, slope, scaled, keep, cotangent, vectors),
        weights.specs + [WHOLE] * 6,
        [
            shaped((rows, width), bf16),
            shaped((rows, width), f32),
            shaped((rows, wide), bf16),
            shaped(halves, bf16),
            shaped(halves, bf16),
            shaped((8, wide), f32),
        ],
        [WHOLE] * 6,
        weights.scratch + [pltpu.VMEM((width, width), f32), pltpu.VMEM((rows, width), bf16)],
        30,
        36,
    )


def middle_body(weights, pers, tokens, ids, *refs):
    count = len(weights.operands)
    sources, refs = refs[:count], refs[count:]
    g_inner, g_second, scaled, inverse, keep, vectors, context, down_sums = refs[:8]
    g_first_out, g_context, own, send, block = refs[8:13]
    *places, sems, g_normeds, g_attendeds, sums = refs[13:]
    copies = weights.copies(ids, sources, places, sems)
    begin([copies[1], copies[0]])
    rows, width = scaled.shape
    out_w, up_w = weights.matrix(places, 0), weights.matrix(places, 1)
    finish(copies[1])
    step = 256

    def columns_part(n, carry):
        at = pl.ds(pl.multiple_of(n * step, step), step)
        g_normeds[:rows, at] = g_second[:, at] + dot_t(g_inner[...], up_w[at, :])
        return carry

    lax.fori_loop(0, width // step, columns_part, 0)
    sums[...] = jnp.zeros_like(sums)

    def rows_part(m, carry):
        at = pl.ds(pl.multiple_of(m * tokens, tokens), tokens)
        normal = scaled[at]
        g_normed = g_normeds[at, :]
        weighted = g_normed * vectors[1:2, :width]
        g_first = inverse[at, 0:1] * (
            weighted
            - jnp.mean(weighted, axis=-1, keepdims=True)
            - normal * jnp.mean(weighted * normal, axis=-1, keepdims=True)
        )
        g_first_out[at] = g_first
        g_attended = (g_first * (keep[at].astype(f32) * keep_scale)).astype(bf16)
        g_attendeds[at] = g_attended
        sums[0:1, :] += jnp.sum(g_attended.astype(f32), axis=0, keepdims=True)
        sums[1:2, :] += jnp.sum(g_normed * normal, axis=0, keepdims=True)
        sums[2:3, :] += jnp.sum(g_normed, axis=0, keepdims=True)
        return carry

    lax.fori_loop(0, rows // tokens, rows_part, 0)
    finish(copies[0])
    g_context[...] = dot_t(g_attendeds[...], out_w[...]).astype(bf16)
    g_normeds[:width] = t_dot(context[...], g_attendeds[...])
    hand_out(ids[0], g_normeds, width // 32, own, send, 0, 0)
    vector_sums = [sums[n : n + 1, :] for n in range(3)]
    vector_sums += [down_sums[3:4, :]] + [down_sums[n : n + 1, :width] for n in range(3)]
    unspread(vector_sums, pers, block)


def middle(ids, weights, pers, g_inner, g_second, scaled, inverse, keep, vectors, context, sums, tokens):
    rows, width = scaled.shape
    halves = (16, width // 32, width)
    return call(
        functools.partial(middle_body, weights, pers, tokens),
        "middle",
        (1,),
        (ids, *weights.operands, g_inner, g_second, scaled, inverse, keep, vectors, context, sums),
        weights.specs + [WHOLE] * 8,
        [
            shaped((rows, width), f32),
            shaped((rows, width), bf16),
            shaped(halves, bf16),
            shaped(halves, bf16),
            shaped((32, 8, width), f32),
        ],
        [WHOLE] * 5,
        weights.scratch
        + [pltpu.VMEM((max(rows, width), width), f32), pltpu.VMEM((rows, width), bf16), pltpu.VMEM((8, width), f32)],
        26,
        18,
    )


def grads_body(ids, g_inner, scaled, vectors, own, send, total, low_t):
    n = pl.program_id(0)
    width = scaled.shape[1]

    @pl.when(n == 0)
    def _():
        low_t[...] = (scaled[...] * vectors[1:2, :width] + vectors[2:3, :width]).T.astype(bf16)

    total[...] = jnp.dot(low_t[...], g_inner[...], preferred_element_type=f32)
    for block in range(own.shape[1] // (width // 32)):

        @pl.when(n == block)
        def _():
            hand_out(ids[0], total, width // 32, own, send, 0, block * (width // 32))


def up_grads(ids, g_inner, scaled, vectors):
    rows, width = scaled.shape
    wide = g_inner.shape[1]
    halves = (16, wide // 32, width)
    return call(
        grads_body,
        "up_grads",
        (wide // width,),
        (ids, g_inner, scaled, vectors),
        [pl.BlockSpec((rows, width), lambda i, ids: (0, i))] + [WHOLE] * 2,
        [shaped(halves, bf16), shaped(halves, bf16)],
        [WHOLE] * 2,
        [pltpu.VMEM((width, width), f32), pltpu.VMEM((width, rows), bf16)],
        24,
        20,
    )


def hand_out_rows(core, block, own, send, at):
    for n in range(16):
        own[n, at : at + 8, :] = block[2 * n + core].astype(bf16)
        send[n, at : at + 8, :] = block[2 * n + 1 - core].astype(bf16)


def inputs_body(per, ids, hidden, turned, *refs):
    micro = (len(refs) - 8) // 5
    grads, (block, own, send, g_queries, g_keys, g_values, total, bias) = refs[: 5 * micro], refs[5 * micro :]
    width = hidden.shape[1]
    sums = []
    for n, out in enumerate((g_queries, g_keys, g_values)):
        for m in range(micro):
            g_q, near, far = grads[m], grads[micro + 2 * m :][:2], grads[3 * micro + 2 * m :][:2]
            rows = slice(m * g_q.shape[0], (m + 1) * g_q.shape[0])
            if n == 0:
                out[rows] = g_q[...]
            else:
                out[rows] = (near[n - 1][...] + far[n - 1][...].astype(f32)).astype(bf16)
        if n != 1:
            sums.append(jnp.sum(out[...].astype(f32), axis=0, keepdims=True))
        left = hidden if n == 0 else turned

        def part(k, carry, left=left, out=out):
            at = pl.ds(pl.multiple_of(k * 256, 256), 256)
            total[at, :] = t_dot(left[:, at], out[...])
            return carry

        lax.fori_loop(0, width // 256, part, 0)
        hand_out(ids[0], total, width // 32, own, send, 0, n * (width // 32))
    bias[...] = block[...]
    unspread([jnp.concatenate(sums, axis=1)], [per], bias, 7)
    hand_out_rows(ids[0], bias, own, send, 3 * (width // 32))


def input_grads(ids, hidden, turned, grads, block, per):
    rows, width = hidden.shape
    halves = (16, 3 * width // 32 + 8, width)
    return call(
        functools.partial(inputs_body, per),
        "input_grads",
        (1,),
        (ids, hidden, turned, *grads, block),
        [WHOLE] * (3 + len(grads)),
        [shaped(halves, bf16)] * 2 + [shaped((rows, width), bf16)] * 3,
        [WHOLE] * 5,
        [pltpu.VMEM((width, width), f32), pltpu.VMEM((32, 8, width), f32)],
        28,
        12,
    )


def last_body(weights, ids, *refs):
    count = len(weights.operands)
    sources = refs[:count]
    g_first, g_q, g_keys, g_values, out = refs[count : count + 5]
    places, sems = refs[count + 5 : -1], refs[-1]
    copies = weights.copies(ids, sources, places, sems)

    @pl.when(pl.program_id(0) == 0)
    def _():
        begin(copies)
        for group in copies:
            finish(group)

    turn = turn_matrix(g_q.shape[0])
    total = g_first[...] + dot_t(g_q[...], weights.matrix(places, 0)[...])
    total = total + dot_t(t_dot(turn, g_keys[...]).astype(bf16), weights.matrix(places, 1)[...])
    total = total + dot_t(t_dot(turn, g_values[...]).astype(bf16), weights.matrix(places, 2)[...])
    out[...] = total.astype(bf16)


def last(ids, weights, g_first, g_q, g_keys, g_values, tokens):
    rows, width = g_first.shape
    narrow = rows_spec(tokens, width)
    return call(
        functools.partial(last_body, weights),
        "input_back",
        (rows // tokens,),
        (ids, *weights.operands, g_first, g_q, g_keys, g_values),
        weights.specs + [narrow] * 4,
        [shaped((rows, width), bf16)],
        [narrow],
        weights.scratch,
        16,
        10,
    )[0]


def beside(shape, y, x):
    return pl.BlockSpec((4, 1, 1) + shape[3:], lambda i, ids: (0, ids[1] ^ y, ids[2] ^ x, 0, 0))


def rows_of(parts, index, first, last):
    found, start = [], 0
    for part in parts:
        rows = part.shape[-2]
        low, high = max(first, start), min(last, start + rows)
        if low < high:
            found.append(part[index + (slice(low - start, high - start),)].astype(f32))
        start += rows
    return found[0] if len(found) == 1 else jnp.concatenate(found, axis=-2)


def both(parts, index, first, last):
    half = len(parts) // 2
    return rows_of(parts[:half], index, first, last) + rows_of(parts[half:], index, first, last)


def count_rows(parts):
    return sum(part.shape[3] for part in parts[: len(parts) // 2])


PLANE = (slice(None), 0, 0)


def corner_body(ids, *refs):
    *parts, low, high = refs
    half = low.shape[1]
    low[...] = both(parts, PLANE, 0, half).astype(bf16)
    high[...] = both(parts, PLANE, half, half + high.shape[1]).astype(bf16)


def reduce_corner(ids, parts, cut):
    rows, width = count_rows(parts), parts[0].shape[4]
    return call(
        corner_body,
        "reduce_corner",
        (1,),
        (ids, *parts),
        [beside(part.shape, 1, 1) for part in parts],
        [shaped((4, cut, width), bf16), shaped((4, rows - cut, width), bf16)],
        [WHOLE] * 2,
        [],
        8,
        2,
    )


def sides_body(count, ids, *refs):
    for_y, for_x, (low, high, to_y, to_x) = refs[:count], refs[count : 2 * count], refs[2 * count :]
    rows, half = to_y.shape[1], low.shape[1]
    to_y[:, :half] = (both(for_y, PLANE, 0, half) + low[...].astype(f32)).astype(bf16)
    to_y[:, half:] = both(for_y, PLANE, half, rows).astype(bf16)
    to_x[:, :half] = both(for_x, PLANE, 0, half).astype(bf16)
    to_x[:, half:] = (both(for_x, PLANE, half, rows) + high[...].astype(f32)).astype(bf16)


def reduce_sides(ids, parts, low, high):
    rows, width = count_rows(parts), parts[0].shape[4]
    return call(
        functools.partial(sides_body, len(parts)),
        "reduce_sides",
        (1,),
        (ids, *parts, *parts, low, high),
        [beside(part.shape, 1, 0) for part in parts]
        + [beside(part.shape, 0, 1) for part in parts]
        + [WHOLE] * 2,
        [shaped((4, rows, width), bf16)] * 2,
        [WHOLE] * 2,
        [],
        10,
        3,
    )


def depth_body(ids, *refs):
    *parts, from_y, from_x, near, middle, far, mine = refs
    for k, out in enumerate((mine, near, middle, far)):
        z = ids[3] ^ k
        total = both(parts, (z, 0, 0), 0, from_y.shape[1])
        total = total + from_y[z].astype(f32) + from_x[z].astype(f32)
        out[...] = total.astype(out.dtype)


def reduce_depth(ids, parts, from_y, from_x):
    shape = from_y.shape[1:]
    return call(
        depth_body,
        "reduce_depth",
        (1,),
        (ids, *parts, from_y, from_x),
        [beside(part.shape, 0, 0) for part in parts] + [WHOLE] * 2,
        [shaped(shape, bf16)] * 3 + [shaped(shape, f32)],
        [WHOLE] * 4,
        [],
        10,
        3,
    )


def pair_body(ids, one, two, out):
    out[0] = one[...]
    out[1] = two[...]


def pair_z(ids, one, two):
    return call(
        pair_body,
        "pair_z",
        (1,),
        (ids, one, two),
        [WHOLE] * 2,
        [shaped((2,) + one.shape, bf16)],
        [WHOLE],
        [],
        4,
        1,
    )[0]


def order_body(ids, pair, received, out):
    for k in range(2):
        out[ids[3] ^ (2 * k)] = pair[k]
        out[ids[3] ^ (2 * k + 1)] = received[k]


def order_z(ids, pair, received):
    return call(
        order_body,
        "order_z",
        (1,),
        (ids, pair, received),
        [WHOLE] * 2,
        [shaped((4,) + pair.shape[1:], bf16)],
        [WHOLE],
        [],
        6,
        1,
    )[0]


def four_body(ids, *refs):
    *parts, out = refs
    for k, part in enumerate(parts):
        out[ids[3] ^ k] = part[...]


def order_four(ids, *parts):
    return call(
        four_body,
        "order_four",
        (1,),
        (ids, *parts),
        [WHOLE] * 4,
        [shaped((4,) + parts[0].shape, bf16)],
        [WHOLE],
        [],
        6,
        1,
    )[0]


def halves_body(ids, pair, received, low, high):
    rows = low.shape[1]
    for k in range(2):
        for source, z in ((pair, ids[3] ^ (2 * k)), (received, ids[3] ^ (2 * k + 1))):
            low[z] = source[k, :rows]
            high[z] = source[k, rows:]


def order_halves(ids, pair, received):
    shape = (4, pair.shape[1] // 2, pair.shape[2])
    return call(
        halves_body,
        "order_halves",
        (1,),
        (ids, pair, received),
        [WHOLE] * 2,
        [shaped(shape, bf16)] * 2,
        [WHOLE] * 2,
        [],
        6,
        1,
    )


def first_body(ids, *refs):
    at_y, at_x, at_corner, (to_y, to_x) = refs[:2], refs[2:4], refs[4:6], refs[6:]
    half = to_y.shape[1] // 2
    to_y[:, :half] = both(at_y, PLANE, 0, half).astype(bf16)
    to_y[:, half:] = both(at_corner, PLANE, 0, half).astype(bf16)
    to_x[:, :half] = both(at_x, PLANE, half, 2 * half).astype(bf16)
    to_x[:, half:] = both(at_corner, PLANE, half, 2 * half).astype(bf16)


def reduce_first(ids, parts):
    shape = parts[0].shape
    return call(
        first_body,
        "reduce_first",
        (1,),
        (ids, *parts, *parts, *parts),
        [beside(shape, 1, 0)] * 2 + [beside(shape, 0, 1)] * 2 + [beside(shape, 1, 1)] * 2,
        [shaped((4,) + shape[3:], bf16)] * 2,
        [WHOLE] * 2,
        [],
        10,
        3,
    )


def second_body(ids, *refs):
    here, at_y, at_x, (from_y, from_x, send, keep) = refs[:2], refs[2:4], refs[4:6], refs[6:]
    half = from_y.shape[1] // 2
    for k, (out, at) in enumerate(((keep, 0), (send, 0), (keep, 1), (send, 1))):
        z = ids[3] ^ k
        plane = (z, 0, 0)
        quarters = (
            both(here, plane, 0, half) + from_y[z, :half].astype(f32),
            both(at_x, plane, 0, half) + from_y[z, half:].astype(f32),
            both(here, plane, half, 2 * half) + from_x[z, :half].astype(f32),
            both(at_y, plane, half, 2 * half) + from_x[z, half:].astype(f32),
        )
        for i, quarter in enumerate(quarters):
            out[at, i * half : (i + 1) * half] = quarter.astype(out.dtype)


def reduce_second(ids, parts, from_y, from_x):
    shape = parts[0].shape
    wide = (2, 2 * shape[3], shape[4])
    return call(
        second_body,
        "reduce_second",
        (1,),
        (ids, *parts, *parts, *parts, from_y, from_x),
        [beside(shape, 0, 0)] * 2 + [beside(shape, 1, 0)] * 2 + [beside(shape, 0, 1)] * 2 + [WHOLE] * 2,
        [shaped(wide, bf16), shaped(wide, f32)],
        [WHOLE] * 2,
        [],
        14,
        3,
    )


def quarter_body(ids, keep, received, send, mine):
    mine[...] = keep[0] + received[0].astype(f32)
    send[...] = (keep[1] + received[1].astype(f32)).astype(bf16)


def reduce_third(ids, keep, received):
    shape = keep.shape[1:]
    return call(
        quarter_body,
        "reduce_third",
        (1,),
        (ids, keep, received),
        [WHOLE] * 2,
        [shaped(shape, bf16), shaped(shape, f32)],
        [WHOLE] * 2,
        [],
        10,
        2,
    )


def fourth_body(ids, mine, received, to_x, to_y, own):
    half = to_x.shape[0]
    total = mine[...] + received[...].astype(f32)
    own[:half] = total[:half]
    own[half:] = total[2 * half : 3 * half]
    to_x[...] = total[half : 2 * half].astype(bf16)
    to_y[...] = total[3 * half :].astype(bf16)


def reduce_fourth(ids, mine, received):
    rows, width = mine.shape
    return call(
        fourth_body,
        "reduce_fourth",
        (1,),
        (ids, mine, received),
        [WHOLE] * 2,
        [shaped((rows // 4, width), bf16)] * 2 + [shaped((rows // 2, width), f32)],
        [WHOLE] * 3,
        [],
        8,
        2,
    )


def exchange_z(sends):
    return [pp(send, "z", k) for send, k in zip(sends, (1, 2, 3))]


def local(
    hidden_in,
    cotangent,
    attention_keep,
    output_keep,
    feed_keep,
    qkv_weight,
    qkv_bias,
    out_weight,
    out_bias,
    first_gain,
    first_shift,
    up_weight,
    up_bias,
    down_weight,
    down_bias,
    second_gain,
    second_shift,
):
    micro, _, tokens, width = hidden_in.shape
    rows = micro * tokens
    own = qkv_weight.shape[0]
    wide = up_weight.shape[1]
    blocks = wide // width
    c, y, x = lax.axis_index("seq"), lax.axis_index("y"), lax.axis_index("x")
    ids = jnp.stack([c, y, x, lax.axis_index("z")]).astype(jnp.int32)
    bias_parts = (out_bias, first_gain, first_shift, up_bias, down_bias, second_gain, second_shift)
    pers = [part.shape[0] for part in bias_parts]
    per = qkv_bias.shape[0]

    column = lambda weight, i: weight[:, i * width : (i + 1) * width]
    bias_rows = lambda parts: jnp.concatenate(
        [jnp.pad(part.reshape(1, -1), ((0, 0), (0, width - part.shape[0]))) for part in parts]
        + [jnp.zeros((8 - len(parts), width), bf16)]
    )
    square = (own, width)
    hidden = hidden_in.reshape(rows, width)

    shard_a = jnp.concatenate([column(qkv_weight, i) for i in range(3)] + [bias_rows((qkv_bias,))])
    half_c = down_weight.shape[0] // 2
    x_c, y_c = pp(down_weight[:half_c], "x"), pp(down_weight[half_c:], "y")
    shard_b = jnp.concatenate(
        [out_weight] + [column(up_weight, i) for i in range(blocks)] + [bias_rows(bias_parts)]
    )
    z_a = hold([pp(shard_a, "z", k) for k in (1, 2, 3)], x_c, y_c, shard_b)
    own_a = order_four(ids, shard_a, *z_a)
    group_c = jnp.concatenate([down_weight[:half_c], x_c, down_weight[half_c:], y_c])
    x_a, y_a = pp(own_a, "x"), pp(own_a, "y")
    shard_b = after(shard_b, own_a)
    far_b = pp(shard_b, "z", 2)
    turned, keep_output, keep_feed = prepare(
        ids, after(hidden, own_a), output_keep.transpose(0, 1, 3, 2), feed_keep.transpose(0, 1, 3, 2), tokens
    )
    x_a, y_a, far_b = hold((x_a, y_a, far_b), turned)
    cut_a = shard_a.shape[0] // 2
    low_a, high_a = pp(x_a[:, :cut_a], "y"), pp(y_a[:, cut_a:], "x")
    pieces = [whole(0, 0, own_a), whole(1, 0, x_a), whole(2, 0, y_a), whole(3, 0, low_a), whole(3, cut_a, high_a)]
    late = whole(2, 0, after(y_a, low_a))
    pieces += [at_core(piece) for piece in pieces[:2] + [late] + pieces[3:]]
    pair_b = pair_z(ids, shard_b, far_b)
    near_b = pp(pair_b, "z", 1)
    plan = [(i * own, own, i, 0, 0) for i in range(3)]
    plan = divide(plan, cut_a)
    weights = Weights(pieces, plan + [(3 * own, 8, 3, 0, 0)], [square] * 3 + [(8, width)])
    weights_again = Weights(pieces, plan, [square] * 3)
    own_b = order_z(ids, pair_b, after(near_b, low_a, high_a))
    far_c = pp(after(group_c, own_b), "z", 2)
    x_b, y_b = pp(own_b, "x"), pp(own_b, "y")
    queries, *near = project(ids, weights, hidden, after(turned, own_b), micro, per)
    near = (near[: 2 * PARTS[0]], near[2 * PARTS[0] :])
    far = [[pp(value, "seq") for value in values] for values in near]
    words = attention_keep.reshape(micro, H, tokens, -1)
    *far[0], far_c = hold((*far[0], far_c))
    pair_c = pair_z(ids, group_c, far_c)
    near_c = pp(pair_c, "z", 1)
    context, signed = attention(ids, 0, after(queries, pair_c), near, far, words)
    own_b, x_b, y_b, *far[1] = hold((own_b, x_b, y_b, *far[1]), context)
    cut_b = shard_b.shape[0] // 2
    low_b, high_b = pp(x_b[:, :cut_b], "y"), pp(y_b[:, cut_b:], "x")
    context, signed = attention(ids, 1, queries, near, far, words, (context, signed))
    low_b, high_b, near_c = hold((low_b, high_b, near_c), context)
    pieces = [whole(0, 0, own_b), whole(1, 0, x_b), whole(2, 0, after(y_b, context))]
    pieces += [at_core(piece) for piece in pieces]
    corners = [whole(3, 0, low_b), whole(3, cut_b, high_b)]
    pieces += corners + [at_core(piece) for piece in corners]
    plan = [(0, own, 0, 0, 0)] + [((i + 1) * own, own, 1, 0, i * width) for i in range(blocks)]
    plan = divide(plan, cut_b)
    weights = Weights(
        pieces, plan + [((blocks + 1) * own, 8, 2, 0, 0)], [square, (own, wide), (8, width)]
    )
    back_weights = Weights(pieces, plan, [square, (own, wide)])
    by_x, by_y = order_halves(ids, pair_c, after(near_c, low_b, high_b))
    from_y, from_x = pp(by_x, "y"), pp(by_y, "x")
    context = context.reshape(rows, width)
    vectors, scaled, inverse, activated, slope = feed_up(
        ids, weights, pers, context, hidden, keep_output, tokens, wide
    )
    from_y, from_x = hold((from_y, from_x), activated)
    down_rows = down_weight.shape[0]
    pieces = []
    for core in range(2):
        held = [by_x, from_y, by_y, from_x]
        if core == 1:
            held = [pp(array, "seq") for array in held]
        for array, numbers, first in zip(held, ((0, 1), (2, 3), (0, 2), (1, 3)), (0, 0, half_c, half_c)):
            pieces += [(4 * core + number, first, array, i * half_c, half_c) for i, number in enumerate(numbers)]
    plan = divide([(0, down_rows, 0, 0, 0)], half_c)
    weights = Weights(pieces, plan, [(down_rows, width)])
    layer_out, g_second, g_inner, down_own, down_send, sums = feed_down(
        ids, weights, activated, slope, scaled, keep_feed, cotangent.reshape(rows, width), vectors, tokens
    )

    unit = lambda value: value.reshape((4, 2, 2) + value.shape[1:])
    down_core = pp(down_send, "seq")
    mid_own, mid_send = up_grads(ids, g_inner, scaled, vectors)
    down = [unit(down_own), unit(after(down_core, mid_send))]
    to_y, to_x = reduce_first(ids, down)
    down_y, down_x = pp(to_y, "y"), pp(to_x, "x")
    mid_core = pp(after(mid_send, to_y), "seq")
    g_first, g_context, out_own, out_send, block = middle(
        ids, back_weights, pers, after(g_inner, to_y), g_second, scaled, inverse, keep_output, vectors, context, sums, tokens
    )
    out_core = pp(out_send, "seq")
    down_y, down_x, mid_core = hold((down_y, down_x, mid_core), g_context)
    mid = [unit(value) for value in (mid_own, out_own, mid_core, out_core)]
    cut_m = (count_rows(mid) + 15) // 16 * 8
    corner = reduce_corner(ids, mid, cut_m)
    low, high = pp(corner[0], "x"), pp(corner[1], "y")
    down_send, down_keep = reduce_second(ids, down, down_y, down_x)
    down_near = pp(down_send, "z", 1)
    first_q, *first_near, far_k, far_v = attention_back(
        ids, 0, queries, near, far, signed, after(g_context, down_send, *corner)
    )
    low, high = hold((low, high), first_q)
    first_far = [pp(after(value, low, high), "seq") for value in (far_k, far_v)]
    to_y, to_x = reduce_sides(ids, mid, low, high)
    mid_y, mid_x = pp(to_y, "y"), pp(to_x, "x")
    second_q, *second_near, far_k, far_v = attention_back(
        ids, 1, queries, near, far, signed, after(g_context, to_y, to_x)
    )
    first_far = hold(first_far, second_q)
    second_far = [pp(value, "seq") for value in (far_k, far_v)]
    down_near = after(down_near, second_q)
    down_send, down_mine = reduce_third(ids, down_keep, down_near)
    down_far = pp(down_send, "z", 2)
    grads = (first_q, second_q, *first_near, *second_near, *first_far, *hold(second_far, down_send))
    a_own, a_send, g_q, g_keys, g_values = input_grads(ids, hidden, turned, grads, block, per)
    mid_y, mid_x = hold((mid_y, mid_x), a_send)
    down_far = after(down_far, a_send)
    core_sums = pp(after(a_send, mid_y, mid_x, down_far), "seq")
    to_far_x, to_far_y, down_mine = reduce_fourth(ids, down_mine, down_far)
    part = [unit(a_own), unit(core_sums)]
    corner = reduce_corner(ids, part, cut_a)
    low, high = pp(corner[0], "x"), pp(corner[1], "y")
    *sends, mid_mine = reduce_depth(ids, mid, after(mid_y, *corner), mid_x)
    mid_z = exchange_z(sends)
    low, high = hold((low, high), *sends)
    to_y, to_x = reduce_sides(ids, part, low, high)
    side_y, side_x = pp(to_y, "y"), pp(to_x, "x")
    received = [pp(after(to_far_x, to_x), "x"), pp(after(to_far_y, to_y), "y")]
    grad_in = last(
        ids, weights_again, g_first, g_q, g_keys, after(g_values, to_y, to_x), tokens
    )
    mid_z = hold(mid_z, grad_in)
    mid = add_up([mid_mine, *mid_z])
    side_y, side_x, *received = hold((side_y, side_x, *received), mid, grad_in)
    *sends, part_mine = reduce_depth(ids, part, side_y, side_x)
    grad_down = add_up([down_mine, jnp.concatenate(received)])
    part = add_up([part_mine, *exchange_z(sends)])

    stripe = lambda value, i: value[i * own : (i + 1) * own]
    grad_qkv = jnp.concatenate([stripe(part, i) for i in range(3)], axis=1)
    grad_up = jnp.concatenate([stripe(mid, i) for i in range(blocks)], axis=1)
    vector_grads = [part[3 * own + i, :length] for i, length in enumerate(pers)]
    grad_out = mid[blocks * own :]
    return (
        layer_out.reshape(hidden_in.shape),
        grad_in.reshape(hidden_in.shape),
        grad_qkv,
        part[3 * own + 7, :per],
        grad_out,
        vector_grads[0],
        vector_grads[1],
        vector_grads[2],
        grad_up,
        vector_grads[3],
        grad_down,
        vector_grads[4],
        vector_grads[5],
        vector_grads[6],
    )


def solution(mesh):
    groups, cores = mesh.devices.shape
    split = Mesh(mesh.devices.reshape(groups // 4, 2, 2, cores), ("z", "y", "x", "seq"))
    dp = ("z", "y", "x")
    token_rows = P(None, dp, "seq", None)
    matrix = P(every, None)
    vector = P(every)
    params = (matrix, vector, matrix, vector, vector, vector, matrix, vector, matrix, vector, vector, vector)

    def layer(*arrays):
        tiled = groups == 16 and cores == 2 and arrays[5].shape[0] % 8 == 0
        return (local if tiled else plain_local)(*arrays)

    return jax.shard_map(
        layer,
        mesh=split,
        in_specs=(token_rows, token_rows, P(None, dp, None, "seq", None), token_rows, token_rows) + params,
        out_specs=(token_rows, token_rows) + params,
        check_vma=False,
    )
```

profile of v0, /device:TPU:0, one launch (start us, length us, event | category | flops | bytes accessed | tf_op | source)
XLA Modules:
  0.0 231.0 jit_solution(11056706199239719847)
XLA Ops:
  0.7 0.9 fusion.4
  2.3 5.1 %collective-permute-start.4 = (bf16[80,768]{1,0:T(8,128)(2,1)S(1)}, bf16[80,768]{1,0:T(8,128)(2,1)S(1)}, u32[]{:S(2)}, u32[]{:S(2)}) collective-permute-start(bf16[80,768]{1,0:T(8,128)(2,1)S(1)} %concatenate.19.refs_0_), channel_id=1, source_target_pairs={{0,24},{8,16},{16,8},{24,0},{1,25},{9,17},{17,9},{25,1},{2,26},{10... | collective-permute-start | bytes 368648 | tf_op jit(solution)/shard_map/ppermute | solution.py:336
  8.0 0.9 fusion.3
  9.0 1.7 collective-permute-start
  10.7 1.5 collective-permute-start.1
  20.4 1.0 collective-permute-start.5
  21.5 1.6 collective-permute-start.7
  23.1 1.0 copy-done.30
  24.1 3.0 %prepare.1 = (bf16[512,768]{1,0:T(8,128)(2,1)S(1)}, bf16[512,768]{1,0:T(8,128)(2,1)S(1)}, bf16[512,768]{1,0:T(8,128)(2,1)S(1)}) custom-call(s32[4]{0:T(128)S(1)} %pad_add_fusion.ids, bf16[512,768]{1,0:T(8,128)(2,1)S(1)} %bitcast.78, s32[2,1,192,256]{3,2,1,0:T(8,128)S(1)} %bitcast.93, s32[2,1,192,256]{3,2,1,0:T(8,128)S(1)} %bitcast.94), custom_call_target="tpu_custom_call" | custom-call | flops 1024 | bytes 393216 | tf_op jit(solution)/shard_map/prepare/pallas_call | solution.py:455
  27.2 4.6 %collective-permute-done.7.two = bf16[128,768]{1,0:T(8,128)(2,1)S(1)} collective-permute-done((bf16[128,768]{1,0:T(8,128)(2,1)S(1)}, bf16[128,768]{1,0:T(8,128)(2,1)S(1)}, u32[]{:S(2)}, u32[]{:S(2)}) %collective-permute-start.7) | collective-permute-done | bytes 196640 | tf_op jit(solution)/shard_map/ppermute | solution.py:336
  32.0 1.4 collective-permute-start.8
  34.0 1.5 collective-permute-start.15
  36.3 2.9 %collective-permute-done.8.refs_3_ = bf16[4,40,768]{2,1,0:T(8,128)(2,1)S(1)} collective-permute-done((bf16[4,40,768]{2,1,0:T(8,128)(2,1)S(1)}, bf16[4,40,768]{2,1,0:T(8,128)(2,1)S(1)}, u32[]{:S(2)}, u32[]{:S(2)}) %collective-permute-start.8) | collective-permute-done | bytes 245792 | tf_op jit(solution)/shard_map/ppermute | solution.py:336
  39.2 4.7 %collective-permute-done.9.refs_4_ = bf16[4,40,768]{2,1,0:T(8,128)(2,1)S(1)} collective-permute-done((bf16[4,40,768]{2,1,0:T(8,128)(2,1)S(1)}, bf16[4,40,768]{2,1,0:T(8,128)(2,1)S(1)}, u32[]{:S(2)}, u32[]{:S(2)}) %collective-permute-start.9) | collective-permute-done | bytes 245792 | tf_op jit(solution)/shard_map/ppermute | solution.py:336
  44.0 1.6 collective-permute-done.15.received
  46.3 2.4 %collective-permute-start.20 = (bf16[192,768]{1,0:T(8,128)(2,1)S(1)}, bf16[192,768]{1,0:T(8,128)(2,1)S(1)}, u32[]{:S(2)}, u32[]{:S(2)}) collective-permute-start(bf16[192,768]{1,0:T(8,128)(2,1)S(1)} %pad_maximum_fusion.one), channel_id=1, source_target_pairs={{0,16},{8,24},{16,0},{24,8},{1,17},{9,25},{17,1},{25,9},{2,18},{10... | collective-permute-start | bytes 884744 | tf_op jit(solution)/shard_map/ppermute | solution.py:336
  51.7 5.2 %project.1 = (bf16[2,256,768]{2,1,0:T(8,128)(2,1)S(1)}, bf16[128,768]{1,0:T(8,128)(2,1)S(1)}, bf16[128,768]{1,0:T(8,128)(2,1)S(1)}, bf16[128,768]{1,0:T(8,128)(2...) custom-call(s32[4]{0:T(128)S(1)} %pad_add_fusion.ids, ...), custom_call_target="tpu_custom_call" | custom-call | flops 1024 | bytes 655360 | tf_op jit(solution)/shard_map/project/pallas_call | solution.py:455
  57.5 4.7 %collective-permute-done.20.two = bf16[192,768]{1,0:T(8,128)(2,1)S(1)} collective-permute-done((bf16[192,768]{1,0:T(8,128)(2,1)S(1)}, bf16[192,768]{1,0:T(8,128)(2,1)S(1)}, u32[]{:S(2)}, u32[]{:S(2)}) %collective-permute-start.20) | collective-permute-done | bytes 294944 | tf_op jit(solution)/shard_map/ppermute | solution.py:336
  63.8 1.3 collective-permute-done.19.refs_7_
  66.1 4.6 %attention.2 = (bf16[2,256,768]{2,1,0:T(8,128)(2,1)S(1)}, bf16[2,6,4,512,128]{4,3,2,1,0:T(8,128)(2,1)S(1)}) custom-call(s32[4]{0:T(128)S(1)} %pad_add_fusion.ids, bf16[2,256,768]{2,1,0:T(8,128)(2,1)S(1)} %get-tuple-element.173.q, bf16[128,768]{1,0:T(8,128)(2,1)S(1)} %get-tuple-element.164.refs_0_, bf16[128,768]{1,0:T(8,128)(2,1)S(1)} %get-tuple-element.165.refs_1_, ...), custom_call_target="tpu_custom_call" | custom-call | flops 1024 | bytes 917504 | tf_op jit(solution)/shard_map/attention/pallas_call | solution.py:455
  71.5 1.0 collective-permute-start.26
  72.5 4.5 %attention.3 = (bf16[2,256,768]{2,1,0:T(8,128)(2,1)S(1)}, bf16[2,6,4,512,128]{4,3,2,1,0:T(8,128)(2,1)S(1)}) custom-call(s32[4]{0:T(128)S(1)} %pad_add_fusion.ids, bf16[2,256,768]{2,1,0:T(8,128)(2,1)S(1)} %get-tuple-element.173.q, bf16[256,768]{1,0:T(8,128)(2,1)S(1)} %get-tuple-element.170.refs_0_, ...), custom_call_target="tpu_custom_call", output_to_operand_aliasing={{0}: (7, {}), {1}: (8, {})} | custom-call | flops 1024 | bytes 917504 | tf_op jit(solution)/shard_map/attention/pallas_call | solution.py:455
  77.1 4.0 %collective-permute-done.27.received = bf16[2,192,768]{2,1,0:T(8,128)(2,1)S(1)} collective-permute-done((bf16[2,192,768]{2,1,0:T(8,128)(2,1)S(1)}, bf16[2,192,768]{2,1,0:T(8,128)(2,1)S(1)}, u32[]{:S(2)}, u32[]{:S(2)}) %collective-permute-start.27) | collective-permute-done | bytes 589856 | tf_op jit(solution)/shard_map/ppermute | solution.py:336
  84.0 1.5 collective-permute-start.28
  86.9 1.0 collective-permute-done.31.refs_4_
  88.8 10.1 %feed_up.1 = (f32[8,3072]{1,0:T(8,128)S(1)}, f32[512,768]{1,0:T(8,128)S(1)}, f32[512,128]{1,0:T(8,128)S(1)}, bf16[512,3072]{1,0:T(8,128)(2,1)S(1)}, bf16[512,3072]{1,0:T(8,128)(2,1)S(1)}) custom-call(s32[4]{0:T(128)S(1)} %pad_add_fusion.ids, bf16[4,128,768]{2,1,0:T(8,128)(2,1)} %copy-done.2, bf16[4,128,768]{2,1,0:T(8,128)(2,1)} %copy-done.32, ...), custom_call_target="tpu_custom_call" | custom-call | flops 1024 | bytes 1572864 | tf_op jit(solution)/shard_map/feed_up/pallas_call | solution.py:455
  98.9 0.8 collective-permute-done.28.refs_1_
  99.8 1.2 collective-permute-done.29.refs_3_
  101.5 1.5 collective-permute-done.36.refs_5_
  104.6 16.1 %feed_down.1 = (bf16[512,768]{1,0:T(8,128)(2,1)}, f32[512,768]{1,0:T(8,128)S(1)}, bf16[512,3072]{1,0:T(8,128)(2,1)S(1)}, bf16[16,96,768]{2,1,0:T(8,128)(2,1)S(1)...) custom-call(s32[4]{0:T(128)S(1)} %pad_add_fusion.ids, bf16[4,96,768]{2,1,0:T(8,128)(2,1)} %copy-done.27, ...), custom_call_target="tpu_custom_call" | custom-call | flops 1024 | bytes 2359296 | tf_op jit(solution)/shard_map/feed_down/pallas_call | solution.py:455
  120.7 1.1 copy-done.10
  122.0 5.1 %up_grads.1 = (bf16[16,96,768]{2,1,0:T(8,128)(2,1)S(1)}, bf16[16,96,768]{2,1,0:T(8,128)(2,1)S(1)}) custom-call(s32[4]{0:T(128)S(1)} %pad_add_fusion.ids, bf16[512,3072]{1,0:T(8,128)(2,1)S(1)} %get-tuple-element.208.g_inner.refs_10_, f32[512,768]{1,0:T(8,128)S(1)} %get-tuple-element.198.refs_10_.scaled.refs_12_, ...), custom_call_target="tpu_custom_call" | custom-call | flops 1024 | bytes 1310720 | tf_op jit(solution)/shard_map/up_grads/pallas_call | solution.py:455
  129.0 1.2 collective-permute-start.41
  130.2 10.5 %middle.1 = (f32[512,768]{1,0:T(8,128)S(1)}, bf16[512,768]{1,0:T(8,128)(2,1)S(1)}, bf16[16,24,768]{2,1,0:T(8,128)(2,1)S(1)}, bf16[16,24,768]{2,1,0:T(8,128)(2,1)S(1)}, f32[32,8,768]{2,1,0:T(8,128)S(1)}) custom-call(s32[4]{0:T(128)S(1)} %pad_add_fusion.ids, bf16[4,128,768]{2,1,0:T(8,128)(2,1)} %copy-done.2, bf16[4,128,768]{2,1,0:T(8,128)(2,1)} %copy-done.32, ...), custom_call_target="tpu_custom_call" | custom-call | flops 1024 | bytes 1179648 | tf_op jit(solution)/shard_map/middle/pallas_call | solution.py:455
  140.7 3.3 %collective-permute-done.41.refs_7_ = bf16[4,96,768]{2,1,0:T(8,128)(2,1)S(1)} collective-permute-done((bf16[4,96,768]{2,1,0:T(8,128)(2,1)S(1)}, bf16[4,96,768]{2,1,0:T(8,128)(2,1)S(1)}, u32[]{:S(2)}, u32[]{:S(2)}) %collective-permute-start.41) | collective-permute-done | bytes 589856 | tf_op jit(solution)/shard_map/ppermute | solution.py:336
  144.8 1.3 collective-permute-start.44
  146.1 0.8 collective-permute-start.45
  147.0 1.3 reduce_second.1
  148.3 1.8 collective-permute-start.50
  150.1 6.6 %attention_back.2 = (bf16[256,768]{1,0:T(8,128)(2,1)S(1)}, f32[256,768]{1,0:T(8,128)S(1)}, f32[256,768]{1,0:T(8,128)S(1)}, bf16[256,768]{1,0:T(8,128)(2,1)S(1)}, bf16[256,768]{1,0:T(8,128)(2,1)S(1)}) custom-call(s32[4]{0:T(128)S(1)} %pad_add_fusion.ids, bf16[2,256,768]{2,1,0:T(8,128)(2,1)S(1)} %get-tuple-element.173.q, ...), custom_call_target="tpu_custom_call" | custom-call | flops 1024 | bytes 1310720 | tf_op jit(solution)/shard_map/attention_back/pallas_call | solution.py:455
  156.8 1.0 reduce_sides.2
  157.8 1.3 collective-permute-start.51
  159.9 6.3 %attention_back.3 = (bf16[256,768]{1,0:T(8,128)(2,1)S(1)}, f32[256,768]{1,0:T(8,128)S(1)}, f32[256,768]{1,0:T(8,128)S(1)}, bf16[256,768]{1,0:T(8,128)(2,1)S(1)}, bf16[256,768]{1,0:T(8,128)(2,1)S(1)}) custom-call(s32[4]{0:T(128)S(1)} %pad_add_fusion.ids, bf16[2,256,768]{2,1,0:T(8,128)(2,1)S(1)} %get-tuple-element.173.q, ...), custom_call_target="tpu_custom_call" | custom-call | flops 1024 | bytes 1310720 | tf_op jit(solution)/shard_map/attention_back/pallas_call | solution.py:455
  167.5 1.9 collective-permute-start.53
  169.5 6.1 %input_grads.1 = (bf16[16,80,768]{2,1,0:T(8,128)(2,1)S(1)}, bf16[16,80,768]{2,1,0:T(8,128)(2,1)S(1)}, bf16[512,768]{1,0:T(8,128)(2,1)S(1)}, bf16[512,768]{1,0:T(8,128)(2,1)S(1)}, bf16[512,768]{1,0:T(8,128)(2,1)S(1)}) custom-call(s32[4]{0:T(128)S(1)} %pad_add_fusion.ids, bf16[512,768]{1,0:T(8,128)(2,1)S(1)} %bitcast.81, ...), custom_call_target="tpu_custom_call" | custom-call | flops 1024 | bytes 786432 | tf_op jit(solution)/shard_map/input_grads/pallas_call | solution.py:455
  175.6 8.5 %collective-permute-done.53.received = bf16[192,768]{1,0:T(8,128)(2,1)S(1)} collective-permute-done((bf16[192,768]{1,0:T(8,128)(2,1)S(1)}, bf16[192,768]{1,0:T(8,128)(2,1)S(1)}, u32[]{:S(2)}, u32[]{:S(2)}) %collective-permute-start.53) | collective-permute-done | bytes 294944 | tf_op jit(solution)/shard_map/ppermute | solution.py:336
  184.2 4.0 %collective-permute-done.54 = bf16[16,80,768]{2,1,0:T(8,128)(2,1)S(1)} collective-permute-done((bf16[16,80,768]{2,1,0:T(8,128)(2,1)S(1)}, bf16[16,80,768]{2,1,0:T(8,128)(2,1)S(1)}, u32[]{:S(2)}, u32[]{:S(2)}) %collective-permute-start.54) | collective-permute-done | bytes 1966112 | tf_op jit(solution)/shard_map/ppermute | solution.py:336
  188.8 1.0 collective-permute-start.55
  189.9 1.0 collective-permute-start.56
  190.9 1.2 reduce_depth.2
  192.2 3.4 %collective-permute-start.62 = (bf16[120,768]{1,0:T(8,128)(2,1)S(1)}, bf16[120,768]{1,0:T(8,128)(2,1)S(1)}, u32[]{:S(2)}, u32[]{:S(2)}) collective-permute-start(bf16[120,768]{1,0:T(8,128)(2,1)S(1)} %get-tuple-element.265), channel_id=1, source_target_pairs={{0,16},{8,24},{16,0},{24,8},{1,17},{9,25},{17,1},{25,9},{2,18},{10... | collective-permute-start | bytes 552968 | tf_op jit(solution)/shard_map/ppermute | solution.py:336
  195.5 1.0 collective-permute-start.63
  198.4 1.1 collective-permute-start.57
  199.5 1.4 collective-permute-start.58
  200.9 6.5 %input_back.1 = bf16[512,768]{1,0:T(8,128)(2,1)} custom-call(s32[4]{0:T(128)S(1)} %pad_add_fusion.ids, bf16[4,80,768]{2,1,0:T(8,128)(2,1)} %copy-done.3, bf16[4,80,768]{2,1,0:T(8,128)(2,1)} %copy-done.37, bf16[4,80,768]{2,1,0:T(8,128)(2,1)} %copy-done.36, bf16[4,40,768]{2,1,0:T(8,128)(2,1)} %copy-done.45, bf16[4,40,768]{2,1,0:T(8,128)(2,1)} %copy-done.46, ...), custom_call_target="tpu_custom_call" | custom-call | flops 1024 | bytes 655360 | tf_op jit(solution)/shard_map/input_back/pallas_call | solution.py:455
  207.4 1.6 collective-permute-done.62
  209.0 1.5 collective-permute-start.59
  212.5 0.9 collective-permute-done.59
  213.3 1.5 collective-permute-done.60
  214.9 0.9 reduce_depth.3
  215.8 3.2 %collective-permute-start.64 = (bf16[80,768]{1,0:T(8,128)(2,1)S(1)}, bf16[80,768]{1,0:T(8,128)(2,1)S(1)}, u32[]{:S(2)}, u32[]{:S(2)}) collective-permute-start(bf16[80,768]{1,0:T(8,128)(2,1)S(1)} %get-tuple-element.284), channel_id=1, source_target_pairs={{0,8},{8,0},{16,24},{24,16},{1,9},{9,1},{17,25},{25,17},{2,10},{10... | collective-permute-start | bytes 368648 | tf_op jit(solution)/shard_map/ppermute | solution.py:336
  219.0 1.1 collective-permute-start.65
  220.0 1.4 collective-permute-start.66
  222.2 6.5 %collective-permute-done.65 = bf16[80,768]{1,0:T(8,128)(2,1)S(1)} collective-permute-done((bf16[80,768]{1,0:T(8,128)(2,1)S(1)}, bf16[80,768]{1,0:T(8,128)(2,1)S(1)}, u32[]{:S(2)}, u32[]{:S(2)}) %collective-permute-start.65) | collective-permute-done | bytes 122912 | tf_op jit(solution)/shard_map/ppermute | solution.py:336
  (250 shorter events, 38.6 us)
Async XLA Ops:
  2.3 16.3 %collective-permute-start.4 = (bf16[80,768]{1,0:T(8,128)(2,1)S(1)}, bf16[80,768]{1,0:T(8,128)(2,1)S(1)}, u32[]{:S(2)}, u32[]{:S(2)}) collective-permute-start(bf16[80,768]{1,0:T(8,128)(2,1)S(1)} %concatenate.19.refs_0_), channel_id=1, source_target_pairs={{0,24},{8,16},{16,8},{24,0},{1,25},{9,17},{17,9},{25,1},{2,26},{10... | collective-permute-start | bytes 368648 | tf_op jit(solution)/shard_map/ppermute | solution.py:336
  7.4 11.2 %collective-permute-start.3 = (bf16[80,768]{1,0:T(8,128)(2,1)S(1)}, bf16[80,768]{1,0:T(8,128)(2,1)S(1)}, u32[]{:S(2)}, u32[]{:S(2)}) collective-permute-start(bf16[80,768]{1,0:T(8,128)(2,1)S(1)} %concatenate.19.refs_0_), channel_id=1, source_target_pairs={{0,16},{8,24},{16,0},{24,8},{1,17},{9,25},{17,1},{25,9},{2,18},{10... | collective-permute-start | bytes 368648 | tf_op jit(solution)/shard_map/ppermute | solution.py:336
  7.4 11.9 %collective-permute-start.2 = (bf16[80,768]{1,0:T(8,128)(2,1)S(1)}, bf16[80,768]{1,0:T(8,128)(2,1)S(1)}, u32[]{:S(2)}, u32[]{:S(2)}) collective-permute-start(bf16[80,768]{1,0:T(8,128)(2,1)S(1)} %concatenate.19.refs_0_), channel_id=1, source_target_pairs={{0,8},{8,0},{16,24},{24,16},{1,9},{9,1},{17,25},{25,17},{2,10},{10... | collective-permute-start | bytes 368648 | tf_op jit(solution)/shard_map/ppermute | solution.py:336
  9.0 9.6 %collective-permute-start = (bf16[48,768]{1,0:T(8,128)(2,1)S(1)}, bf16[48,768]{1,0:T(8,128)(2,1)S(1)}, u32[]{:S(2)}, u32[]{:S(2)}) collective-permute-start(bf16[48,768]{1,0:T(8,128)(2,1)S(1)} %get-tuple-element.322), channel_id=1, source_target_pairs={{0,2},{2,0},{1,3},{3,1},{4,6},{6,4},{5,7},{7,5},{8,10},{10,8},{9,1... | collective-permute-start | bytes 221192 | tf_op jit(solution)/shard_map/ppermute | solution.py:336
  10.7 7.9 %collective-permute-start.1 = (bf16[48,768]{1,0:T(8,128)(2,1)S(1)}, bf16[48,768]{1,0:T(8,128)(2,1)S(1)}, u32[]{:S(2)}, u32[]{:S(2)}) collective-permute-start(bf16[48,768]{1,0:T(8,128)(2,1)S(1)} %get-tuple-element.323), channel_id=1, source_target_pairs={{0,4},{4,0},{1,5},{5,1},{2,6},{6,2},{3,7},{7,3},{8,12},{12,8},{9,1... | collective-permute-start | bytes 221192 | tf_op jit(solution)/shard_map/ppermute | solution.py:336
  19.9 11.9 %collective-permute-start.6 = (bf16[4,80,768]{2,1,0:T(8,128)(2,1)S(1)}, bf16[4,80,768]{2,1,0:T(8,128)(2,1)S(1)}, u32[]{:S(2)}, u32[]{:S(2)}) collective-permute-start(bf16[4,80,768]{2,1,0:T(8,128)(2,1)S(1)} %order_four.1.refs_0_), channel_id=1, source_target_pairs={{0,4},{4,0},{1,5},{5,1},{2,6},{6,2},{3,7},{7,3},{8,12},{12,8},{9,1... | collective-permute-start | bytes 1474568 | tf_op jit(solution)/shard_map/ppermute | solution.py:336
  20.4 11.6 %collective-permute-start.5 = (bf16[4,80,768]{2,1,0:T(8,128)(2,1)S(1)}, bf16[4,80,768]{2,1,0:T(8,128)(2,1)S(1)}, u32[]{:S(2)}, u32[]{:S(2)}) collective-permute-start(bf16[4,80,768]{2,1,0:T(8,128)(2,1)S(1)} %order_four.1.refs_0_), channel_id=1, source_target_pairs={{0,2},{2,0},{1,3},{3,1},{4,6},{6,4},{5,7},{7,5},{8,10},{10,8},{9,1... | collective-permute-start | bytes 1474568 | tf_op jit(solution)/shard_map/ppermute | solution.py:336
  21.5 10.2 %collective-permute-start.7 = (bf16[128,768]{1,0:T(8,128)(2,1)S(1)}, bf16[128,768]{1,0:T(8,128)(2,1)S(1)}, u32[]{:S(2)}, u32[]{:S(2)}) collective-permute-start(bf16[128,768]{1,0:T(8,128)(2,1)S(1)} %concatenate.20.one), channel_id=1, source_target_pairs={{0,16},{8,24},{16,0},{24,8},{1,17},{9,25},{17,1},{25,9},{2,18},{10... | collective-permute-start | bytes 589832 | tf_op jit(solution)/shard_map/ppermute | solution.py:336
  32.0 7.2 %collective-permute-start.8 = (bf16[4,40,768]{2,1,0:T(8,128)(2,1)S(1)}, bf16[4,40,768]{2,1,0:T(8,128)(2,1)S(1)}, u32[]{:S(2)}, u32[]{:S(2)}) collective-permute-start(bf16[4,40,768]{2,1,0:T(8,128)(2,1)S(1)} %slice.98), channel_id=1, source_target_pairs={{0,4},{4,0},{1,5},{5,1},{2,6},{6,2},{3,7},{7,3},{8,12},{12,8},{9,1... | collective-permute-start | bytes 737288 | tf_op jit(solution)/shard_map/ppermute | solution.py:336
  33.5 15.2 %collective-permute-start.10 = (bf16[4,80,768]{2,1,0:T(8,128)(2,1)S(1)}, bf16[4,80,768]{2,1,0:T(8,128)(2,1)S(1)}, u32[]{:S(2)}, u32[]{:S(2)}) collective-permute-start(bf16[4,80,768]{2,1,0:T(8,128)(2,1)S(1)} %order_four.1.refs_0_), channel_id=1, source_target_pairs={{0,1},{1,0},{2,3},{3,2},{4,5},{5,4},{6,7},{7,6},{8,9},{9,8},{10,11... | collective-permute-start | bytes 1474568 | tf_op jit(solution)/shard_map/ppermute | solution.py:336
  34.0 11.6 %collective-permute-start.15 = (bf16[2,128,768]{2,1,0:T(8,128)(2,1)S(1)}, bf16[2,128,768]{2,1,0:T(8,128)(2,1)S(1)}, u32[]{:S(2)}, u32[]{:S(2)}) collective-permute-start(bf16[2,128,768]{2,1,0:T(8,128)(2,1)S(1)} %pair_z.2.pair), channel_id=1, source_target_pairs={{0,8},{8,0},{16,24},{24,16},{1,9},{9,1},{17,25},{25,17},{2,10},{10... | collective-permute-start | bytes 1179656 | tf_op jit(solution)/shard_map/ppermute | solution.py:336
  35.5 13.1 %collective-permute-start.11 = (bf16[4,80,768]{2,1,0:T(8,128)(2,1)S(1)}, bf16[4,80,768]{2,1,0:T(8,128)(2,1)S(1)}, u32[]{:S(2)}, u32[]{:S(2)}) collective-permute-start(bf16[4,80,768]{2,1,0:T(8,128)(2,1)S(1)} %collective-permute-done.5.refs_1_), channel_id=1, source_target_pairs={{0,1},{1,0},{2,3},{3,2},{4,5},{5,4},{6,7},{7,6},{8,9},{9,8},{10,11... | collective-permute-start | bytes 1474568 | tf_op jit(solution)/shard_map/ppermute | solution.py:336
  35.7 8.2 %collective-permute-start.9 = (bf16[4,40,768]{2,1,0:T(8,128)(2,1)S(1)}, bf16[4,40,768]{2,1,0:T(8,128)(2,1)S(1)}, u32[]{:S(2)}, u32[]{:S(2)}) collective-permute-start(bf16[4,40,768]{2,1,0:T(8,128)(2,1)S(1)} %slice.99), channel_id=1, source_target_pairs={{0,2},{2,0},{1,3},{3,1},{4,6},{6,4},{5,7},{7,5},{8,10},{10,8},{9,1... | collective-permute-start | bytes 737288 | tf_op jit(solution)/shard_map/ppermute | solution.py:336
  39.2 10.9 %collective-permute-start.12 = (bf16[4,80,768]{2,1,0:T(8,128)(2,1)S(1)}, bf16[4,80,768]{2,1,0:T(8,128)(2,1)S(1)}, u32[]{:S(2)}, u32[]{:S(2)}) collective-permute-start(bf16[4,80,768]{2,1,0:T(8,128)(2,1)S(1)} %collective-permute-done.6.refs_2_), channel_id=1, source_target_pairs={{0,1},{1,0},{2,3},{3,2},{4,5},{5,4},{6,7},{7,6},{8,9},{9,8},{10,11... | collective-permute-start | bytes 1474568 | tf_op jit(solution)/shard_map/ppermute | solution.py:336
  43.9 5.3 %collective-permute-start.14 = (bf16[4,40,768]{2,1,0:T(8,128)(2,1)S(1)}, bf16[4,40,768]{2,1,0:T(8,128)(2,1)S(1)}, u32[]{:S(2)}, u32[]{:S(2)}) collective-permute-start(bf16[4,40,768]{2,1,0:T(8,128)(2,1)S(1)} %collective-permute-done.9.refs_4_), channel_id=1, source_target_pairs={{0,1},{1,0},{2,3},{3,2},{4,5},{5,4},{6,7},{7,6},{8,9},{9,8},{10,11... | collective-permute-start | bytes 737288 | tf_op jit(solution)/shard_map/ppermute | solution.py:336
  46.3 15.9 %collective-permute-start.20 = (bf16[192,768]{1,0:T(8,128)(2,1)S(1)}, bf16[192,768]{1,0:T(8,128)(2,1)S(1)}, u32[]{:S(2)}, u32[]{:S(2)}) collective-permute-start(bf16[192,768]{1,0:T(8,128)(2,1)S(1)} %pad_maximum_fusion.one), channel_id=1, source_target_pairs={{0,16},{8,24},{16,0},{24,8},{1,17},{9,25},{17,1},{25,9},{2,18},{10... | collective-permute-start | bytes 884744 | tf_op jit(solution)/shard_map/ppermute | solution.py:336
  48.7 22.2 %collective-permute-start.22 = (bf16[4,128,768]{2,1,0:T(8,128)(2,1)S(1)}, bf16[4,128,768]{2,1,0:T(8,128)(2,1)S(1)}, u32[]{:S(2)}, u32[]{:S(2)}) collective-permute-start(bf16[4,128,768]{2,1,0:T(8,128)(2,1)S(1)} %order_z.1.refs_0_), channel_id=1, source_target_pairs={{0,4},{4,0},{1,5},{5,1},{2,6},{6,2},{3,7},{7,3},{8,12},{12,8},{9,1... | collective-permute-start | bytes 2359304 | tf_op jit(solution)/shard_map/ppermute | solution.py:336
  49.2 21.7 %collective-permute-start.21 = (bf16[4,128,768]{2,1,0:T(8,128)(2,1)S(1)}, bf16[4,128,768]{2,1,0:T(8,128)(2,1)S(1)}, u32[]{:S(2)}, u32[]{:S(2)}) collective-permute-start(bf16[4,128,768]{2,1,0:T(8,128)(2,1)S(1)} %order_z.1.refs_0_), channel_id=1, source_target_pairs={{0,2},{2,0},{1,3},{3,1},{4,6},{6,4},{5,7},{7,5},{8,10},{10,8},{9,1... | collective-permute-start | bytes 2359304 | tf_op jit(solution)/shard_map/ppermute | solution.py:336
  56.9 5.3 %collective-permute-start.16 = (bf16[128,768]{1,0:T(8,128)(2,1)S(1)}, bf16[128,768]{1,0:T(8,128)(2,1)S(1)}, u32[]{:S(2)}, u32[]{:S(2)}) collective-permute-start(bf16[128,768]{1,0:T(8,128)(2,1)S(1)} %get-tuple-element.164.refs_0_), channel_id=1, source_target_pairs={{0,1},{1,0},{2,3},{3,2},{4,5},{5,4},{6,7},{7,6},{8,9},{9,8},{10,11... | collective-permute-start | bytes 589832 | tf_op jit(solution)/shard_map/ppermute | solution.py:336
  57.1 5.6 %collective-permute-start.17 = (bf16[128,768]{1,0:T(8,128)(2,1)S(1)}, bf16[128,768]{1,0:T(8,128)(2,1)S(1)}, u32[]{:S(2)}, u32[]{:S(2)}) collective-permute-start(bf16[128,768]{1,0:T(8,128)(2,1)S(1)} %get-tuple-element.165.refs_1_), channel_id=1, source_target_pairs={{0,1},{1,0},{2,3},{3,2},{4,5},{5,4},{6,7},{7,6},{8,9},{9,8},{10,11... | collective-permute-start | bytes 589832 | tf_op jit(solution)/shard_map/ppermute | solution.py:336
  62.2 8.6 %collective-permute-start.23 = (bf16[256,768]{1,0:T(8,128)(2,1)S(1)}, bf16[256,768]{1,0:T(8,128)(2,1)S(1)}, u32[]{:S(2)}, u32[]{:S(2)}) collective-permute-start(bf16[256,768]{1,0:T(8,128)(2,1)S(1)} %get-tuple-element.170.refs_0_), channel_id=1, source_target_pairs={{0,1},{1,0},{2,3},{3,2},{4,5},{5,4},{6,7},{7,6},{8,9},{9,8},{10,11... | collective-permute-start | bytes 1179656 | tf_op jit(solution)/shard_map/ppermute | solution.py:336
  62.7 8.1 %collective-permute-start.24 = (bf16[256,768]{1,0:T(8,128)(2,1)S(1)}, bf16[256,768]{1,0:T(8,128)(2,1)S(1)}, u32[]{:S(2)}, u32[]{:S(2)}) collective-permute-start(bf16[256,768]{1,0:T(8,128)(2,1)S(1)} %get-tuple-element.171.refs_1_), channel_id=1, source_target_pairs={{0,1},{1,0},{2,3},{3,2},{4,5},{5,4},{6,7},{7,6},{8,9},{9,8},{10,11... | collective-permute-start | bytes 1179656 | tf_op jit(solution)/shard_map/ppermute | solution.py:336
  65.7 15.5 %collective-permute-start.27 = (bf16[2,192,768]{2,1,0:T(8,128)(2,1)S(1)}, bf16[2,192,768]{2,1,0:T(8,128)(2,1)S(1)}, u32[]{:S(2)}, u32[]{:S(2)}) collective-permute-start(bf16[2,192,768]{2,1,0:T(8,128)(2,1)S(1)} %pair_z.3.pair), channel_id=1, source_target_pairs={{0,8},{8,0},{16,24},{24,16},{1,9},{9,1},{17,25},{25,17},{2,10},{10... | collective-permute-start | bytes 1769480 | tf_op jit(solution)/shard_map/ppermute | solution.py:336
  71.0 11.0 %collective-permute-start.25 = (bf16[4,64,768]{2,1,0:T(8,128)(2,1)S(1)}, bf16[4,64,768]{2,1,0:T(8,128)(2,1)S(1)}, u32[]{:S(2)}, u32[]{:S(2)}) collective-permute-start(bf16[4,64,768]{2,1,0:T(8,128)(2,1)S(1)} %slice.100), channel_id=1, source_target_pairs={{0,4},{4,0},{1,5},{5,1},{2,6},{6,2},{3,7},{7,3},{8,12},{12,8},{9,1... | collective-permute-start | bytes 1179656 | tf_op jit(solution)/shard_map/ppermute | solution.py:336
  71.5 10.7 %collective-permute-start.26 = (bf16[4,64,768]{2,1,0:T(8,128)(2,1)S(1)}, bf16[4,64,768]{2,1,0:T(8,128)(2,1)S(1)}, u32[]{:S(2)}, u32[]{:S(2)}) collective-permute-start(bf16[4,64,768]{2,1,0:T(8,128)(2,1)S(1)} %slice.101), channel_id=1, source_target_pairs={{0,2},{2,0},{1,3},{3,1},{4,6},{6,4},{5,7},{7,5},{8,10},{10,8},{9,1... | collective-permute-start | bytes 1179656 | tf_op jit(solution)/shard_map/ppermute | solution.py:336
  82.3 1.8 collective-permute-start.33
  82.3 3.3 %collective-permute-start.34 = (bf16[4,64,768]{2,1,0:T(8,128)(2,1)S(1)}, bf16[4,64,768]{2,1,0:T(8,128)(2,1)S(1)}, u32[]{:S(2)}, u32[]{:S(2)}) collective-permute-start(bf16[4,64,768]{2,1,0:T(8,128)(2,1)S(1)} %collective-permute-done.26.refs_7_), channel_id=1, source_target_pairs={{0,1},{1,0},{2,3},{3,2},{4,5},{5,4},{6,7},{7,6},{8,9},{9,8},{10,11... | collective-permute-start | bytes 1179656 | tf_op jit(solution)/shard_map/ppermute | solution.py:336
  82.8 3.3 %collective-permute-start.32 = (bf16[4,128,768]{2,1,0:T(8,128)(2,1)S(1)}, bf16[4,128,768]{2,1,0:T(8,128)(2,1)S(1)}, u32[]{:S(2)}, u32[]{:S(2)}) collective-permute-start(bf16[4,128,768]{2,1,0:T(8,128)(2,1)S(1)} %collective-permute-done.22.refs_2_), channel_id=1, source_target_pairs={{0,1},{1,0},{2,3},{3,2},{4,5},{5,4},{6,7},{7,6},{8,9},{9,8},{10,11... | collective-permute-start | bytes 2359304 | tf_op jit(solution)/shard_map/ppermute | solution.py:336
  82.8 4.0 %collective-permute-start.30 = (bf16[4,128,768]{2,1,0:T(8,128)(2,1)S(1)}, bf16[4,128,768]{2,1,0:T(8,128)(2,1)S(1)}, u32[]{:S(2)}, u32[]{:S(2)}) collective-permute-start(bf16[4,128,768]{2,1,0:T(8,128)(2,1)S(1)} %order_z.1.refs_0_), channel_id=1, source_target_pairs={{0,1},{1,0},{2,3},{3,2},{4,5},{5,4},{6,7},{7,6},{8,9},{9,8},{10,11... | collective-permute-start | bytes 2359304 | tf_op jit(solution)/shard_map/ppermute | solution.py:336
  83.3 4.6 %collective-permute-start.31 = (bf16[4,128,768]{2,1,0:T(8,128)(2,1)S(1)}, bf16[4,128,768]{2,1,0:T(8,128)(2,1)S(1)}, u32[]{:S(2)}, u32[]{:S(2)}) collective-permute-start(bf16[4,128,768]{2,1,0:T(8,128)(2,1)S(1)} %collective-permute-done.21.refs_1_), channel_id=1, source_target_pairs={{0,1},{1,0},{2,3},{3,2},{4,5},{5,4},{6,7},{7,6},{8,9},{9,8},{10,11... | collective-permute-start | bytes 2359304 | tf_op jit(solution)/shard_map/ppermute | solution.py:336
  84.0 15.7 %collective-permute-start.28 = (bf16[4,96,768]{2,1,0:T(8,128)(2,1)S(1)}, bf16[4,96,768]{2,1,0:T(8,128)(2,1)S(1)}, u32[]{:S(2)}, u32[]{:S(2)}) collective-permute-start(bf16[4,96,768]{2,1,0:T(8,128)(2,1)S(1)} %get-tuple-element.189.refs_0_), channel_id=1, source_target_pairs={{0,4},{4,0},{1,5},{5,1},{2,6},{6,2},{3,7},{7,3},{8,12},{12,8},{9,1... | collective-permute-start | bytes 1769480 | tf_op jit(solution)/shard_map/ppermute | solution.py:336
  85.5 15.4 %collective-permute-start.29 = (bf16[4,96,768]{2,1,0:T(8,128)(2,1)S(1)}, bf16[4,96,768]{2,1,0:T(8,128)(2,1)S(1)}, u32[]{:S(2)}, u32[]{:S(2)}) collective-permute-start(bf16[4,96,768]{2,1,0:T(8,128)(2,1)S(1)} %get-tuple-element.190.refs_2_), channel_id=1, source_target_pairs={{0,2},{2,0},{1,3},{3,1},{4,6},{6,4},{5,7},{7,5},{8,10},{10,8},{9,1... | collective-permute-start | bytes 1769480 | tf_op jit(solution)/shard_map/ppermute | solution.py:336
  86.1 15.3 %collective-permute-start.35 = (bf16[4,96,768]{2,1,0:T(8,128)(2,1)S(1)}, bf16[4,96,768]{2,1,0:T(8,128)(2,1)S(1)}, u32[]{:S(2)}, u32[]{:S(2)}) collective-permute-start(bf16[4,96,768]{2,1,0:T(8,128)(2,1)S(1)} %get-tuple-element.189.refs_0_), channel_id=1, source_target_pairs={{0,1},{1,0},{2,3},{3,2},{4,5},{5,4},{6,7},{7,6},{8,9},{9,8},{10,11... | collective-permute-start | bytes 1769480 | tf_op jit(solution)/shard_map/ppermute | solution.py:336
  86.8 14.7 %collective-permute-start.37 = (bf16[4,96,768]{2,1,0:T(8,128)(2,1)S(1)}, bf16[4,96,768]{2,1,0:T(8,128)(2,1)S(1)}, u32[]{:S(2)}, u32[]{:S(2)}) collective-permute-start(bf16[4,96,768]{2,1,0:T(8,128)(2,1)S(1)} %get-tuple-element.190.refs_2_), channel_id=1, source_target_pairs={{0,1},{1,0},{2,3},{3,2},{4,5},{5,4},{6,7},{7,6},{8,9},{9,8},{10,11... | collective-permute-start | bytes 1769480 | tf_op jit(solution)/shard_map/ppermute | solution.py:336
  100.9 2.0 collective-permute-start.36
  100.9 2.8 %collective-permute-start.38 = (bf16[4,96,768]{2,1,0:T(8,128)(2,1)S(1)}, bf16[4,96,768]{2,1,0:T(8,128)(2,1)S(1)}, u32[]{:S(2)}, u32[]{:S(2)}) collective-permute-start(bf16[4,96,768]{2,1,0:T(8,128)(2,1)S(1)} %collective-permute-done.29.refs_3_), channel_id=1, source_target_pairs={{0,1},{1,0},{2,3},{3,2},{4,5},{5,4},{6,7},{7,6},{8,9},{9,8},{10,11... | collective-permute-start | bytes 1769480 | tf_op jit(solution)/shard_map/ppermute | solution.py:336
  121.8 5.2 %collective-permute-start.39 = (bf16[16,96,768]{2,1,0:T(8,128)(2,1)S(1)}, bf16[16,96,768]{2,1,0:T(8,128)(2,1)S(1)}, u32[]{:S(2)}, u32[]{:S(2)}) collective-permute-start(bf16[16,96,768]{2,1,0:T(8,128)(2,1)S(1)} %get-tuple-element.204), channel_id=1, source_target_pairs={{0,1},{1,0},{2,3},{3,2},{4,5},{5,4},{6,7},{7,6},{8,9},{9,8},{10,11... | collective-permute-start | bytes 7077896 | tf_op jit(solution)/shard_map/ppermute | solution.py:336
  127.9 16.1 %collective-permute-start.42 = (bf16[16,96,768]{2,1,0:T(8,128)(2,1)S(1)}, bf16[16,96,768]{2,1,0:T(8,128)(2,1)S(1)}, u32[]{:S(2)}, u32[]{:S(2)}) collective-permute-start(bf16[16,96,768]{2,1,0:T(8,128)(2,1)S(1)} %get-tuple-element.216), channel_id=1, source_target_pairs={{0,1},{1,0},{2,3},{3,2},{4,5},{5,4},{6,7},{7,6},{8,9},{9,8},{10,11... | collective-permute-start | bytes 7077896 | tf_op jit(solution)/shard_map/ppermute | solution.py:336
  128.4 15.7 %collective-permute-start.40 = (bf16[4,96,768]{2,1,0:T(8,128)(2,1)S(1)}, bf16[4,96,768]{2,1,0:T(8,128)(2,1)S(1)}, u32[]{:S(2)}, u32[]{:S(2)}) collective-permute-start(bf16[4,96,768]{2,1,0:T(8,128)(2,1)S(1)} %get-tuple-element.207), channel_id=1, source_target_pairs={{0,4},{4,0},{1,5},{5,1},{2,6},{6,2},{3,7},{7,3},{8,12},{12,8},{9,1... | collective-permute-start | bytes 1769480 | tf_op jit(solution)/shard_map/ppermute | solution.py:336
  129.0 15.1 %collective-permute-start.41 = (bf16[4,96,768]{2,1,0:T(8,128)(2,1)S(1)}, bf16[4,96,768]{2,1,0:T(8,128)(2,1)S(1)}, u32[]{:S(2)}, u32[]{:S(2)}) collective-permute-start(bf16[4,96,768]{2,1,0:T(8,128)(2,1)S(1)} %get-tuple-element.215), channel_id=1, source_target_pairs={{0,2},{2,0},{1,3},{3,1},{4,6},{6,4},{5,7},{7,5},{8,10},{10,8},{9,1... | collective-permute-start | bytes 1769480 | tf_op jit(solution)/shard_map/ppermute | solution.py:336
  140.7 3.4 %collective-permute-start.43 = (bf16[16,24,768]{2,1,0:T(8,128)(2,1)S(1)}, bf16[16,24,768]{2,1,0:T(8,128)(2,1)S(1)}, u32[]{:S(2)}, u32[]{:S(2)}) collective-permute-start(bf16[16,24,768]{2,1,0:T(8,128)(2,1)S(1)} %get-tuple-element.223), channel_id=1, source_target_pairs={{0,1},{1,0},{2,3},{3,2},{4,5},{5,4},{6,7},{7,6},{8,9},{9,8},{10,11... | collective-permute-start | bytes 1769480 | tf_op jit(solution)/shard_map/ppermute | solution.py:336
  144.8 11.9 %collective-permute-start.44 = (bf16[4,64,768]{2,1,0:T(8,128)(2,1)S(1)}, bf16[4,64,768]{2,1,0:T(8,128)(2,1)S(1)}, u32[]{:S(2)}, u32[]{:S(2)}) collective-permute-start(bf16[4,64,768]{2,1,0:T(8,128)(2,1)S(1)} %get-tuple-element.224), channel_id=1, source_target_pairs={{0,2},{2,0},{1,3},{3,1},{4,6},{6,4},{5,7},{7,5},{8,10},{10,8},{9,1... | collective-permute-start | bytes 1179656 | tf_op jit(solution)/shard_map/ppermute | solution.py:336
  146.1 10.5 %collective-permute-start.45 = (bf16[4,56,768]{2,1,0:T(8,128)(2,1)S(1)}, bf16[4,56,768]{2,1,0:T(8,128)(2,1)S(1)}, u32[]{:S(2)}, u32[]{:S(2)}) collective-permute-start(bf16[4,56,768]{2,1,0:T(8,128)(2,1)S(1)} %get-tuple-element.225), channel_id=1, source_target_pairs={{0,4},{4,0},{1,5},{5,1},{2,6},{6,2},{3,7},{7,3},{8,12},{12,8},{9,1... | collective-permute-start | bytes 1032200 | tf_op jit(solution)/shard_map/ppermute | solution.py:336
  148.3 18.0 %collective-permute-start.50 = (bf16[2,192,768]{2,1,0:T(8,128)(2,1)S(1)}, bf16[2,192,768]{2,1,0:T(8,128)(2,1)S(1)}, u32[]{:S(2)}, u32[]{:S(2)}) collective-permute-start(bf16[2,192,768]{2,1,0:T(8,128)(2,1)S(1)} %get-tuple-element.219), channel_id=1, source_target_pairs={{0,8},{8,0},{16,24},{24,16},{1,9},{9,1},{17,25},{25,17},{2,10},{10... | collective-permute-start | bytes 1769480 | tf_op jit(solution)/shard_map/ppermute | solution.py:336
  156.7 10.1 %collective-permute-start.46 = (bf16[256,768]{1,0:T(8,128)(2,1)S(1)}, bf16[256,768]{1,0:T(8,128)(2,1)S(1)}, u32[]{:S(2)}, u32[]{:S(2)}) collective-permute-start(bf16[256,768]{1,0:T(8,128)(2,1)S(1)} %get-tuple-element.239), channel_id=1, source_target_pairs={{0,1},{1,0},{2,3},{3,2},{4,5},{5,4},{6,7},{7,6},{8,9},{9,8},{10,11... | collective-permute-start | bytes 1179656 | tf_op jit(solution)/shard_map/ppermute | solution.py:336
  157.8 26.4 %collective-permute-start.51 = (bf16[4,120,768]{2,1,0:T(8,128)(2,1)S(1)}, bf16[4,120,768]{2,1,0:T(8,128)(2,1)S(1)}, u32[]{:S(2)}, u32[]{:S(2)}) collective-permute-start(bf16[4,120,768]{2,1,0:T(8,128)(2,1)S(1)} %get-tuple-element.230), channel_id=1, source_target_pairs={{0,4},{4,0},{1,5},{5,1},{2,6},{6,2},{3,7},{7,3},{8,12},{12,8},{9,1... | collective-permute-start | bytes 2211848 | tf_op jit(solution)/shard_map/ppermute | solution.py:336
  159.1 25.1 %collective-permute-start.52 = (bf16[4,120,768]{2,1,0:T(8,128)(2,1)S(1)}, bf16[4,120,768]{2,1,0:T(8,128)(2,1)S(1)}, u32[]{:S(2)}, u32[]{:S(2)}) collective-permute-start(bf16[4,120,768]{2,1,0:T(8,128)(2,1)S(1)} %get-tuple-element.231), channel_id=1, source_target_pairs={{0,2},{2,0},{1,3},{3,1},{4,6},{6,4},{5,7},{7,5},{8,10},{10,8},{9,1... | collective-permute-start | bytes 2211848 | tf_op jit(solution)/shard_map/ppermute | solution.py:336
  159.9 7.6 %collective-permute-start.47 = (bf16[256,768]{1,0:T(8,128)(2,1)S(1)}, bf16[256,768]{1,0:T(8,128)(2,1)S(1)}, u32[]{:S(2)}, u32[]{:S(2)}) collective-permute-start(bf16[256,768]{1,0:T(8,128)(2,1)S(1)} %get-tuple-element.241), channel_id=1, source_target_pairs={{0,1},{1,0},{2,3},{3,2},{4,5},{5,4},{6,7},{7,6},{8,9},{9,8},{10,11... | collective-permute-start | bytes 1179656 | tf_op jit(solution)/shard_map/ppermute | solution.py:336
  166.2 3.3 %collective-permute-start.48 = (bf16[256,768]{1,0:T(8,128)(2,1)S(1)}, bf16[256,768]{1,0:T(8,128)(2,1)S(1)}, u32[]{:S(2)}, u32[]{:S(2)}) collective-permute-start(bf16[256,768]{1,0:T(8,128)(2,1)S(1)} %get-tuple-element.244), channel_id=1, source_target_pairs={{0,1},{1,0},{2,3},{3,2},{4,5},{5,4},{6,7},{7,6},{8,9},{9,8},{10,11... | collective-permute-start | bytes 1179656 | tf_op jit(solution)/shard_map/ppermute | solution.py:336
  166.8 2.7 %collective-permute-start.49 = (bf16[256,768]{1,0:T(8,128)(2,1)S(1)}, bf16[256,768]{1,0:T(8,128)(2,1)S(1)}, u32[]{:S(2)}, u32[]{:S(2)}) collective-permute-start(bf16[256,768]{1,0:T(8,128)(2,1)S(1)} %get-tuple-element.245), channel_id=1, source_target_pairs={{0,1},{1,0},{2,3},{3,2},{4,5},{5,4},{6,7},{7,6},{8,9},{9,8},{10,11... | collective-permute-start | bytes 1179656 | tf_op jit(solution)/shard_map/ppermute | solution.py:336
  167.5 16.6 %collective-permute-start.53 = (bf16[192,768]{1,0:T(8,128)(2,1)S(1)}, bf16[192,768]{1,0:T(8,128)(2,1)S(1)}, u32[]{:S(2)}, u32[]{:S(2)}) collective-permute-start(bf16[192,768]{1,0:T(8,128)(2,1)S(1)} %get-tuple-element.248), channel_id=1, source_target_pairs={{0,16},{8,24},{16,0},{24,8},{1,17},{9,25},{17,1},{25,9},{2,18},{10... | collective-permute-start | bytes 884744 | tf_op jit(solution)/shard_map/ppermute | solution.py:336
  184.2 4.0 %collective-permute-start.54 = (bf16[16,80,768]{2,1,0:T(8,128)(2,1)S(1)}, bf16[16,80,768]{2,1,0:T(8,128)(2,1)S(1)}, u32[]{:S(2)}, u32[]{:S(2)}) collective-permute-start(bf16[16,80,768]{2,1,0:T(8,128)(2,1)S(1)} %get-tuple-element.260), channel_id=1, source_target_pairs={{0,1},{1,0},{2,3},{3,2},{4,5},{5,4},{6,7},{7,6},{8,9},{9,8},{10,11... | collective-permute-start | bytes 5898248 | tf_op jit(solution)/shard_map/ppermute | solution.py:336
  188.8 8.3 %collective-permute-start.55 = (bf16[4,40,768]{2,1,0:T(8,128)(2,1)S(1)}, bf16[4,40,768]{2,1,0:T(8,128)(2,1)S(1)}, u32[]{:S(2)}, u32[]{:S(2)}) collective-permute-start(bf16[4,40,768]{2,1,0:T(8,128)(2,1)S(1)} %get-tuple-element.261), channel_id=1, source_target_pairs={{0,2},{2,0},{1,3},{3,1},{4,6},{6,4},{5,7},{7,5},{8,10},{10,8},{9,1... | collective-permute-start | bytes 737288 | tf_op jit(solution)/shard_map/ppermute | solution.py:336
  189.9 7.7 %collective-permute-start.56 = (bf16[4,40,768]{2,1,0:T(8,128)(2,1)S(1)}, bf16[4,40,768]{2,1,0:T(8,128)(2,1)S(1)}, u32[]{:S(2)}, u32[]{:S(2)}) collective-permute-start(bf16[4,40,768]{2,1,0:T(8,128)(2,1)S(1)} %get-tuple-element.262), channel_id=1, source_target_pairs={{0,4},{4,0},{1,5},{5,1},{2,6},{6,2},{3,7},{7,3},{8,12},{12,8},{9,1... | collective-permute-start | bytes 737288 | tf_op jit(solution)/shard_map/ppermute | solution.py:336
  192.1 15.3 %collective-permute-start.61 = (bf16[120,768]{1,0:T(8,128)(2,1)S(1)}, bf16[120,768]{1,0:T(8,128)(2,1)S(1)}, u32[]{:S(2)}, u32[]{:S(2)}) collective-permute-start(bf16[120,768]{1,0:T(8,128)(2,1)S(1)} %get-tuple-element.264), channel_id=1, source_target_pairs={{0,8},{8,0},{16,24},{24,16},{1,9},{9,1},{17,25},{25,17},{2,10},{10... | collective-permute-start | bytes 552968 | tf_op jit(solution)/shard_map/ppermute | solution.py:336
  192.2 16.8 %collective-permute-start.62 = (bf16[120,768]{1,0:T(8,128)(2,1)S(1)}, bf16[120,768]{1,0:T(8,128)(2,1)S(1)}, u32[]{:S(2)}, u32[]{:S(2)}) collective-permute-start(bf16[120,768]{1,0:T(8,128)(2,1)S(1)} %get-tuple-element.265), channel_id=1, source_target_pairs={{0,16},{8,24},{16,0},{24,8},{1,17},{9,25},{17,1},{25,9},{2,18},{10... | collective-permute-start | bytes 552968 | tf_op jit(solution)/shard_map/ppermute | solution.py:336
  195.5 13.4 %collective-permute-start.63 = (bf16[120,768]{1,0:T(8,128)(2,1)S(1)}, bf16[120,768]{1,0:T(8,128)(2,1)S(1)}, u32[]{:S(2)}, u32[]{:S(2)}) collective-permute-start(bf16[120,768]{1,0:T(8,128)(2,1)S(1)} %get-tuple-element.266), channel_id=1, source_target_pairs={{0,24},{8,16},{16,8},{24,0},{1,25},{9,17},{17,9},{25,1},{2,26},{10... | collective-permute-start | bytes 552968 | tf_op jit(solution)/shard_map/ppermute | solution.py:336
  198.4 16.5 %collective-permute-start.57 = (bf16[4,80,768]{2,1,0:T(8,128)(2,1)S(1)}, bf16[4,80,768]{2,1,0:T(8,128)(2,1)S(1)}, u32[]{:S(2)}, u32[]{:S(2)}) collective-permute-start(bf16[4,80,768]{2,1,0:T(8,128)(2,1)S(1)} %get-tuple-element.269), channel_id=1, source_target_pairs={{0,4},{4,0},{1,5},{5,1},{2,6},{6,2},{3,7},{7,3},{8,12},{12,8},{9,1... | collective-permute-start | bytes 1474568 | tf_op jit(solution)/shard_map/ppermute | solution.py:336
  199.5 15.4 %collective-permute-start.58 = (bf16[4,80,768]{2,1,0:T(8,128)(2,1)S(1)}, bf16[4,80,768]{2,1,0:T(8,128)(2,1)S(1)}, u32[]{:S(2)}, u32[]{:S(2)}) collective-permute-start(bf16[4,80,768]{2,1,0:T(8,128)(2,1)S(1)} %get-tuple-element.270), channel_id=1, source_target_pairs={{0,2},{2,0},{1,3},{3,1},{4,6},{6,4},{5,7},{7,5},{8,10},{10,8},{9,1... | collective-permute-start | bytes 1474568 | tf_op jit(solution)/shard_map/ppermute | solution.py:336
  209.0 4.4 %collective-permute-start.59 = (bf16[48,768]{1,0:T(8,128)(2,1)S(1)}, bf16[48,768]{1,0:T(8,128)(2,1)S(1)}, u32[]{:S(2)}, u32[]{:S(2)}) collective-permute-start(bf16[48,768]{1,0:T(8,128)(2,1)S(1)} %get-tuple-element.274), channel_id=1, source_target_pairs={{0,2},{2,0},{1,3},{3,1},{4,6},{6,4},{5,7},{7,5},{8,10},{10,8},{9,1... | collective-permute-start | bytes 221192 | tf_op jit(solution)/shard_map/ppermute | solution.py:336
  210.5 4.4 %collective-permute-start.60 = (bf16[48,768]{1,0:T(8,128)(2,1)S(1)}, bf16[48,768]{1,0:T(8,128)(2,1)S(1)}, u32[]{:S(2)}, u32[]{:S(2)}) collective-permute-start(bf16[48,768]{1,0:T(8,128)(2,1)S(1)} %get-tuple-element.276), channel_id=1, source_target_pairs={{0,4},{4,0},{1,5},{5,1},{2,6},{6,2},{3,7},{7,3},{8,12},{12,8},{9,1... | collective-permute-start | bytes 221192 | tf_op jit(solution)/shard_map/ppermute | solution.py:336
  215.8 6.4 %collective-permute-start.64 = (bf16[80,768]{1,0:T(8,128)(2,1)S(1)}, bf16[80,768]{1,0:T(8,128)(2,1)S(1)}, u32[]{:S(2)}, u32[]{:S(2)}) collective-permute-start(bf16[80,768]{1,0:T(8,128)(2,1)S(1)} %get-tuple-element.284), channel_id=1, source_target_pairs={{0,8},{8,0},{16,24},{24,16},{1,9},{9,1},{17,25},{25,17},{2,10},{10... | collective-permute-start | bytes 368648 | tf_op jit(solution)/shard_map/ppermute | solution.py:336
  219.0 9.7 %collective-permute-start.65 = (bf16[80,768]{1,0:T(8,128)(2,1)S(1)}, bf16[80,768]{1,0:T(8,128)(2,1)S(1)}, u32[]{:S(2)}, u32[]{:S(2)}) collective-permute-start(bf16[80,768]{1,0:T(8,128)(2,1)S(1)} %get-tuple-element.285), channel_id=1, source_target_pairs={{0,16},{8,24},{16,0},{24,8},{1,17},{9,25},{17,1},{25,9},{2,18},{10... | collective-permute-start | bytes 368648 | tf_op jit(solution)/shard_map/ppermute | solution.py:336
  220.0 8.7 %collective-permute-start.66 = (bf16[80,768]{1,0:T(8,128)(2,1)S(1)}, bf16[80,768]{1,0:T(8,128)(2,1)S(1)}, u32[]{:S(2)}, u32[]{:S(2)}) collective-permute-start(bf16[80,768]{1,0:T(8,128)(2,1)S(1)} %get-tuple-element.286), channel_id=1, source_target_pairs={{0,24},{8,16},{16,8},{24,0},{1,25},{9,17},{17,9},{25,1},{2,26},{10... | collective-permute-start | bytes 368648 | tf_op jit(solution)/shard_map/ppermute | solution.py:336
  (64 other events, 516.6 us)
where the time goes:
time: 232 us; the launch traced here: 231 us
  Pallas kernels  96.3 us (42%)
  waiting for transfers between devices  59.2 us (26%)
  starting transfers between devices  54.3 us (23%)
  local copies, waits for them, and re-layouts  17.2 us (7%)
  other arithmetic  2.41 us (1%)
    pallas_call x27, Pallas kernels, call(): pl.pallas_call(body, grid_spec=pltpu.PrefetchScalarGridSpec(num_scalar_pr...  96.3 us
    ppermute x67, waiting for transfers between devices, pp(): return lax.ppermute(value, axis, [(i, i ^ step) for i in range(size)])  59.2 us
    ppermute x67, starting transfers between devices, pp(): return lax.ppermute(value, axis, [(i, i ^ step) for i in range(size)])  54.3 us
    unnamed x122, local copies, waits for them, and re-layouts  6.05 us
    pad x8, local copies, waits for them, and re-layouts, local(): jnp.pad(part.reshape(1, -1), ((0, 0), (0, width - part.shape[0])))  5.29 us
  transfers between devices with their start and end apart: 67, of which 26 were waited for; matrix products, arithmetic and copies ran while one was open for 4% of the time, Pallas kernels for 33%

commit v1 on v0

--- a/solution.py
+++ b/solution.py
@@ -986,13 +986,8 @@
         if n != 1:
             sums.append(jnp.sum(out[...].astype(f32), axis=0, keepdims=True))
         left = hidden if n == 0 else turned
-
-        def part(k, carry, left=left, out=out):
-            at = pl.ds(pl.multiple_of(k * 256, 256), 256)
-            total[at, :] = t_dot(left[:, at], out[...])
-            return carry
-
-        lax.fori_loop(0, width // 256, part, 0)
+        for start in range(0, width, 256):
+            total[start : start + 256, :] = t_dot(left[:, start : start + 256], out[...])
         hand_out(ids[0], total, width // 32, own, send, 0, n * (width // 32))
     bias[...] = block[...]
     unspread([jnp.concatenate(sums, axis=1)], [per], bias, 7)
@@ -1267,9 +1262,15 @@
 
 
 def second_body(ids, *refs):
-    here, at_y, at_x, (from_y, from_x, send, keep) = refs[:2], refs[2:4], refs[4:6], refs[6:]
+    here, at_y, at_x, (from_y, from_x, *outs) = refs[:2], refs[2:4], refs[4:6], refs[6:]
     half = from_y.shape[1] // 2
-    for k, (out, at) in enumerate(((keep, 0), (send, 0), (keep, 1), (send, 1))):
+    by_next, keep_next, by_far, keep_far = outs
+    for k, upper, lower in (
+        (0, (keep_next, 0), (keep_far, 0)),
+        (1, (by_next, 0), (keep_far, 1)),
+        (2, (keep_next, 1), (by_far, 0)),
+        (3, (by_next, 1), (by_far, 1)),
+    ):
         z = ids[3] ^ k
         plane = (z, 0, 0)
         quarters = (
@@ -1279,65 +1280,69 @@
             both(at_y, plane, half, 2 * half) + from_x[z, half:].astype(f32),
         )
         for i, quarter in enumerate(quarters):
-            out[at, i * half : (i + 1) * half] = quarter.astype(out.dtype)
+            out, at = upper if i < 2 else lower
+            out[at, i % 2 * half : (i % 2 + 1) * half] = quarter.astype(out.dtype)
 
 
 def reduce_second(ids, parts, from_y, from_x):
     shape = parts[0].shape
-    wide = (2, 2 * shape[3], shape[4])
+    wide = (2,) + shape[3:]
     return call(
         second_body,
         "reduce_second",
         (1,),
         (ids, *parts, *parts, *parts, from_y, from_x),
         [beside(shape, 0, 0)] * 2 + [beside(shape, 1, 0)] * 2 + [beside(shape, 0, 1)] * 2 + [WHOLE] * 2,
-        [shaped(wide, bf16), shaped(wide, f32)],
-        [WHOLE] * 2,
+        [shaped(wide, bf16), shaped(wide, f32)] * 2,
+        [WHOLE] * 4,
         [],
         14,
         3,
     )
 
 
-def quarter_body(ids, keep, received, send, mine):
-    mine[...] = keep[0] + received[0].astype(f32)
-    send[...] = (keep[1] + received[1].astype(f32)).astype(bf16)
-
-
-def reduce_third(ids, keep, received):
-    shape = keep.shape[1:]
-    return call(
-        quarter_body,
+def third_body(ids, keep_next, keep_far, next_in, far_in, next_mine, far_mine, to_far, to_next):
+    next_mine[...] = keep_next[0] + next_in[0].astype(f32)
+    to_far[...] = (keep_next[1] + next_in[1].astype(f32)).astype(bf16)
+    far_mine[...] = keep_far[0] + far_in[0].astype(f32)
+    to_next[...] = (keep_far[1] + far_in[1].astype(f32)).astype(bf16)
+
+
+def reduce_third(ids, keep_next, keep_far, next_in, far_in):
+    shape = keep_next.shape[1:]
+    return call(
+        third_body,
         "reduce_third",
         (1,),
-        (ids, keep, received),
-        [WHOLE] * 2,
-        [shaped(shape, bf16), shaped(shape, f32)],
-        [WHOLE] * 2,
+        (ids, keep_next, keep_far, next_in, far_in),
+        [WHOLE] * 4,
+        [shaped(shape, f32)] * 2 + [shaped(shape, bf16)] * 2,
+        [WHOLE] * 4,
         [],
         10,
         2,
     )
 
 
-def fourth_body(ids, mine, received, to_x, to_y, own):
+def fourth_body(ids, upper, lower, from_far, from_next, to_x, to_y, own):
     half = to_x.shape[0]
-    total = mine[...] + received[...].astype(f32)
-    own[:half] = total[:half]
-    own[half:] = total[2 * half : 3 * half]
-    to_x[...] = total[half : 2 * half].astype(bf16)
-    to_y[...] = total[3 * half :].astype(bf16)
-
-
-def reduce_fourth(ids, mine, received):
-    rows, width = mine.shape
+    first = upper[...] + from_far[...].astype(f32)
+    second = lower[...] + from_next[...].astype(f32)
+    own[:half] = first[:half]
+    own[half:] = second[:half]
+    to_x[...] = first[half:].astype(bf16)
+    to_y[...] = second[half:].astype(bf16)
+
+
+def reduce_fourth(ids, upper, lower, from_far, from_next):
+    rows, width = upper.shape
     return call(
         fourth_body,
         "reduce_fourth",
         (1,),
-        (ids, mine, received),
-        [WHOLE] * 2,
-        [shaped((rows // 4, width), bf16)] * 2 + [shaped((rows // 2, width), f32)],
+        (ids, upper, lower, from_far, from_next),
+        [WHOLE] * 4,
+        [shaped((rows // 2, width), bf16)] * 2 + [shaped((rows, width), f32)],
         [WHOLE] * 3,
         [],
         8,
@@ -1477,10 +1482,10 @@
     cut_m = (count_rows(mid) + 15) // 16 * 8
     corner = reduce_corner(ids, mid, cut_m)
     low, high = pp(corner[0], "x"), pp(corner[1], "y")
-    down_send, down_keep = reduce_second(ids, down, down_y, down_x)
-    down_near = pp(down_send, "z", 1)
+    to_next, keep_next, to_far, keep_far = reduce_second(ids, down, down_y, down_x)
+    next_in, far_in = pp(to_next, "z", 1), pp(to_far, "z", 2)
     first_q, *first_near, far_k, far_v = attention_back(
-        ids, 0, queries, near, far, signed, after(g_context, down_send, *corner)
+        ids, 0, queries, near, far, signed, after(g_context, to_next, *corner)
     )
     low, high = hold((low, high), first_q)
     first_far = [pp(after(value, low, high), "seq") for value in (far_k, far_v)]
@@ -1491,15 +1496,15 @@
     )
     first_far = hold(first_far, second_q)
     second_far = [pp(value, "seq") for value in (far_k, far_v)]
-    down_near = after(down_near, second_q)
-    down_send, down_mine = reduce_third(ids, down_keep, down_near)
-    down_far = pp(down_send, "z", 2)
-    grads = (first_q, second_q, *first_near, *second_near, *first_far, *hold(second_far, down_send))
+    next_in, far_in = hold((next_in, far_in), second_q)
+    upper, lower, to_far, to_next = reduce_third(ids, keep_next, keep_far, next_in, far_in)
+    far_in, next_in = pp(to_far, "z", 2), pp(to_next, "z", 1)
+    grads = (first_q, second_q, *first_near, *second_near, *first_far, *hold(second_far, to_far))
     a_own, a_send, g_q, g_keys, g_values = input_grads(ids, hidden, turned, grads, block, per)
     mid_y, mid_x = hold((mid_y, mid_x), a_send)
-    down_far = after(down_far, a_send)
-    core_sums = pp(after(a_send, mid_y, mid_x, down_far), "seq")
-    to_far_x, to_far_y, down_mine = reduce_fourth(ids, down_mine, down_far)
+    far_in, next_in = hold((far_in, next_in), a_send)
+    core_sums = pp(after(a_send, mid_y, mid_x, far_in, next_in), "seq")
+    to_far_x, to_far_y, down_mine = reduce_fourth(ids, upper, lower, far_in, next_in)
     part = [unit(a_own), unit(core_sums)]
     corner = reduce_corner(ids, part, cut_a)
     low, high = pp(corner[0], "x"), pp(corner[1], "y")

time: 232 us -> 228 us (0.983)
  waiting for transfers between devices: 59.2 us -> 55.3 us
    ppermute x67 -> x69, waiting for transfers between devices: 59.2 us -> 55.3 us  [pp(): return lax.ppermute(value, axis, [(i, i ^ step) for i in range(size)])]
    ppermute x67 -> x69, starting transfers between devices: 54.3 us -> 56.6 us  [pp(): return lax.ppermute(value, axis, [(i, i ^ step) for i in range(size)])]
  transfers between devices with their start and end apart: 67 -> 69, of which waited for: 26 -> 28; matrix products, arithmetic and copies ran while one was open for 4% -> 4% of each run, Pallas kernels for 33% -> 33%
where the time goes in v1:
time: 228 us
  Pallas kernels  94.5 us (41%)
  starting transfers between devices  56.6 us (25%)
  waiting for transfers between devices  55.3 us (24%)
  local copies, waits for them, and re-layouts  17.2 us (8%)
  other arithmetic  2.42 us (1%)
    pallas_call x27, Pallas kernels, call(): pl.pallas_call(body, grid_spec=pltpu.PrefetchScalarGridSpec(num_scalar_pr...  94.5 us
    ppermute x69, starting transfers between devices, pp(): return lax.ppermute(value, axis, [(i, i ^ step) for i in range(size)])  56.6 us
    ppermute x69, waiting for transfers between devices, pp(): return lax.ppermute(value, axis, [(i, i ^ step) for i in range(size)])  55.3 us
    unnamed x122, local copies, waits for them, and re-layouts  6.07 us
    pad x8, local copies, waits for them, and re-layouts, local(): jnp.pad(part.reshape(1, -1), ((0, 0), (0, width - part.shape[0])))  5.29 us
  transfers between devices with their start and end apart: 69, of which 28 were waited for; matrix products, arithmetic and copies ran while one was open for 4% of the time, Pallas kernels for 33%

profile of v1, /device:TPU:0, one launch (start us, length us, event | category | flops | bytes accessed | tf_op | source)
XLA Modules:
  0.0 227.7 jit_solution(6573675713681010234)
XLA Ops:
  0.7 0.9 fusion.4
  2.3 5.1 %collective-permute-start.4 = (bf16[80,768]{1,0:T(8,128)(2,1)S(1)}, bf16[80,768]{1,0:T(8,128)(2,1)S(1)}, u32[]{:S(2)}, u32[]{:S(2)}) collective-permute-start(bf16[80,768]{1,0:T(8,128)(2,1)S(1)} %concatenate.19.refs_0_), channel_id=1, source_target_pairs={{0,24},{8,16},{16,8},{24,0},{1,25},{9,17},{17,9},{25,1},{2,26},{10... | collective-permute-start | bytes 368648 | tf_op jit(solution)/shard_map/ppermute | solution.py:336
  8.0 0.9 fusion.3
  9.0 1.7 collective-permute-start
  10.7 1.5 collective-permute-start.1
  20.4 1.0 collective-permute-start.5
  21.5 1.6 collective-permute-start.7
  23.1 1.0 copy-done.30
  24.1 3.0 %prepare.1 = (bf16[512,768]{1,0:T(8,128)(2,1)S(1)}, bf16[512,768]{1,0:T(8,128)(2,1)S(1)}, bf16[512,768]{1,0:T(8,128)(2,1)S(1)}) custom-call(s32[4]{0:T(128)S(1)} %pad_add_fusion.ids, bf16[512,768]{1,0:T(8,128)(2,1)S(1)} %bitcast.78, s32[2,1,192,256]{3,2,1,0:T(8,128)S(1)} %bitcast.93, s32[2,1,192,256]{3,2,1,0:T(8,128)S(1)} %bitcast.94), custom_call_target="tpu_custom_call" | custom-call | flops 1024 | bytes 393216 | tf_op jit(solution)/shard_map/prepare/pallas_call | solution.py:455
  27.2 4.6 %collective-permute-done.7.two = bf16[128,768]{1,0:T(8,128)(2,1)S(1)} collective-permute-done((bf16[128,768]{1,0:T(8,128)(2,1)S(1)}, bf16[128,768]{1,0:T(8,128)(2,1)S(1)}, u32[]{:S(2)}, u32[]{:S(2)}) %collective-permute-start.7) | collective-permute-done | bytes 196640 | tf_op jit(solution)/shard_map/ppermute | solution.py:336
  32.0 1.4 collective-permute-start.8
  34.0 1.5 collective-permute-start.15
  36.3 2.9 %collective-permute-done.8.refs_3_ = bf16[4,40,768]{2,1,0:T(8,128)(2,1)S(1)} collective-permute-done((bf16[4,40,768]{2,1,0:T(8,128)(2,1)S(1)}, bf16[4,40,768]{2,1,0:T(8,128)(2,1)S(1)}, u32[]{:S(2)}, u32[]{:S(2)}) %collective-permute-start.8) | collective-permute-done | bytes 245792 | tf_op jit(solution)/shard_map/ppermute | solution.py:336
  39.2 4.7 %collective-permute-done.9.refs_4_ = bf16[4,40,768]{2,1,0:T(8,128)(2,1)S(1)} collective-permute-done((bf16[4,40,768]{2,1,0:T(8,128)(2,1)S(1)}, bf16[4,40,768]{2,1,0:T(8,128)(2,1)S(1)}, u32[]{:S(2)}, u32[]{:S(2)}) %collective-permute-start.9) | collective-permute-done | bytes 245792 | tf_op jit(solution)/shard_map/ppermute | solution.py:336
  44.0 1.6 collective-permute-done.15.received
  46.3 2.4 %collective-permute-start.20 = (bf16[192,768]{1,0:T(8,128)(2,1)S(1)}, bf16[192,768]{1,0:T(8,128)(2,1)S(1)}, u32[]{:S(2)}, u32[]{:S(2)}) collective-permute-start(bf16[192,768]{1,0:T(8,128)(2,1)S(1)} %pad_maximum_fusion.one), channel_id=1, source_target_pairs={{0,16},{8,24},{16,0},{24,8},{1,17},{9,25},{17,1},{25,9},{2,18},{10... | collective-permute-start | bytes 884744 | tf_op jit(solution)/shard_map/ppermute | solution.py:336
  51.6 5.2 %project.1 = (bf16[2,256,768]{2,1,0:T(8,128)(2,1)S(1)}, bf16[128,768]{1,0:T(8,128)(2,1)S(1)}, bf16[128,768]{1,0:T(8,128)(2,1)S(1)}, bf16[128,768]{1,0:T(8,128)(2...) custom-call(s32[4]{0:T(128)S(1)} %pad_add_fusion.ids, ...), custom_call_target="tpu_custom_call" | custom-call | flops 1024 | bytes 655360 | tf_op jit(solution)/shard_map/project/pallas_call | solution.py:455
  57.5 4.7 %collective-permute-done.20.two = bf16[192,768]{1,0:T(8,128)(2,1)S(1)} collective-permute-done((bf16[192,768]{1,0:T(8,128)(2,1)S(1)}, bf16[192,768]{1,0:T(8,128)(2,1)S(1)}, u32[]{:S(2)}, u32[]{:S(2)}) %collective-permute-start.20) | collective-permute-done | bytes 294944 | tf_op jit(solution)/shard_map/ppermute | solution.py:336
  63.8 1.3 collective-permute-done.19.refs_7_
  66.1 4.6 %attention.2 = (bf16[2,256,768]{2,1,0:T(8,128)(2,1)S(1)}, bf16[2,6,4,512,128]{4,3,2,1,0:T(8,128)(2,1)S(1)}) custom-call(s32[4]{0:T(128)S(1)} %pad_add_fusion.ids, bf16[2,256,768]{2,1,0:T(8,128)(2,1)S(1)} %get-tuple-element.179.q, bf16[128,768]{1,0:T(8,128)(2,1)S(1)} %get-tuple-element.170.refs_0_, bf16[128,768]{1,0:T(8,128)(2,1)S(1)} %get-tuple-element.171.refs_1_, ...), custom_call_target="tpu_custom_call" | custom-call | flops 1024 | bytes 917504 | tf_op jit(solution)/shard_map/attention/pallas_call | solution.py:455
  71.5 1.0 collective-permute-start.26
  72.5 4.5 %attention.3 = (bf16[2,256,768]{2,1,0:T(8,128)(2,1)S(1)}, bf16[2,6,4,512,128]{4,3,2,1,0:T(8,128)(2,1)S(1)}) custom-call(s32[4]{0:T(128)S(1)} %pad_add_fusion.ids, bf16[2,256,768]{2,1,0:T(8,128)(2,1)S(1)} %get-tuple-element.179.q, bf16[256,768]{1,0:T(8,128)(2,1)S(1)} %get-tuple-element.176.refs_0_, ...), custom_call_target="tpu_custom_call", output_to_operand_aliasing={{0}: (7, {}), {1}: (8, {})} | custom-call | flops 1024 | bytes 917504 | tf_op jit(solution)/shard_map/attention/pallas_call | solution.py:455
  77.1 4.0 %collective-permute-done.27.received = bf16[2,192,768]{2,1,0:T(8,128)(2,1)S(1)} collective-permute-done((bf16[2,192,768]{2,1,0:T(8,128)(2,1)S(1)}, bf16[2,192,768]{2,1,0:T(8,128)(2,1)S(1)}, u32[]{:S(2)}, u32[]{:S(2)}) %collective-permute-start.27) | collective-permute-done | bytes 589856 | tf_op jit(solution)/shard_map/ppermute | solution.py:336
  84.0 1.5 collective-permute-start.28
  86.9 1.0 collective-permute-done.31.refs_4_
  88.0 0.8 copy-done.35
  88.8 10.1 %feed_up.1 = (f32[8,3072]{1,0:T(8,128)S(1)}, f32[512,768]{1,0:T(8,128)S(1)}, f32[512,128]{1,0:T(8,128)S(1)}, bf16[512,3072]{1,0:T(8,128)(2,1)S(1)}, bf16[512,3072]{1,0:T(8,128)(2,1)S(1)}) custom-call(s32[4]{0:T(128)S(1)} %pad_add_fusion.ids, bf16[4,128,768]{2,1,0:T(8,128)(2,1)} %copy-done.2, bf16[4,128,768]{2,1,0:T(8,128)(2,1)} %copy-done.32, ...), custom_call_target="tpu_custom_call" | custom-call | flops 1024 | bytes 1572864 | tf_op jit(solution)/shard_map/feed_up/pallas_call | solution.py:455
  99.8 1.2 collective-permute-done.29.refs_3_
  101.5 1.5 collective-permute-done.36.refs_5_
  103.0 0.8 collective-permute-done.38.refs_7_
  104.6 16.1 %feed_down.1 = (bf16[512,768]{1,0:T(8,128)(2,1)}, f32[512,768]{1,0:T(8,128)S(1)}, bf16[512,3072]{1,0:T(8,128)(2,1)S(1)}, bf16[16,96,768]{2,1,0:T(8,128)(2,1)S(1)...) custom-call(s32[4]{0:T(128)S(1)} %pad_add_fusion.ids, bf16[4,96,768]{2,1,0:T(8,128)(2,1)} %copy-done.27, ...), custom_call_target="tpu_custom_call" | custom-call | flops 1024 | bytes 2359296 | tf_op jit(solution)/shard_map/feed_down/pallas_call | solution.py:455
  120.7 1.1 copy-done.10
  122.0 5.1 %up_grads.1 = (bf16[16,96,768]{2,1,0:T(8,128)(2,1)S(1)}, bf16[16,96,768]{2,1,0:T(8,128)(2,1)S(1)}) custom-call(s32[4]{0:T(128)S(1)} %pad_add_fusion.ids, bf16[512,3072]{1,0:T(8,128)(2,1)S(1)} %get-tuple-element.214.g_inner.refs_10_, f32[512,768]{1,0:T(8,128)S(1)} %get-tuple-element.204.refs_10_.scaled.refs_12_, ...), custom_call_target="tpu_custom_call" | custom-call | flops 1024 | bytes 1310720 | tf_op jit(solution)/shard_map/up_grads/pallas_call | solution.py:455
  129.0 1.2 collective-permute-start.41
  130.2 10.5 %middle.1 = (f32[512,768]{1,0:T(8,128)S(1)}, bf16[512,768]{1,0:T(8,128)(2,1)S(1)}, bf16[16,24,768]{2,1,0:T(8,128)(2,1)S(1)}, bf16[16,24,768]{2,1,0:T(8,128)(2,1)S(1)}, f32[32,8,768]{2,1,0:T(8,128)S(1)}) custom-call(s32[4]{0:T(128)S(1)} %pad_add_fusion.ids, bf16[4,128,768]{2,1,0:T(8,128)(2,1)} %copy-done.2, bf16[4,128,768]{2,1,0:T(8,128)(2,1)} %copy-done.32, ...), custom_call_target="tpu_custom_call" | custom-call | flops 1024 | bytes 1179648 | tf_op jit(solution)/shard_map/middle/pallas_call | solution.py:455
  140.7 3.3 %collective-permute-done.41.refs_7_ = bf16[4,96,768]{2,1,0:T(8,128)(2,1)S(1)} collective-permute-done((bf16[4,96,768]{2,1,0:T(8,128)(2,1)S(1)}, bf16[4,96,768]{2,1,0:T(8,128)(2,1)S(1)}, u32[]{:S(2)}, u32[]{:S(2)}) %collective-permute-start.41) | collective-permute-done | bytes 589856 | tf_op jit(solution)/shard_map/ppermute | solution.py:336
  144.8 1.3 collective-permute-start.44
  146.1 0.8 collective-permute-start.45
  147.0 1.3 reduce_second.1
  148.3 3.4 %collective-permute-start.51 = (bf16[2,96,768]{2,1,0:T(8,128)(2,1)S(1)}, bf16[2,96,768]{2,1,0:T(8,128)(2,1)S(1)}, u32[]{:S(2)}, u32[]{:S(2)}) collective-permute-start(bf16[2,96,768]{2,1,0:T(8,128)(2,1)S(1)} %get-tuple-element.254), channel_id=1, source_target_pairs={{0,16},{8,24},{16,0},{24,8},{1,17},{9,25},{17,1},{25,9},{2,18},{10... | collective-permute-start | bytes 884744 | tf_op jit(solution)/shard_map/ppermute | solution.py:336
  152.1 6.6 %attention_back.2 = (bf16[256,768]{1,0:T(8,128)(2,1)S(1)}, f32[256,768]{1,0:T(8,128)S(1)}, f32[256,768]{1,0:T(8,128)S(1)}, bf16[256,768]{1,0:T(8,128)(2,1)S(1)}, bf16[256,768]{1,0:T(8,128)(2,1)S(1)}) custom-call(s32[4]{0:T(128)S(1)} %pad_add_fusion.ids, bf16[2,256,768]{2,1,0:T(8,128)(2,1)S(1)} %get-tuple-element.179.q, ...), custom_call_target="tpu_custom_call" | custom-call | flops 1024 | bytes 1310720 | tf_op jit(solution)/shard_map/attention_back/pallas_call | solution.py:455
  158.8 1.0 reduce_sides.2
  160.3 1.5 collective-permute-start.53
  161.8 6.3 %attention_back.3 = (bf16[256,768]{1,0:T(8,128)(2,1)S(1)}, f32[256,768]{1,0:T(8,128)S(1)}, f32[256,768]{1,0:T(8,128)S(1)}, bf16[256,768]{1,0:T(8,128)(2,1)S(1)}, bf16[256,768]{1,0:T(8,128)(2,1)S(1)}) custom-call(s32[4]{0:T(128)S(1)} %pad_add_fusion.ids, bf16[2,256,768]{2,1,0:T(8,128)(2,1)S(1)} %get-tuple-element.179.q, ...), custom_call_target="tpu_custom_call" | custom-call | flops 1024 | bytes 1310720 | tf_op jit(solution)/shard_map/attention_back/pallas_call | solution.py:455
  169.9 1.7 collective-permute-start.55
  171.7 4.4 %input_grads.1 = (bf16[16,80,768]{2,1,0:T(8,128)(2,1)S(1)}, bf16[16,80,768]{2,1,0:T(8,128)(2,1)S(1)}, bf16[512,768]{1,0:T(8,128)(2,1)S(1)}, bf16[512,768]{1,0:T(8,128)(2,1)S(1)}, bf16[512,768]{1,0:T(8,128)(2,1)S(1)}) custom-call(s32[4]{0:T(128)S(1)} %pad_add_fusion.ids, bf16[512,768]{1,0:T(8,128)(2,1)S(1)} %bitcast.81, ...), custom_call_target="tpu_custom_call" | custom-call | flops 1024 | bytes 786432 | tf_op jit(solution)/shard_map/input_grads/pallas_call | solution.py:455
  176.1 1.0 collective-permute-done.55.from_next
  177.1 4.2 %collective-permute-done.54.from_far = bf16[96,768]{1,0:T(8,128)(2,1)S(1)} collective-permute-done((bf16[96,768]{1,0:T(8,128)(2,1)S(1)}, bf16[96,768]{1,0:T(8,128)(2,1)S(1)}, u32[]{:S(2)}, u32[]{:S(2)}) %collective-permute-start.54) | collective-permute-done | bytes 147488 | tf_op jit(solution)/shard_map/ppermute | solution.py:336
  181.3 4.0 %collective-permute-done.56 = bf16[16,80,768]{2,1,0:T(8,128)(2,1)S(1)} collective-permute-done((bf16[16,80,768]{2,1,0:T(8,128)(2,1)S(1)}, bf16[16,80,768]{2,1,0:T(8,128)(2,1)S(1)}, u32[]{:S(2)}, u32[]{:S(2)}) %collective-permute-start.56) | collective-permute-done | bytes 1966112 | tf_op jit(solution)/shard_map/ppermute | solution.py:336
  186.6 1.5 collective-permute-start.58
  188.1 1.2 reduce_depth.2
  189.9 3.8 %collective-permute-start.65 = (bf16[120,768]{1,0:T(8,128)(2,1)S(1)}, bf16[120,768]{1,0:T(8,128)(2,1)S(1)}, u32[]{:S(2)}, u32[]{:S(2)}) collective-permute-start(bf16[120,768]{1,0:T(8,128)(2,1)S(1)} %get-tuple-element.277), channel_id=1, source_target_pairs={{0,24},{8,16},{16,8},{24,0},{1,25},{9,17},{17,9},{25,1},{2,26},{10... | collective-permute-start | bytes 552968 | tf_op jit(solution)/shard_map/ppermute | solution.py:336
  195.2 1.5 collective-permute-start.59
  196.7 1.5 collective-permute-start.60
  198.2 6.5 %input_back.1 = bf16[512,768]{1,0:T(8,128)(2,1)} custom-call(s32[4]{0:T(128)S(1)} %pad_add_fusion.ids, bf16[4,80,768]{2,1,0:T(8,128)(2,1)} %copy-done.3, bf16[4,80,768]{2,1,0:T(8,128)(2,1)} %copy-done.37, bf16[4,80,768]{2,1,0:T(8,128)(2,1)} %copy-done.36, bf16[4,40,768]{2,1,0:T(8,128)(2,1)} %copy-done.45, bf16[4,40,768]{2,1,0:T(8,128)(2,1)} %copy-done.46, ...), custom_call_target="tpu_custom_call" | custom-call | flops 1024 | bytes 655360 | tf_op jit(solution)/shard_map/input_back/pallas_call | solution.py:455
  204.7 1.1 collective-permute-done.64
  205.8 1.4 collective-permute-start.61
  209.2 1.0 collective-permute-done.61
  210.2 1.4 collective-permute-done.62
  211.6 0.9 reduce_depth.3
  212.5 3.3 %collective-permute-start.66 = (bf16[80,768]{1,0:T(8,128)(2,1)S(1)}, bf16[80,768]{1,0:T(8,128)(2,1)S(1)}, u32[]{:S(2)}, u32[]{:S(2)}) collective-permute-start(bf16[80,768]{1,0:T(8,128)(2,1)S(1)} %get-tuple-element.296), channel_id=1, source_target_pairs={{0,8},{8,0},{16,24},{24,16},{1,9},{9,1},{17,25},{25,17},{2,10},{10... | collective-permute-start | bytes 368648 | tf_op jit(solution)/shard_map/ppermute | solution.py:336
  215.8 2.4 %collective-permute-start.68 = (bf16[80,768]{1,0:T(8,128)(2,1)S(1)}, bf16[80,768]{1,0:T(8,128)(2,1)S(1)}, u32[]{:S(2)}, u32[]{:S(2)}) collective-permute-start(bf16[80,768]{1,0:T(8,128)(2,1)S(1)} %get-tuple-element.298), channel_id=1, source_target_pairs={{0,24},{8,16},{16,8},{24,0},{1,25},{9,17},{17,9},{25,1},{2,26},{10... | collective-permute-start | bytes 368648 | tf_op jit(solution)/shard_map/ppermute | solution.py:336
  218.9 2.2 collective-permute-done.66
  221.2 4.2 %collective-permute-done.67 = bf16[80,768]{1,0:T(8,128)(2,1)S(1)} collective-permute-done((bf16[80,768]{1,0:T(8,128)(2,1)S(1)}, bf16[80,768]{1,0:T(8,128)(2,1)S(1)}, u32[]{:S(2)}, u32[]{:S(2)}) %collective-permute-start.67) | collective-permute-done | bytes 122912 | tf_op jit(solution)/shard_map/ppermute | solution.py:336
  (254 shorter events, 39.2 us)
Async XLA Ops:
  2.3 16.3 %collective-permute-start.4 = (bf16[80,768]{1,0:T(8,128)(2,1)S(1)}, bf16[80,768]{1,0:T(8,128)(2,1)S(1)}, u32[]{:S(2)}, u32[]{:S(2)}) collective-permute-start(bf16[80,768]{1,0:T(8,128)(2,1)S(1)} %concatenate.19.refs_0_), channel_id=1, source_target_pairs={{0,24},{8,16},{16,8},{24,0},{1,25},{9,17},{17,9},{25,1},{2,26},{10... | collective-permute-start | bytes 368648 | tf_op jit(solution)/shard_map/ppermute | solution.py:336
  7.4 11.2 %collective-permute-start.3 = (bf16[80,768]{1,0:T(8,128)(2,1)S(1)}, bf16[80,768]{1,0:T(8,128)(2,1)S(1)}, u32[]{:S(2)}, u32[]{:S(2)}) collective-permute-start(bf16[80,768]{1,0:T(8,128)(2,1)S(1)} %concatenate.19.refs_0_), channel_id=1, source_target_pairs={{0,16},{8,24},{16,0},{24,8},{1,17},{9,25},{17,1},{25,9},{2,18},{10... | collective-permute-start | bytes 368648 | tf_op jit(solution)/shard_map/ppermute | solution.py:336
  7.4 11.9 %collective-permute-start.2 = (bf16[80,768]{1,0:T(8,128)(2,1)S(1)}, bf16[80,768]{1,0:T(8,128)(2,1)S(1)}, u32[]{:S(2)}, u32[]{:S(2)}) collective-permute-start(bf16[80,768]{1,0:T(8,128)(2,1)S(1)} %concatenate.19.refs_0_), channel_id=1, source_target_pairs={{0,8},{8,0},{16,24},{24,16},{1,9},{9,1},{17,25},{25,17},{2,10},{10... | collective-permute-start | bytes 368648 | tf_op jit(solution)/shard_map/ppermute | solution.py:336
  9.0 9.6 %collective-permute-start = (bf16[48,768]{1,0:T(8,128)(2,1)S(1)}, bf16[48,768]{1,0:T(8,128)(2,1)S(1)}, u32[]{:S(2)}, u32[]{:S(2)}) collective-permute-start(bf16[48,768]{1,0:T(8,128)(2,1)S(1)} %get-tuple-element.334), channel_id=1, source_target_pairs={{0,2},{2,0},{1,3},{3,1},{4,6},{6,4},{5,7},{7,5},{8,10},{10,8},{9,1... | collective-permute-start | bytes 221192 | tf_op jit(solution)/shard_map/ppermute | solution.py:336
  10.7 7.9 %collective-permute-start.1 = (bf16[48,768]{1,0:T(8,128)(2,1)S(1)}, bf16[48,768]{1,0:T(8,128)(2,1)S(1)}, u32[]{:S(2)}, u32[]{:S(2)}) collective-permute-start(bf16[48,768]{1,0:T(8,128)(2,1)S(1)} %get-tuple-element.335), channel_id=1, source_target_pairs={{0,4},{4,0},{1,5},{5,1},{2,6},{6,2},{3,7},{7,3},{8,12},{12,8},{9,1... | collective-permute-start | bytes 221192 | tf_op jit(solution)/shard_map/ppermute | solution.py:336
  19.9 11.9 %collective-permute-start.6 = (bf16[4,80,768]{2,1,0:T(8,128)(2,1)S(1)}, bf16[4,80,768]{2,1,0:T(8,128)(2,1)S(1)}, u32[]{:S(2)}, u32[]{:S(2)}) collective-permute-start(bf16[4,80,768]{2,1,0:T(8,128)(2,1)S(1)} %order_four.1.refs_0_), channel_id=1, source_target_pairs={{0,4},{4,0},{1,5},{5,1},{2,6},{6,2},{3,7},{7,3},{8,12},{12,8},{9,1... | collective-permute-start | bytes 1474568 | tf_op jit(solution)/shard_map/ppermute | solution.py:336
  20.4 11.6 %collective-permute-start.5 = (bf16[4,80,768]{2,1,0:T(8,128)(2,1)S(1)}, bf16[4,80,768]{2,1,0:T(8,128)(2,1)S(1)}, u32[]{:S(2)}, u32[]{:S(2)}) collective-permute-start(bf16[4,80,768]{2,1,0:T(8,128)(2,1)S(1)} %order_four.1.refs_0_), channel_id=1, source_target_pairs={{0,2},{2,0},{1,3},{3,1},{4,6},{6,4},{5,7},{7,5},{8,10},{10,8},{9,1... | collective-permute-start | bytes 1474568 | tf_op jit(solution)/shard_map/ppermute | solution.py:336
  21.5 10.2 %collective-permute-start.7 = (bf16[128,768]{1,0:T(8,128)(2,1)S(1)}, bf16[128,768]{1,0:T(8,128)(2,1)S(1)}, u32[]{:S(2)}, u32[]{:S(2)}) collective-permute-start(bf16[128,768]{1,0:T(8,128)(2,1)S(1)} %concatenate.20.one), channel_id=1, source_target_pairs={{0,16},{8,24},{16,0},{24,8},{1,17},{9,25},{17,1},{25,9},{2,18},{10... | collective-permute-start | bytes 589832 | tf_op jit(solution)/shard_map/ppermute | solution.py:336
  32.0 7.2 %collective-permute-start.8 = (bf16[4,40,768]{2,1,0:T(8,128)(2,1)S(1)}, bf16[4,40,768]{2,1,0:T(8,128)(2,1)S(1)}, u32[]{:S(2)}, u32[]{:S(2)}) collective-permute-start(bf16[4,40,768]{2,1,0:T(8,128)(2,1)S(1)} %slice.98), channel_id=1, source_target_pairs={{0,4},{4,0},{1,5},{5,1},{2,6},{6,2},{3,7},{7,3},{8,12},{12,8},{9,1... | collective-permute-start | bytes 737288 | tf_op jit(solution)/shard_map/ppermute | solution.py:336
  33.5 15.2 %collective-permute-start.10 = (bf16[4,80,768]{2,1,0:T(8,128)(2,1)S(1)}, bf16[4,80,768]{2,1,0:T(8,128)(2,1)S(1)}, u32[]{:S(2)}, u32[]{:S(2)}) collective-permute-start(bf16[4,80,768]{2,1,0:T(8,128)(2,1)S(1)} %order_four.1.refs_0_), channel_id=1, source_target_pairs={{0,1},{1,0},{2,3},{3,2},{4,5},{5,4},{6,7},{7,6},{8,9},{9,8},{10,11... | collective-permute-start | bytes 1474568 | tf_op jit(solution)/shard_map/ppermute | solution.py:336
  34.0 11.6 %collective-permute-start.15 = (bf16[2,128,768]{2,1,0:T(8,128)(2,1)S(1)}, bf16[2,128,768]{2,1,0:T(8,128)(2,1)S(1)}, u32[]{:S(2)}, u32[]{:S(2)}) collective-permute-start(bf16[2,128,768]{2,1,0:T(8,128)(2,1)S(1)} %pair_z.2.pair), channel_id=1, source_target_pairs={{0,8},{8,0},{16,24},{24,16},{1,9},{9,1},{17,25},{25,17},{2,10},{10... | collective-permute-start | bytes 1179656 | tf_op jit(solution)/shard_map/ppermute | solution.py:336
  35.5 13.1 %collective-permute-start.11 = (bf16[4,80,768]{2,1,0:T(8,128)(2,1)S(1)}, bf16[4,80,768]{2,1,0:T(8,128)(2,1)S(1)}, u32[]{:S(2)}, u32[]{:S(2)}) collective-permute-start(bf16[4,80,768]{2,1,0:T(8,128)(2,1)S(1)} %collective-permute-done.5.refs_1_), channel_id=1, source_target_pairs={{0,1},{1,0},{2,3},{3,2},{4,5},{5,4},{6,7},{7,6},{8,9},{9,8},{10,11... | collective-permute-start | bytes 1474568 | tf_op jit(solution)/shard_map/ppermute | solution.py:336
  35.7 8.2 %collective-permute-start.9 = (bf16[4,40,768]{2,1,0:T(8,128)(2,1)S(1)}, bf16[4,40,768]{2,1,0:T(8,128)(2,1)S(1)}, u32[]{:S(2)}, u32[]{:S(2)}) collective-permute-start(bf16[4,40,768]{2,1,0:T(8,128)(2,1)S(1)} %slice.99), channel_id=1, source_target_pairs={{0,2},{2,0},{1,3},{3,1},{4,6},{6,4},{5,7},{7,5},{8,10},{10,8},{9,1... | collective-permute-start | bytes 737288 | tf_op jit(solution)/shard_map/ppermute | solution.py:336
  39.2 10.9 %collective-permute-start.12 = (bf16[4,80,768]{2,1,0:T(8,128)(2,1)S(1)}, bf16[4,80,768]{2,1,0:T(8,128)(2,1)S(1)}, u32[]{:S(2)}, u32[]{:S(2)}) collective-permute-start(bf16[4,80,768]{2,1,0:T(8,128)(2,1)S(1)} %collective-permute-done.6.refs_2_), channel_id=1, source_target_pairs={{0,1},{1,0},{2,3},{3,2},{4,5},{5,4},{6,7},{7,6},{8,9},{9,8},{10,11... | collective-permute-start | bytes 1474568 | tf_op jit(solution)/shard_map/ppermute | solution.py:336
  43.9 5.3 %collective-permute-start.14 = (bf16[4,40,768]{2,1,0:T(8,128)(2,1)S(1)}, bf16[4,40,768]{2,1,0:T(8,128)(2,1)S(1)}, u32[]{:S(2)}, u32[]{:S(2)}) collective-permute-start(bf16[4,40,768]{2,1,0:T(8,128)(2,1)S(1)} %collective-permute-done.9.refs_4_), channel_id=1, source_target_pairs={{0,1},{1,0},{2,3},{3,2},{4,5},{5,4},{6,7},{7,6},{8,9},{9,8},{10,11... | collective-permute-start | bytes 737288 | tf_op jit(solution)/shard_map/ppermute | solution.py:336
  46.3 15.9 %collective-permute-start.20 = (bf16[192,768]{1,0:T(8,128)(2,1)S(1)}, bf16[192,768]{1,0:T(8,128)(2,1)S(1)}, u32[]{:S(2)}, u32[]{:S(2)}) collective-permute-start(bf16[192,768]{1,0:T(8,128)(2,1)S(1)} %pad_maximum_fusion.one), channel_id=1, source_target_pairs={{0,16},{8,24},{16,0},{24,8},{1,17},{9,25},{17,1},{25,9},{2,18},{10... | collective-permute-start | bytes 884744 | tf_op jit(solution)/shard_map/ppermute | solution.py:336
  48.7 22.2 %collective-permute-start.22 = (bf16[4,128,768]{2,1,0:T(8,128)(2,1)S(1)}, bf16[4,128,768]{2,1,0:T(8,128)(2,1)S(1)}, u32[]{:S(2)}, u32[]{:S(2)}) collective-permute-start(bf16[4,128,768]{2,1,0:T(8,128)(2,1)S(1)} %order_z.1.refs_0_), channel_id=1, source_target_pairs={{0,4},{4,0},{1,5},{5,1},{2,6},{6,2},{3,7},{7,3},{8,12},{12,8},{9,1... | collective-permute-start | bytes 2359304 | tf_op jit(solution)/shard_map/ppermute | solution.py:336
  49.2 21.7 %collective-permute-start.21 = (bf16[4,128,768]{2,1,0:T(8,128)(2,1)S(1)}, bf16[4,128,768]{2,1,0:T(8,128)(2,1)S(1)}, u32[]{:S(2)}, u32[]{:S(2)}) collective-permute-start(bf16[4,128,768]{2,1,0:T(8,128)(2,1)S(1)} %order_z.1.refs_0_), channel_id=1, source_target_pairs={{0,2},{2,0},{1,3},{3,1},{4,6},{6,4},{5,7},{7,5},{8,10},{10,8},{9,1... | collective-permute-start | bytes 2359304 | tf_op jit(solution)/shard_map/ppermute | solution.py:336
  56.9 5.3 %collective-permute-start.16 = (bf16[128,768]{1,0:T(8,128)(2,1)S(1)}, bf16[128,768]{1,0:T(8,128)(2,1)S(1)}, u32[]{:S(2)}, u32[]{:S(2)}) collective-permute-start(bf16[128,768]{1,0:T(8,128)(2,1)S(1)} %get-tuple-element.170.refs_0_), channel_id=1, source_target_pairs={{0,1},{1,0},{2,3},{3,2},{4,5},{5,4},{6,7},{7,6},{8,9},{9,8},{10,11... | collective-permute-start | bytes 589832 | tf_op jit(solution)/shard_map/ppermute | solution.py:336
  57.1 5.6 %collective-permute-start.17 = (bf16[128,768]{1,0:T(8,128)(2,1)S(1)}, bf16[128,768]{1,0:T(8,128)(2,1)S(1)}, u32[]{:S(2)}, u32[]{:S(2)}) collective-permute-start(bf16[128,768]{1,0:T(8,128)(2,1)S(1)} %get-tuple-element.171.refs_1_), channel_id=1, source_target_pairs={{0,1},{1,0},{2,3},{3,2},{4,5},{5,4},{6,7},{7,6},{8,9},{9,8},{10,11... | collective-permute-start | bytes 589832 | tf_op jit(solution)/shard_map/ppermute | solution.py:336
  62.2 8.6 %collective-permute-start.23 = (bf16[256,768]{1,0:T(8,128)(2,1)S(1)}, bf16[256,768]{1,0:T(8,128)(2,1)S(1)}, u32[]{:S(2)}, u32[]{:S(2)}) collective-permute-start(bf16[256,768]{1,0:T(8,128)(2,1)S(1)} %get-tuple-element.176.refs_0_), channel_id=1, source_target_pairs={{0,1},{1,0},{2,3},{3,2},{4,5},{5,4},{6,7},{7,6},{8,9},{9,8},{10,11... | collective-permute-start | bytes 1179656 | tf_op jit(solution)/shard_map/ppermute | solution.py:336
  62.7 8.1 %collective-permute-start.24 = (bf16[256,768]{1,0:T(8,128)(2,1)S(1)}, bf16[256,768]{1,0:T(8,128)(2,1)S(1)}, u32[]{:S(2)}, u32[]{:S(2)}) collective-permute-start(bf16[256,768]{1,0:T(8,128)(2,1)S(1)} %get-tuple-element.177.refs_1_), channel_id=1, source_target_pairs={{0,1},{1,0},{2,3},{3,2},{4,5},{5,4},{6,7},{7,6},{8,9},{9,8},{10,11... | collective-permute-start | bytes 1179656 | tf_op jit(solution)/shard_map/ppermute | solution.py:336
  65.7 15.5 %collective-permute-start.27 = (bf16[2,192,768]{2,1,0:T(8,128)(2,1)S(1)}, bf16[2,192,768]{2,1,0:T(8,128)(2,1)S(1)}, u32[]{:S(2)}, u32[]{:S(2)}) collective-permute-start(bf16[2,192,768]{2,1,0:T(8,128)(2,1)S(1)} %pair_z.3.pair), channel_id=1, source_target_pairs={{0,8},{8,0},{16,24},{24,16},{1,9},{9,1},{17,25},{25,17},{2,10},{10... | collective-permute-start | bytes 1769480 | tf_op jit(solution)/shard_map/ppermute | solution.py:336
  71.0 11.0 %collective-permute-start.25 = (bf16[4,64,768]{2,1,0:T(8,128)(2,1)S(1)}, bf16[4,64,768]{2,1,0:T(8,128)(2,1)S(1)}, u32[]{:S(2)}, u32[]{:S(2)}) collective-permute-start(bf16[4,64,768]{2,1,0:T(8,128)(2,1)S(1)} %slice.100), channel_id=1, source_target_pairs={{0,4},{4,0},{1,5},{5,1},{2,6},{6,2},{3,7},{7,3},{8,12},{12,8},{9,1... | collective-permute-start | bytes 1179656 | tf_op jit(solution)/shard_map/ppermute | solution.py:336
  71.5 10.7 %collective-permute-start.26 = (bf16[4,64,768]{2,1,0:T(8,128)(2,1)S(1)}, bf16[4,64,768]{2,1,0:T(8,128)(2,1)S(1)}, u32[]{:S(2)}, u32[]{:S(2)}) collective-permute-start(bf16[4,64,768]{2,1,0:T(8,128)(2,1)S(1)} %slice.101), channel_id=1, source_target_pairs={{0,2},{2,0},{1,3},{3,1},{4,6},{6,4},{5,7},{7,5},{8,10},{10,8},{9,1... | collective-permute-start | bytes 1179656 | tf_op jit(solution)/shard_map/ppermute | solution.py:336
  82.3 3.3 %collective-permute-start.34 = (bf16[4,64,768]{2,1,0:T(8,128)(2,1)S(1)}, bf16[4,64,768]{2,1,0:T(8,128)(2,1)S(1)}, u32[]{:S(2)}, u32[]{:S(2)}) collective-permute-start(bf16[4,64,768]{2,1,0:T(8,128)(2,1)S(1)} %collective-permute-done.26.refs_7_), channel_id=1, source_target_pairs={{0,1},{1,0},{2,3},{3,2},{4,5},{5,4},{6,7},{7,6},{8,9},{9,8},{10,11... | collective-permute-start | bytes 1179656 | tf_op jit(solution)/shard_map/ppermute | solution.py:336
  82.8 3.3 %collective-permute-start.32 = (bf16[4,128,768]{2,1,0:T(8,128)(2,1)S(1)}, bf16[4,128,768]{2,1,0:T(8,128)(2,1)S(1)}, u32[]{:S(2)}, u32[]{:S(2)}) collective-permute-start(bf16[4,128,768]{2,1,0:T(8,128)(2,1)S(1)} %collective-permute-done.22.refs_2_), channel_id=1, source_target_pairs={{0,1},{1,0},{2,3},{3,2},{4,5},{5,4},{6,7},{7,6},{8,9},{9,8},{10,11... | collective-permute-start | bytes 2359304 | tf_op jit(solution)/shard_map/ppermute | solution.py:336
  82.8 4.0 %collective-permute-start.30 = (bf16[4,128,768]{2,1,0:T(8,128)(2,1)S(1)}, bf16[4,128,768]{2,1,0:T(8,128)(2,1)S(1)}, u32[]{:S(2)}, u32[]{:S(2)}) collective-permute-start(bf16[4,128,768]{2,1,0:T(8,128)(2,1)S(1)} %order_z.1.refs_0_), channel_id=1, source_target_pairs={{0,1},{1,0},{2,3},{3,2},{4,5},{5,4},{6,7},{7,6},{8,9},{9,8},{10,11... | collective-permute-start | bytes 2359304 | tf_op jit(solution)/shard_map/ppermute | solution.py:336
  83.3 4.6 %collective-permute-start.31 = (bf16[4,128,768]{2,1,0:T(8,128)(2,1)S(1)}, bf16[4,128,768]{2,1,0:T(8,128)(2,1)S(1)}, u32[]{:S(2)}, u32[]{:S(2)}) collective-permute-start(bf16[4,128,768]{2,1,0:T(8,128)(2,1)S(1)} %collective-permute-done.21.refs_1_), channel_id=1, source_target_pairs={{0,1},{1,0},{2,3},{3,2},{4,5},{5,4},{6,7},{7,6},{8,9},{9,8},{10,11... | collective-permute-start | bytes 2359304 | tf_op jit(solution)/shard_map/ppermute | solution.py:336
  84.0 15.7 %collective-permute-start.28 = (bf16[4,96,768]{2,1,0:T(8,128)(2,1)S(1)}, bf16[4,96,768]{2,1,0:T(8,128)(2,1)S(1)}, u32[]{:S(2)}, u32[]{:S(2)}) collective-permute-start(bf16[4,96,768]{2,1,0:T(8,128)(2,1)S(1)} %get-tuple-element.195.refs_0_), channel_id=1, source_target_pairs={{0,4},{4,0},{1,5},{5,1},{2,6},{6,2},{3,7},{7,3},{8,12},{12,8},{9,1... | collective-permute-start | bytes 1769480 | tf_op jit(solution)/shard_map/ppermute | solution.py:336
  85.5 15.4 %collective-permute-start.29 = (bf16[4,96,768]{2,1,0:T(8,128)(2,1)S(1)}, bf16[4,96,768]{2,1,0:T(8,128)(2,1)S(1)}, u32[]{:S(2)}, u32[]{:S(2)}) collective-permute-start(bf16[4,96,768]{2,1,0:T(8,128)(2,1)S(1)} %get-tuple-element.196.refs_2_), channel_id=1, source_target_pairs={{0,2},{2,0},{1,3},{3,1},{4,6},{6,4},{5,7},{7,5},{8,10},{10,8},{9,1... | collective-permute-start | bytes 1769480 | tf_op jit(solution)/shard_map/ppermute | solution.py:336
  86.1 15.3 %collective-permute-start.35 = (bf16[4,96,768]{2,1,0:T(8,128)(2,1)S(1)}, bf16[4,96,768]{2,1,0:T(8,128)(2,1)S(1)}, u32[]{:S(2)}, u32[]{:S(2)}) collective-permute-start(bf16[4,96,768]{2,1,0:T(8,128)(2,1)S(1)} %get-tuple-element.195.refs_0_), channel_id=1, source_target_pairs={{0,1},{1,0},{2,3},{3,2},{4,5},{5,4},{6,7},{7,6},{8,9},{9,8},{10,11... | collective-permute-start | bytes 1769480 | tf_op jit(solution)/shard_map/ppermute | solution.py:336
  86.8 14.7 %collective-permute-start.37 = (bf16[4,96,768]{2,1,0:T(8,128)(2,1)S(1)}, bf16[4,96,768]{2,1,0:T(8,128)(2,1)S(1)}, u32[]{:S(2)}, u32[]{:S(2)}) collective-permute-start(bf16[4,96,768]{2,1,0:T(8,128)(2,1)S(1)} %get-tuple-element.196.refs_2_), channel_id=1, source_target_pairs={{0,1},{1,0},{2,3},{3,2},{4,5},{5,4},{6,7},{7,6},{8,9},{9,8},{10,11... | collective-permute-start | bytes 1769480 | tf_op jit(solution)/shard_map/ppermute | solution.py:336
  100.9 2.0 collective-permute-start.36
  100.9 2.8 %collective-permute-start.38 = (bf16[4,96,768]{2,1,0:T(8,128)(2,1)S(1)}, bf16[4,96,768]{2,1,0:T(8,128)(2,1)S(1)}, u32[]{:S(2)}, u32[]{:S(2)}) collective-permute-start(bf16[4,96,768]{2,1,0:T(8,128)(2,1)S(1)} %collective-permute-done.29.refs_3_), channel_id=1, source_target_pairs={{0,1},{1,0},{2,3},{3,2},{4,5},{5,4},{6,7},{7,6},{8,9},{9,8},{10,11... | collective-permute-start | bytes 1769480 | tf_op jit(solution)/shard_map/ppermute | solution.py:336
  121.9 5.2 %collective-permute-start.39 = (bf16[16,96,768]{2,1,0:T(8,128)(2,1)S(1)}, bf16[16,96,768]{2,1,0:T(8,128)(2,1)S(1)}, u32[]{:S(2)}, u32[]{:S(2)}) collective-permute-start(bf16[16,96,768]{2,1,0:T(8,128)(2,1)S(1)} %get-tuple-element.210), channel_id=1, source_target_pairs={{0,1},{1,0},{2,3},{3,2},{4,5},{5,4},{6,7},{7,6},{8,9},{9,8},{10,11... | collective-permute-start | bytes 7077896 | tf_op jit(solution)/shard_map/ppermute | solution.py:336
  127.9 16.1 %collective-permute-start.42 = (bf16[16,96,768]{2,1,0:T(8,128)(2,1)S(1)}, bf16[16,96,768]{2,1,0:T(8,128)(2,1)S(1)}, u32[]{:S(2)}, u32[]{:S(2)}) collective-permute-start(bf16[16,96,768]{2,1,0:T(8,128)(2,1)S(1)} %get-tuple-element.222), channel_id=1, source_target_pairs={{0,1},{1,0},{2,3},{3,2},{4,5},{5,4},{6,7},{7,6},{8,9},{9,8},{10,11... | collective-permute-start | bytes 7077896 | tf_op jit(solution)/shard_map/ppermute | solution.py:336
  128.4 15.7 %collective-permute-start.40 = (bf16[4,96,768]{2,1,0:T(8,128)(2,1)S(1)}, bf16[4,96,768]{2,1,0:T(8,128)(2,1)S(1)}, u32[]{:S(2)}, u32[]{:S(2)}) collective-permute-start(bf16[4,96,768]{2,1,0:T(8,128)(2,1)S(1)} %get-tuple-element.213), channel_id=1, source_target_pairs={{0,4},{4,0},{1,5},{5,1},{2,6},{6,2},{3,7},{7,3},{8,12},{12,8},{9,1... | collective-permute-start | bytes 1769480 | tf_op jit(solution)/shard_map/ppermute | solution.py:336
  129.0 15.1 %collective-permute-start.41 = (bf16[4,96,768]{2,1,0:T(8,128)(2,1)S(1)}, bf16[4,96,768]{2,1,0:T(8,128)(2,1)S(1)}, u32[]{:S(2)}, u32[]{:S(2)}) collective-permute-start(bf16[4,96,768]{2,1,0:T(8,128)(2,1)S(1)} %get-tuple-element.221), channel_id=1, source_target_pairs={{0,2},{2,0},{1,3},{3,1},{4,6},{6,4},{5,7},{7,5},{8,10},{10,8},{9,1... | collective-permute-start | bytes 1769480 | tf_op jit(solution)/shard_map/ppermute | solution.py:336
  140.7 3.4 %collective-permute-start.43 = (bf16[16,24,768]{2,1,0:T(8,128)(2,1)S(1)}, bf16[16,24,768]{2,1,0:T(8,128)(2,1)S(1)}, u32[]{:S(2)}, u32[]{:S(2)}) collective-permute-start(bf16[16,24,768]{2,1,0:T(8,128)(2,1)S(1)} %get-tuple-element.229), channel_id=1, source_target_pairs={{0,1},{1,0},{2,3},{3,2},{4,5},{5,4},{6,7},{7,6},{8,9},{9,8},{10,11... | collective-permute-start | bytes 1769480 | tf_op jit(solution)/shard_map/ppermute | solution.py:336
  144.8 13.8 %collective-permute-start.44 = (bf16[4,64,768]{2,1,0:T(8,128)(2,1)S(1)}, bf16[4,64,768]{2,1,0:T(8,128)(2,1)S(1)}, u32[]{:S(2)}, u32[]{:S(2)}) collective-permute-start(bf16[4,64,768]{2,1,0:T(8,128)(2,1)S(1)} %get-tuple-element.230), channel_id=1, source_target_pairs={{0,2},{2,0},{1,3},{3,1},{4,6},{6,4},{5,7},{7,5},{8,10},{10,8},{9,1... | collective-permute-start | bytes 1179656 | tf_op jit(solution)/shard_map/ppermute | solution.py:336
  146.1 12.5 %collective-permute-start.45 = (bf16[4,56,768]{2,1,0:T(8,128)(2,1)S(1)}, bf16[4,56,768]{2,1,0:T(8,128)(2,1)S(1)}, u32[]{:S(2)}, u32[]{:S(2)}) collective-permute-start(bf16[4,56,768]{2,1,0:T(8,128)(2,1)S(1)} %get-tuple-element.231), channel_id=1, source_target_pairs={{0,4},{4,0},{1,5},{5,1},{2,6},{6,2},{3,7},{7,3},{8,12},{12,8},{9,1... | collective-permute-start | bytes 1032200 | tf_op jit(solution)/shard_map/ppermute | solution.py:336
  148.3 19.8 %collective-permute-start.51 = (bf16[2,96,768]{2,1,0:T(8,128)(2,1)S(1)}, bf16[2,96,768]{2,1,0:T(8,128)(2,1)S(1)}, u32[]{:S(2)}, u32[]{:S(2)}) collective-permute-start(bf16[2,96,768]{2,1,0:T(8,128)(2,1)S(1)} %get-tuple-element.254), channel_id=1, source_target_pairs={{0,16},{8,24},{16,0},{24,8},{1,17},{9,25},{17,1},{25,9},{2,18},{10... | collective-permute-start | bytes 884744 | tf_op jit(solution)/shard_map/ppermute | solution.py:336
  151.7 16.5 %collective-permute-start.50 = (bf16[2,96,768]{2,1,0:T(8,128)(2,1)S(1)}, bf16[2,96,768]{2,1,0:T(8,128)(2,1)S(1)}, u32[]{:S(2)}, u32[]{:S(2)}) collective-permute-start(bf16[2,96,768]{2,1,0:T(8,128)(2,1)S(1)} %get-tuple-element.225), channel_id=1, source_target_pairs={{0,8},{8,0},{16,24},{24,16},{1,9},{9,1},{17,25},{25,17},{2,10},{10... | collective-permute-start | bytes 884744 | tf_op jit(solution)/shard_map/ppermute | solution.py:336
  158.7 10.0 %collective-permute-start.46 = (bf16[256,768]{1,0:T(8,128)(2,1)S(1)}, bf16[256,768]{1,0:T(8,128)(2,1)S(1)}, u32[]{:S(2)}, u32[]{:S(2)}) collective-permute-start(bf16[256,768]{1,0:T(8,128)(2,1)S(1)} %get-tuple-element.245), channel_id=1, source_target_pairs={{0,1},{1,0},{2,3},{3,2},{4,5},{5,4},{6,7},{7,6},{8,9},{9,8},{10,11... | collective-permute-start | bytes 1179656 | tf_op jit(solution)/shard_map/ppermute | solution.py:336
  159.7 21.6 %collective-permute-start.52 = (bf16[4,120,768]{2,1,0:T(8,128)(2,1)S(1)}, bf16[4,120,768]{2,1,0:T(8,128)(2,1)S(1)}, u32[]{:S(2)}, u32[]{:S(2)}) collective-permute-start(bf16[4,120,768]{2,1,0:T(8,128)(2,1)S(1)} %get-tuple-element.236), channel_id=1, source_target_pairs={{0,4},{4,0},{1,5},{5,1},{2,6},{6,2},{3,7},{7,3},{8,12},{12,8},{9,1... | collective-permute-start | bytes 2211848 | tf_op jit(solution)/shard_map/ppermute | solution.py:336
  160.3 21.0 %collective-permute-start.53 = (bf16[4,120,768]{2,1,0:T(8,128)(2,1)S(1)}, bf16[4,120,768]{2,1,0:T(8,128)(2,1)S(1)}, u32[]{:S(2)}, u32[]{:S(2)}) collective-permute-start(bf16[4,120,768]{2,1,0:T(8,128)(2,1)S(1)} %get-tuple-element.237), channel_id=1, source_target_pairs={{0,2},{2,0},{1,3},{3,1},{4,6},{6,4},{5,7},{7,5},{8,10},{10,8},{9,1... | collective-permute-start | bytes 2211848 | tf_op jit(solution)/shard_map/ppermute | solution.py:336
  168.2 3.4 %collective-permute-start.48 = (bf16[256,768]{1,0:T(8,128)(2,1)S(1)}, bf16[256,768]{1,0:T(8,128)(2,1)S(1)}, u32[]{:S(2)}, u32[]{:S(2)}) collective-permute-start(bf16[256,768]{1,0:T(8,128)(2,1)S(1)} %get-tuple-element.250), channel_id=1, source_target_pairs={{0,1},{1,0},{2,3},{3,2},{4,5},{5,4},{6,7},{7,6},{8,9},{9,8},{10,11... | collective-permute-start | bytes 1179656 | tf_op jit(solution)/shard_map/ppermute | solution.py:336
  168.7 3.0 %collective-permute-start.49 = (bf16[256,768]{1,0:T(8,128)(2,1)S(1)}, bf16[256,768]{1,0:T(8,128)(2,1)S(1)}, u32[]{:S(2)}, u32[]{:S(2)}) collective-permute-start(bf16[256,768]{1,0:T(8,128)(2,1)S(1)} %get-tuple-element.251), channel_id=1, source_target_pairs={{0,1},{1,0},{2,3},{3,2},{4,5},{5,4},{6,7},{7,6},{8,9},{9,8},{10,11... | collective-permute-start | bytes 1179656 | tf_op jit(solution)/shard_map/ppermute | solution.py:336
  169.9 7.2 %collective-permute-start.55 = (bf16[96,768]{1,0:T(8,128)(2,1)S(1)}, bf16[96,768]{1,0:T(8,128)(2,1)S(1)}, u32[]{:S(2)}, u32[]{:S(2)}) collective-permute-start(bf16[96,768]{1,0:T(8,128)(2,1)S(1)} %get-tuple-element.268), channel_id=1, source_target_pairs={{0,8},{8,0},{16,24},{24,16},{1,9},{9,1},{17,25},{25,17},{2,10},{10... | collective-permute-start | bytes 442376 | tf_op jit(solution)/shard_map/ppermute | solution.py:336
  171.6 9.7 %collective-permute-start.54 = (bf16[96,768]{1,0:T(8,128)(2,1)S(1)}, bf16[96,768]{1,0:T(8,128)(2,1)S(1)}, u32[]{:S(2)}, u32[]{:S(2)}) collective-permute-start(bf16[96,768]{1,0:T(8,128)(2,1)S(1)} %get-tuple-element.257), channel_id=1, source_target_pairs={{0,16},{8,24},{16,0},{24,8},{1,17},{9,25},{17,1},{25,9},{2,18},{10... | collective-permute-start | bytes 442376 | tf_op jit(solution)/shard_map/ppermute | solution.py:336
  181.3 4.0 %collective-permute-start.56 = (bf16[16,80,768]{2,1,0:T(8,128)(2,1)S(1)}, bf16[16,80,768]{2,1,0:T(8,128)(2,1)S(1)}, u32[]{:S(2)}, u32[]{:S(2)}) collective-permute-start(bf16[16,80,768]{2,1,0:T(8,128)(2,1)S(1)} %get-tuple-element.271), channel_id=1, source_target_pairs={{0,1},{1,0},{2,3},{3,2},{4,5},{5,4},{6,7},{7,6},{8,9},{9,8},{10,11... | collective-permute-start | bytes 5898248 | tf_op jit(solution)/shard_map/ppermute | solution.py:336
  186.0 8.4 %collective-permute-start.57 = (bf16[4,40,768]{2,1,0:T(8,128)(2,1)S(1)}, bf16[4,40,768]{2,1,0:T(8,128)(2,1)S(1)}, u32[]{:S(2)}, u32[]{:S(2)}) collective-permute-start(bf16[4,40,768]{2,1,0:T(8,128)(2,1)S(1)} %get-tuple-element.272), channel_id=1, source_target_pairs={{0,2},{2,0},{1,3},{3,1},{4,6},{6,4},{5,7},{7,5},{8,10},{10,8},{9,1... | collective-permute-start | bytes 737288 | tf_op jit(solution)/shard_map/ppermute | solution.py:336
  186.6 7.7 %collective-permute-start.58 = (bf16[4,40,768]{2,1,0:T(8,128)(2,1)S(1)}, bf16[4,40,768]{2,1,0:T(8,128)(2,1)S(1)}, u32[]{:S(2)}, u32[]{:S(2)}) collective-permute-start(bf16[4,40,768]{2,1,0:T(8,128)(2,1)S(1)} %get-tuple-element.273), channel_id=1, source_target_pairs={{0,4},{4,0},{1,5},{5,1},{2,6},{6,2},{3,7},{7,3},{8,12},{12,8},{9,1... | collective-permute-start | bytes 737288 | tf_op jit(solution)/shard_map/ppermute | solution.py:336
  189.3 15.4 %collective-permute-start.63 = (bf16[120,768]{1,0:T(8,128)(2,1)S(1)}, bf16[120,768]{1,0:T(8,128)(2,1)S(1)}, u32[]{:S(2)}, u32[]{:S(2)}) collective-permute-start(bf16[120,768]{1,0:T(8,128)(2,1)S(1)} %get-tuple-element.275), channel_id=1, source_target_pairs={{0,8},{8,0},{16,24},{24,16},{1,9},{9,1},{17,25},{25,17},{2,10},{10... | collective-permute-start | bytes 552968 | tf_op jit(solution)/shard_map/ppermute | solution.py:336
  189.6 16.2 %collective-permute-start.64 = (bf16[120,768]{1,0:T(8,128)(2,1)S(1)}, bf16[120,768]{1,0:T(8,128)(2,1)S(1)}, u32[]{:S(2)}, u32[]{:S(2)}) collective-permute-start(bf16[120,768]{1,0:T(8,128)(2,1)S(1)} %get-tuple-element.276), channel_id=1, source_target_pairs={{0,16},{8,24},{16,0},{24,8},{1,17},{9,25},{17,1},{25,9},{2,18},{10... | collective-permute-start | bytes 552968 | tf_op jit(solution)/shard_map/ppermute | solution.py:336
  189.9 15.9 %collective-permute-start.65 = (bf16[120,768]{1,0:T(8,128)(2,1)S(1)}, bf16[120,768]{1,0:T(8,128)(2,1)S(1)}, u32[]{:S(2)}, u32[]{:S(2)}) collective-permute-start(bf16[120,768]{1,0:T(8,128)(2,1)S(1)} %get-tuple-element.277), channel_id=1, source_target_pairs={{0,24},{8,16},{16,8},{24,0},{1,25},{9,17},{17,9},{25,1},{2,26},{10... | collective-permute-start | bytes 552968 | tf_op jit(solution)/shard_map/ppermute | solution.py:336
  195.2 16.4 %collective-permute-start.59 = (bf16[4,80,768]{2,1,0:T(8,128)(2,1)S(1)}, bf16[4,80,768]{2,1,0:T(8,128)(2,1)S(1)}, u32[]{:S(2)}, u32[]{:S(2)}) collective-permute-start(bf16[4,80,768]{2,1,0:T(8,128)(2,1)S(1)} %get-tuple-element.280), channel_id=1, source_target_pairs={{0,4},{4,0},{1,5},{5,1},{2,6},{6,2},{3,7},{7,3},{8,12},{12,8},{9,1... | collective-permute-start | bytes 1474568 | tf_op jit(solution)/shard_map/ppermute | solution.py:336
  196.7 14.9 %collective-permute-start.60 = (bf16[4,80,768]{2,1,0:T(8,128)(2,1)S(1)}, bf16[4,80,768]{2,1,0:T(8,128)(2,1)S(1)}, u32[]{:S(2)}, u32[]{:S(2)}) collective-permute-start(bf16[4,80,768]{2,1,0:T(8,128)(2,1)S(1)} %get-tuple-element.281), channel_id=1, source_target_pairs={{0,2},{2,0},{1,3},{3,1},{4,6},{6,4},{5,7},{7,5},{8,10},{10,8},{9,1... | collective-permute-start | bytes 1474568 | tf_op jit(solution)/shard_map/ppermute | solution.py:336
  205.8 4.4 %collective-permute-start.61 = (bf16[48,768]{1,0:T(8,128)(2,1)S(1)}, bf16[48,768]{1,0:T(8,128)(2,1)S(1)}, u32[]{:S(2)}, u32[]{:S(2)}) collective-permute-start(bf16[48,768]{1,0:T(8,128)(2,1)S(1)} %get-tuple-element.286), channel_id=1, source_target_pairs={{0,2},{2,0},{1,3},{3,1},{4,6},{6,4},{5,7},{7,5},{8,10},{10,8},{9,1... | collective-permute-start | bytes 221192 | tf_op jit(solution)/shard_map/ppermute | solution.py:336
  207.2 4.4 %collective-permute-start.62 = (bf16[48,768]{1,0:T(8,128)(2,1)S(1)}, bf16[48,768]{1,0:T(8,128)(2,1)S(1)}, u32[]{:S(2)}, u32[]{:S(2)}) collective-permute-start(bf16[48,768]{1,0:T(8,128)(2,1)S(1)} %get-tuple-element.288), channel_id=1, source_target_pairs={{0,4},{4,0},{1,5},{5,1},{2,6},{6,2},{3,7},{7,3},{8,12},{12,8},{9,1... | collective-permute-start | bytes 221192 | tf_op jit(solution)/shard_map/ppermute | solution.py:336
  212.5 8.7 %collective-permute-start.66 = (bf16[80,768]{1,0:T(8,128)(2,1)S(1)}, bf16[80,768]{1,0:T(8,128)(2,1)S(1)}, u32[]{:S(2)}, u32[]{:S(2)}) collective-permute-start(bf16[80,768]{1,0:T(8,128)(2,1)S(1)} %get-tuple-element.296), channel_id=1, source_target_pairs={{0,8},{8,0},{16,24},{24,16},{1,9},{9,1},{17,25},{25,17},{2,10},{10... | collective-permute-start | bytes 368648 | tf_op jit(solution)/shard_map/ppermute | solution.py:336
  215.8 9.6 %collective-permute-start.67 = (bf16[80,768]{1,0:T(8,128)(2,1)S(1)}, bf16[80,768]{1,0:T(8,128)(2,1)S(1)}, u32[]{:S(2)}, u32[]{:S(2)}) collective-permute-start(bf16[80,768]{1,0:T(8,128)(2,1)S(1)} %get-tuple-element.297), channel_id=1, source_target_pairs={{0,16},{8,24},{16,0},{24,8},{1,17},{9,25},{17,1},{25,9},{2,18},{10... | collective-permute-start | bytes 368648 | tf_op jit(solution)/shard_map/ppermute | solution.py:336
  215.8 9.6 %collective-permute-start.68 = (bf16[80,768]{1,0:T(8,128)(2,1)S(1)}, bf16[80,768]{1,0:T(8,128)(2,1)S(1)}, u32[]{:S(2)}, u32[]{:S(2)}) collective-permute-start(bf16[80,768]{1,0:T(8,128)(2,1)S(1)} %get-tuple-element.298), channel_id=1, source_target_pairs={{0,24},{8,16},{16,8},{24,0},{1,25},{9,17},{17,9},{25,1},{2,26},{10... | collective-permute-start | bytes 368648 | tf_op jit(solution)/shard_map/ppermute | solution.py:336
  (66 other events, 533.8 us)

commit v2 on v1

--- a/solution.py
+++ b/solution.py
@@ -374,7 +374,7 @@
 
 
 class Weights:
-    def __init__(self, pieces, plan, shapes):
+    def __init__(self, pieces, plan, shapes, free=()):
         arrays = []
         self.spans = []
         for number, first, array, row, rows in pieces:
@@ -382,9 +382,13 @@
             if place == len(arrays):
                 arrays.append(array)
             self.spans.append((number, first, place, row, rows))
-        self.operands = [pltpu.with_memory_space_constraint(array, pltpu.HBM) for array in arrays]
+        loose = [any(array is other for other in free) for array in arrays]
+        self.operands = [
+            array if found else pltpu.with_memory_space_constraint(array, pltpu.HBM)
+            for array, found in zip(arrays, loose)
+        ]
         self.plan, self.shapes = plan, shapes
-        self.specs = [pl.BlockSpec(memory_space=pltpu.HBM)] * len(arrays)
+        self.specs = [ANY if found else pl.BlockSpec(memory_space=pltpu.HBM) for found in loose]
         self.scratch = [pltpu.VMEM((4, 2, 2, 2, rows, columns), bf16) for rows, columns in shapes]
         self.scratch.append(pltpu.SemaphoreType.DMA((8 * len(plan),)))
 
@@ -758,7 +762,7 @@
         ],
         [WHOLE] * 5,
         weights.scratch + [pltpu.VMEM((rows, width), bf16)],
-        28,
+        16,
         24,
     )
 
@@ -852,7 +856,7 @@
         ],
         [WHOLE] * 6,
         weights.scratch + [pltpu.VMEM((width, width), f32), pltpu.VMEM((rows, width), bf16)],
-        30,
+        16,
         36,
     )
 
@@ -925,7 +929,7 @@
         [WHOLE] * 5,
         weights.scratch
         + [pltpu.VMEM((max(rows, width), width), f32), pltpu.VMEM((rows, width), bf16), pltpu.VMEM((8, width), f32)],
-        26,
+        16,
         18,
     )
 
@@ -959,7 +963,7 @@
         [shaped(halves, bf16), shaped(halves, bf16)],
         [WHOLE] * 2,
         [pltpu.VMEM((width, width), f32), pltpu.VMEM((width, rows), bf16)],
-        24,
+        14,
         20,
     )
 
@@ -1006,7 +1010,7 @@
         [shaped(halves, bf16)] * 2 + [shaped((rows, width), bf16)] * 3,
         [WHOLE] * 5,
         [pltpu.VMEM((width, width), f32), pltpu.VMEM((32, 8, width), f32)],
-        28,
+        14,
         12,
     )
 
@@ -1417,7 +1421,8 @@
     near_b = pp(pair_b, "z", 1)
     plan = [(i * own, own, i, 0, 0) for i in range(3)]
     plan = divide(plan, cut_a)
-    weights = Weights(pieces, plan + [(3 * own, 8, 3, 0, 0)], [square] * 3 + [(8, width)])
+    loose = [piece[2] for piece in pieces]
+    weights = Weights(pieces, plan + [(3 * own, 8, 3, 0, 0)], [square] * 3 + [(8, width)], loose)
     weights_again = Weights(pieces, plan, [square] * 3)
     own_b = order_z(ids, pair_b, after(near_b, low_a, high_a))
     far_c = pp(after(group_c, own_b), "z", 2)
@@ -1442,7 +1447,10 @@
     plan = [(0, own, 0, 0, 0)] + [((i + 1) * own, own, 1, 0, i * width) for i in range(blocks)]
     plan = divide(plan, cut_b)
     weights = Weights(
-        pieces, plan + [((blocks + 1) * own, 8, 2, 0, 0)], [square, (own, wide), (8, width)]
+        pieces,
+        plan + [((blocks + 1) * own, 8, 2, 0, 0)],
+        [square, (own, wide), (8, width)],
+        [piece[2] for piece in pieces],
     )
     back_weights = Weights(pieces, plan, [square, (own, wide)])
     by_x, by_y = order_halves(ids, pair_c, after(near_c, low_b, high_b))
@@ -1461,7 +1469,7 @@
         for array, numbers, first in zip(held, ((0, 1), (2, 3), (0, 2), (1, 3)), (0, 0, half_c, half_c)):
             pieces += [(4 * core + number, first, array, i * half_c, half_c) for i, number in enumerate(numbers)]
     plan = divide([(0, down_rows, 0, 0, 0)], half_c)
-    weights = Weights(pieces, plan, [(down_rows, width)])
+    weights = Weights(pieces, plan, [(down_rows, width)], [piece[2] for piece in pieces])
     layer_out, g_second, g_inner, down_own, down_send, sums = feed_down(
         ids, weights, activated, slope, scaled, keep_feed, cotangent.reshape(rows, width), vectors, tokens
     )

time: 228 us -> 224 us (0.982)
  local copies, waits for them, and re-layouts: 17.2 us -> 11.3 us
  waiting for transfers between devices: 55.3 us -> 58.8 us
  Pallas kernels: 94.5 us -> 92.2 us
    unnamed x122 -> x54, local copies, waits for them, and re-layouts: 6.07 us -> 0.11 us
    ppermute x69, waiting for transfers between devices: 55.3 us -> 58.8 us  [pp(): return lax.ppermute(value, axis, [(i, i ^ step) for i in range(size)])]
    pallas_call x27, Pallas kernels: 94.5 us -> 92.2 us  [call(): pl.pallas_call(body, grid_spec=pltpu.PrefetchScalarGridSpec(num_scalar_pr...]
  transfers between devices with their start and end apart: 69 -> 69, of which waited for: 28 -> 29; matrix products, arithmetic and copies ran while one was open for 4% -> 4% of each run, Pallas kernels for 33% -> 33%
where the time goes in v2:
time: 224 us; the launch traced here: 223 us
  Pallas kernels  92.2 us (41%)
  waiting for transfers between devices  58.8 us (26%)
  starting transfers between devices  57.1 us (25%)
  local copies, waits for them, and re-layouts  11.3 us (5%)
  other arithmetic  2.42 us (1%)
    pallas_call x27, Pallas kernels, call(): pl.pallas_call(body, grid_spec=pltpu.PrefetchScalarGridSpec(num_scalar_pr...  92.2 us
    ppermute x69, waiting for transfers between devices, pp(): return lax.ppermute(value, axis, [(i, i ^ step) for i in range(size)])  58.8 us
    ppermute x69, starting transfers between devices, pp(): return lax.ppermute(value, axis, [(i, i ^ step) for i in range(size)])  57.1 us
    pad x8, local copies, waits for them, and re-layouts, local(): jnp.pad(part.reshape(1, -1), ((0, 0), (0, width - part.shape[0])))  5.29 us
  transfers between devices with their start and end apart: 69, of which 29 were waited for; matrix products, arithmetic and copies ran while one was open for 4% of the time, Pallas kernels for 33%

profile of v2, /device:TPU:0, one launch (start us, length us, event | category | flops | bytes accessed | tf_op | source)
XLA Modules:
  0.0 223.2 jit_solution(11382270094706483095)
XLA Ops:
  0.7 0.9 fusion.4
  2.3 5.1 %collective-permute-start.4 = (bf16[80,768]{1,0:T(8,128)(2,1)S(1)}, bf16[80,768]{1,0:T(8,128)(2,1)S(1)}, u32[]{:S(2)}, u32[]{:S(2)}) collective-permute-start(bf16[80,768]{1,0:T(8,128)(2,1)S(1)} %concatenate.19.refs_0_), channel_id=1, source_target_pairs={{0,24},{8,16},{16,8},{24,0},{1,25},{9,17},{17,9},{25,1},{2,26},{10... | collective-permute-start | bytes 368648 | tf_op jit(solution)/shard_map/ppermute | solution.py:336
  8.1 0.9 fusion.3
  9.0 1.7 collective-permute-start
  10.7 1.5 collective-permute-start.1
  20.0 1.5 collective-permute-start.5
  21.5 1.0 collective-permute-start.7
  22.5 3.1 %prepare.1 = (bf16[512,768]{1,0:T(8,128)(2,1)S(1)}, bf16[512,768]{1,0:T(8,128)(2,1)S(1)}, bf16[512,768]{1,0:T(8,128)(2,1)S(1)}) custom-call(s32[4]{0:T(128)S(1)} %pad_add_fusion.ids, bf16[512,768]{1,0:T(8,128)(2,1)S(1)} %bitcast.78, s32[2,1,192,256]{3,2,1,0:T(8,128)S(1)} %bitcast.93, s32[2,1,192,256]{3,2,1,0:T(8,128)S(1)} %bitcast.94), custom_call_target="tpu_custom_call" | custom-call | flops 1024 | bytes 393216 | tf_op jit(solution)/shard_map/prepare/pallas_call | solution.py:459
  25.6 6.0 %collective-permute-done.7.two = bf16[128,768]{1,0:T(8,128)(2,1)S(1)} collective-permute-done((bf16[128,768]{1,0:T(8,128)(2,1)S(1)}, bf16[128,768]{1,0:T(8,128)(2,1)S(1)}, u32[]{:S(2)}, u32[]{:S(2)}) %collective-permute-start.7) | collective-permute-done | bytes 196640 | tf_op jit(solution)/shard_map/ppermute | solution.py:336
  33.4 1.5 collective-permute-start.15
  35.7 3.8 %collective-permute-done.8.refs_3_ = bf16[4,40,768]{2,1,0:T(8,128)(2,1)S(1)} collective-permute-done((bf16[4,40,768]{2,1,0:T(8,128)(2,1)S(1)}, bf16[4,40,768]{2,1,0:T(8,128)(2,1)S(1)}, u32[]{:S(2)}, u32[]{:S(2)}) %collective-permute-start.8) | collective-permute-done | bytes 245792 | tf_op jit(solution)/shard_map/ppermute | solution.py:336
  39.5 3.8 %collective-permute-done.9.refs_4_ = bf16[4,40,768]{2,1,0:T(8,128)(2,1)S(1)} collective-permute-done((bf16[4,40,768]{2,1,0:T(8,128)(2,1)S(1)}, bf16[4,40,768]{2,1,0:T(8,128)(2,1)S(1)}, u32[]{:S(2)}, u32[]{:S(2)}) %collective-permute-start.9) | collective-permute-done | bytes 245792 | tf_op jit(solution)/shard_map/ppermute | solution.py:336
  43.4 1.7 collective-permute-done.15.received
  45.6 2.4 %collective-permute-start.20 = (bf16[192,768]{1,0:T(8,128)(2,1)S(1)}, bf16[192,768]{1,0:T(8,128)(2,1)S(1)}, u32[]{:S(2)}, u32[]{:S(2)}) collective-permute-start(bf16[192,768]{1,0:T(8,128)(2,1)S(1)} %pad_maximum_fusion.one), channel_id=1, source_target_pairs={{0,16},{8,24},{16,0},{24,8},{1,17},{9,25},{17,1},{25,9},{2,18},{10... | collective-permute-start | bytes 884744 | tf_op jit(solution)/shard_map/ppermute | solution.py:336
  48.6 1.1 collective-permute-start.21
  49.7 4.6 %project.1 = (bf16[2,256,768]{2,1,0:T(8,128)(2,1)S(1)}, bf16[128,768]{1,0:T(8,128)(2,1)S(1)}, bf16[128,768]{1,0:T(8,128)(2,1)S(1)}, bf16[128,768]{1,0:T(8,128)(2...) custom-call(s32[4]{0:T(128)S(1)} %pad_add_fusion.ids, ...), custom_call_target="tpu_custom_call" | custom-call | flops 1024 | bytes 655360 | tf_op jit(solution)/shard_map/project/pallas_call | solution.py:459
  55.0 6.6 %collective-permute-done.20.two = bf16[192,768]{1,0:T(8,128)(2,1)S(1)} collective-permute-done((bf16[192,768]{1,0:T(8,128)(2,1)S(1)}, bf16[192,768]{1,0:T(8,128)(2,1)S(1)}, u32[]{:S(2)}, u32[]{:S(2)}) %collective-permute-start.20) | collective-permute-done | bytes 294944 | tf_op jit(solution)/shard_map/ppermute | solution.py:336
  63.1 1.3 collective-permute-done.19.refs_7_
  65.5 4.6 %attention.2 = (bf16[2,256,768]{2,1,0:T(8,128)(2,1)S(1)}, bf16[2,6,4,512,128]{4,3,2,1,0:T(8,128)(2,1)S(1)}) custom-call(s32[4]{0:T(128)S(1)} %pad_add_fusion.ids, bf16[2,256,768]{2,1,0:T(8,128)(2,1)S(1)} %get-tuple-element.179.q, bf16[128,768]{1,0:T(8,128)(2,1)S(1)} %get-tuple-element.170.refs_0_, bf16[128,768]{1,0:T(8,128)(2,1)S(1)} %get-tuple-element.171.refs_1_, ...), custom_call_target="tpu_custom_call" | custom-call | flops 1024 | bytes 917504 | tf_op jit(solution)/shard_map/attention/pallas_call | solution.py:459
  70.2 1.0 collective-permute-start.25
  71.2 1.4 collective-permute-start.26
  72.6 4.5 %attention.3 = (bf16[2,256,768]{2,1,0:T(8,128)(2,1)S(1)}, bf16[2,6,4,512,128]{4,3,2,1,0:T(8,128)(2,1)S(1)}) custom-call(s32[4]{0:T(128)S(1)} %pad_add_fusion.ids, bf16[2,256,768]{2,1,0:T(8,128)(2,1)S(1)} %get-tuple-element.179.q, bf16[256,768]{1,0:T(8,128)(2,1)S(1)} %get-tuple-element.176.refs_0_, ...), custom_call_target="tpu_custom_call", output_to_operand_aliasing={{0}: (7, {}), {1}: (8, {})} | custom-call | flops 1024 | bytes 917504 | tf_op jit(solution)/shard_map/attention/pallas_call | solution.py:459
  77.2 3.3 %collective-permute-done.27.received = bf16[2,192,768]{2,1,0:T(8,128)(2,1)S(1)} collective-permute-done((bf16[2,192,768]{2,1,0:T(8,128)(2,1)S(1)}, bf16[2,192,768]{2,1,0:T(8,128)(2,1)S(1)}, u32[]{:S(2)}, u32[]{:S(2)}) %collective-permute-start.27) | collective-permute-done | bytes 589856 | tf_op jit(solution)/shard_map/ppermute | solution.py:336
  81.3 0.9 collective-permute-done.26.refs_7_
  83.9 0.9 collective-permute-start.28
  84.7 1.1 collective-permute-start.29
  86.8 1.0 collective-permute-done.31.refs_4_
  87.8 10.1 %feed_up.1 = (f32[8,3072]{1,0:T(8,128)S(1)}, f32[512,768]{1,0:T(8,128)S(1)}, f32[512,128]{1,0:T(8,128)S(1)}, bf16[512,3072]{1,0:T(8,128)(2,1)S(1)}, bf16[512,3072]{1,0:T(8,128)(2,1)S(1)}) custom-call(s32[4]{0:T(128)S(1)} %pad_add_fusion.ids, bf16[4,128,768]{2,1,0:T(8,128)(2,1)S(1)} %order_z.1.refs_0_, ...), custom_call_target="tpu_custom_call" | custom-call | flops 1024 | bytes 1572864 | tf_op jit(solution)/shard_map/feed_up/pallas_call | solution.py:459
  98.0 1.7 collective-permute-done.28.refs_1_
  100.7 1.5 collective-permute-done.36.refs_5_
  103.1 14.4 %feed_down.1 = (bf16[512,768]{1,0:T(8,128)(2,1)}, f32[512,768]{1,0:T(8,128)S(1)}, bf16[512,3072]{1,0:T(8,128)(2,1)S(1)}, bf16[16,96,768]{2,1,0:T(8,128)(2,1)S(1)...) custom-call(s32[4]{0:T(128)S(1)} %pad_add_fusion.ids, bf16[4,96,768]{2,1,0:T(8,128)(2,1)S(1)} %get-tuple-element.195.refs_0_, ...), custom_call_target="tpu_custom_call" | custom-call | flops 1024 | bytes 2359296 | tf_op jit(solution)/shard_map/feed_down/pallas_call | solution.py:459
  117.7 5.1 %up_grads.1 = (bf16[16,96,768]{2,1,0:T(8,128)(2,1)S(1)}, bf16[16,96,768]{2,1,0:T(8,128)(2,1)S(1)}) custom-call(s32[4]{0:T(128)S(1)} %pad_add_fusion.ids, bf16[512,3072]{1,0:T(8,128)(2,1)S(1)} %get-tuple-element.214.g_inner.refs_10_, f32[512,768]{1,0:T(8,128)S(1)} %get-tuple-element.204.refs_10_.scaled.refs_12_, ...), custom_call_target="tpu_custom_call" | custom-call | flops 1024 | bytes 1310720 | tf_op jit(solution)/shard_map/up_grads/pallas_call | solution.py:459
  124.1 1.2 collective-permute-start.40
  125.2 1.4 collective-permute-start.41
  126.7 10.5 %middle.1 = (f32[512,768]{1,0:T(8,128)S(1)}, bf16[512,768]{1,0:T(8,128)(2,1)S(1)}, bf16[16,24,768]{2,1,0:T(8,128)(2,1)S(1)}, bf16[16,24,768]{2,1,0:T(8,128)(2,1)S(1)}, f32[32,8,768]{2,1,0:T(8,128)S(1)}) custom-call(s32[4]{0:T(128)S(1)} %pad_add_fusion.ids, bf16[4,128,768]{2,1,0:T(8,128)(2,1)} %copy-done.2, bf16[4,128,768]{2,1,0:T(8,128)(2,1)} %copy-done.4, ...), custom_call_target="tpu_custom_call" | custom-call | flops 1024 | bytes 1179648 | tf_op jit(solution)/shard_map/middle/pallas_call | solution.py:459
  137.2 3.1 %collective-permute-done.41.refs_7_ = bf16[4,96,768]{2,1,0:T(8,128)(2,1)S(1)} collective-permute-done((bf16[4,96,768]{2,1,0:T(8,128)(2,1)S(1)}, bf16[4,96,768]{2,1,0:T(8,128)(2,1)S(1)}, u32[]{:S(2)}, u32[]{:S(2)}) %collective-permute-start.41) | collective-permute-done | bytes 589856 | tf_op jit(solution)/shard_map/ppermute | solution.py:336
  141.1 1.5 collective-permute-start.44
  143.1 1.3 reduce_second.1
  144.4 2.8 %collective-permute-start.51 = (bf16[2,96,768]{2,1,0:T(8,128)(2,1)S(1)}, bf16[2,96,768]{2,1,0:T(8,128)(2,1)S(1)}, u32[]{:S(2)}, u32[]{:S(2)}) collective-permute-start(bf16[2,96,768]{2,1,0:T(8,128)(2,1)S(1)} %get-tuple-element.254), channel_id=1, source_target_pairs={{0,16},{8,24},{16,0},{24,8},{1,17},{9,25},{17,1},{25,9},{2,18},{10... | collective-permute-start | bytes 884744 | tf_op jit(solution)/shard_map/ppermute | solution.py:336
  147.6 6.6 %attention_back.2 = (bf16[256,768]{1,0:T(8,128)(2,1)S(1)}, f32[256,768]{1,0:T(8,128)S(1)}, f32[256,768]{1,0:T(8,128)S(1)}, bf16[256,768]{1,0:T(8,128)(2,1)S(1)}, bf16[256,768]{1,0:T(8,128)(2,1)S(1)}) custom-call(s32[4]{0:T(128)S(1)} %pad_add_fusion.ids, bf16[2,256,768]{2,1,0:T(8,128)(2,1)S(1)} %get-tuple-element.179.q, ...), custom_call_target="tpu_custom_call" | custom-call | flops 1024 | bytes 1310720 | tf_op jit(solution)/shard_map/attention_back/pallas_call | solution.py:459
  154.3 1.0 reduce_sides.2
  155.2 1.3 collective-permute-start.52
  157.3 6.3 %attention_back.3 = (bf16[256,768]{1,0:T(8,128)(2,1)S(1)}, f32[256,768]{1,0:T(8,128)S(1)}, f32[256,768]{1,0:T(8,128)S(1)}, bf16[256,768]{1,0:T(8,128)(2,1)S(1)}, bf16[256,768]{1,0:T(8,128)(2,1)S(1)}) custom-call(s32[4]{0:T(128)S(1)} %pad_add_fusion.ids, bf16[2,256,768]{2,1,0:T(8,128)(2,1)S(1)} %get-tuple-element.179.q, ...), custom_call_target="tpu_custom_call" | custom-call | flops 1024 | bytes 1310720 | tf_op jit(solution)/shard_map/attention_back/pallas_call | solution.py:459
  165.4 1.7 collective-permute-start.55
  167.6 4.3 %input_grads.1 = (bf16[16,80,768]{2,1,0:T(8,128)(2,1)S(1)}, bf16[16,80,768]{2,1,0:T(8,128)(2,1)S(1)}, bf16[512,768]{1,0:T(8,128)(2,1)S(1)}, bf16[512,768]{1,0:T(8,128)(2,1)S(1)}, bf16[512,768]{1,0:T(8,128)(2,1)S(1)}) custom-call(s32[4]{0:T(128)S(1)} %pad_add_fusion.ids, bf16[512,768]{1,0:T(8,128)(2,1)S(1)} %bitcast.81, ...), custom_call_target="tpu_custom_call" | custom-call | flops 1024 | bytes 786432 | tf_op jit(solution)/shard_map/input_grads/pallas_call | solution.py:459
  171.9 1.2 collective-permute-done.55.from_next
  173.1 3.7 %collective-permute-done.54.from_far = bf16[96,768]{1,0:T(8,128)(2,1)S(1)} collective-permute-done((bf16[96,768]{1,0:T(8,128)(2,1)S(1)}, bf16[96,768]{1,0:T(8,128)(2,1)S(1)}, u32[]{:S(2)}, u32[]{:S(2)}) %collective-permute-start.54) | collective-permute-done | bytes 147488 | tf_op jit(solution)/shard_map/ppermute | solution.py:336
  176.9 4.0 %collective-permute-done.56 = bf16[16,80,768]{2,1,0:T(8,128)(2,1)S(1)} collective-permute-done((bf16[16,80,768]{2,1,0:T(8,128)(2,1)S(1)}, bf16[16,80,768]{2,1,0:T(8,128)(2,1)S(1)}, u32[]{:S(2)}, u32[]{:S(2)}) %collective-permute-start.56) | collective-permute-done | bytes 1966112 | tf_op jit(solution)/shard_map/ppermute | solution.py:336
  181.5 1.3 collective-permute-start.57
  183.6 1.2 reduce_depth.2
  185.1 1.6 collective-permute-start.64
  186.7 2.5 %collective-permute-start.65 = (bf16[120,768]{1,0:T(8,128)(2,1)S(1)}, bf16[120,768]{1,0:T(8,128)(2,1)S(1)}, u32[]{:S(2)}, u32[]{:S(2)}) collective-permute-start(bf16[120,768]{1,0:T(8,128)(2,1)S(1)} %get-tuple-element.277), channel_id=1, source_target_pairs={{0,24},{8,16},{16,8},{24,0},{1,25},{9,17},{17,9},{25,1},{2,26},{10... | collective-permute-start | bytes 552968 | tf_op jit(solution)/shard_map/ppermute | solution.py:336
  191.4 0.9 collective-permute-start.59
  192.2 1.4 collective-permute-start.60
  193.7 6.5 %input_back.1 = bf16[512,768]{1,0:T(8,128)(2,1)} custom-call(s32[4]{0:T(128)S(1)} %pad_add_fusion.ids, bf16[4,80,768]{2,1,0:T(8,128)(2,1)} %copy-done.5, bf16[4,80,768]{2,1,0:T(8,128)(2,1)} %copy-done.10, bf16[4,80,768]{2,1,0:T(8,128)(2,1)} %copy-done.9, bf16[4,40,768]{2,1,0:T(8,128)(2,1)} %copy-done.18, bf16[4,40,768]{2,1,0:T(8,128)(2,1)} %copy-done.19, ...), custom_call_target="tpu_custom_call" | custom-call | flops 1024 | bytes 655360 | tf_op jit(solution)/shard_map/input_back/pallas_call | solution.py:459
  200.2 1.2 collective-permute-done.64
  201.3 1.3 collective-permute-start.61
  204.7 1.0 collective-permute-done.61
  205.7 1.3 collective-permute-done.62
  207.0 0.9 reduce_depth.3
  208.0 3.3 %collective-permute-start.66 = (bf16[80,768]{1,0:T(8,128)(2,1)S(1)}, bf16[80,768]{1,0:T(8,128)(2,1)S(1)}, u32[]{:S(2)}, u32[]{:S(2)}) collective-permute-start(bf16[80,768]{1,0:T(8,128)(2,1)S(1)} %get-tuple-element.296), channel_id=1, source_target_pairs={{0,8},{8,0},{16,24},{24,16},{1,9},{9,1},{17,25},{25,17},{2,10},{10... | collective-permute-start | bytes 368648 | tf_op jit(solution)/shard_map/ppermute | solution.py:336
  211.2 2.4 %collective-permute-start.68 = (bf16[80,768]{1,0:T(8,128)(2,1)S(1)}, bf16[80,768]{1,0:T(8,128)(2,1)S(1)}, u32[]{:S(2)}, u32[]{:S(2)}) collective-permute-start(bf16[80,768]{1,0:T(8,128)(2,1)S(1)} %get-tuple-element.298), channel_id=1, source_target_pairs={{0,24},{8,16},{16,8},{24,0},{1,25},{9,17},{17,9},{25,1},{2,26},{10... | collective-permute-start | bytes 368648 | tf_op jit(solution)/shard_map/ppermute | solution.py:336
  214.4 2.2 collective-permute-done.66
  216.6 4.2 %collective-permute-done.67 = bf16[80,768]{1,0:T(8,128)(2,1)S(1)} collective-permute-done((bf16[80,768]{1,0:T(8,128)(2,1)S(1)}, bf16[80,768]{1,0:T(8,128)(2,1)S(1)}, u32[]{:S(2)}, u32[]{:S(2)}) %collective-permute-start.67) | collective-permute-done | bytes 122912 | tf_op jit(solution)/shard_map/ppermute | solution.py:336
  (186 shorter events, 36.8 us)
Async XLA Ops:
  2.3 16.3 %collective-permute-start.4 = (bf16[80,768]{1,0:T(8,128)(2,1)S(1)}, bf16[80,768]{1,0:T(8,128)(2,1)S(1)}, u32[]{:S(2)}, u32[]{:S(2)}) collective-permute-start(bf16[80,768]{1,0:T(8,128)(2,1)S(1)} %concatenate.19.refs_0_), channel_id=1, source_target_pairs={{0,24},{8,16},{16,8},{24,0},{1,25},{9,17},{17,9},{25,1},{2,26},{10... | collective-permute-start | bytes 368648 | tf_op jit(solution)/shard_map/ppermute | solution.py:336
  7.4 11.2 %collective-permute-start.3 = (bf16[80,768]{1,0:T(8,128)(2,1)S(1)}, bf16[80,768]{1,0:T(8,128)(2,1)S(1)}, u32[]{:S(2)}, u32[]{:S(2)}) collective-permute-start(bf16[80,768]{1,0:T(8,128)(2,1)S(1)} %concatenate.19.refs_0_), channel_id=1, source_target_pairs={{0,16},{8,24},{16,0},{24,8},{1,17},{9,25},{17,1},{25,9},{2,18},{10... | collective-permute-start | bytes 368648 | tf_op jit(solution)/shard_map/ppermute | solution.py:336
  7.4 11.2 %collective-permute-start.2 = (bf16[80,768]{1,0:T(8,128)(2,1)S(1)}, bf16[80,768]{1,0:T(8,128)(2,1)S(1)}, u32[]{:S(2)}, u32[]{:S(2)}) collective-permute-start(bf16[80,768]{1,0:T(8,128)(2,1)S(1)} %concatenate.19.refs_0_), channel_id=1, source_target_pairs={{0,8},{8,0},{16,24},{24,16},{1,9},{9,1},{17,25},{25,17},{2,10},{10... | collective-permute-start | bytes 368648 | tf_op jit(solution)/shard_map/ppermute | solution.py:336
  9.0 9.6 %collective-permute-start = (bf16[48,768]{1,0:T(8,128)(2,1)S(1)}, bf16[48,768]{1,0:T(8,128)(2,1)S(1)}, u32[]{:S(2)}, u32[]{:S(2)}) collective-permute-start(bf16[48,768]{1,0:T(8,128)(2,1)S(1)} %get-tuple-element.334), channel_id=1, source_target_pairs={{0,2},{2,0},{1,3},{3,1},{4,6},{6,4},{5,7},{7,5},{8,10},{10,8},{9,1... | collective-permute-start | bytes 221192 | tf_op jit(solution)/shard_map/ppermute | solution.py:336
  10.7 7.9 %collective-permute-start.1 = (bf16[48,768]{1,0:T(8,128)(2,1)S(1)}, bf16[48,768]{1,0:T(8,128)(2,1)S(1)}, u32[]{:S(2)}, u32[]{:S(2)}) collective-permute-start(bf16[48,768]{1,0:T(8,128)(2,1)S(1)} %get-tuple-element.335), channel_id=1, source_target_pairs={{0,4},{4,0},{1,5},{5,1},{2,6},{6,2},{3,7},{7,3},{8,12},{12,8},{9,1... | collective-permute-start | bytes 221192 | tf_op jit(solution)/shard_map/ppermute | solution.py:336
  19.2 12.4 %collective-permute-start.6 = (bf16[4,80,768]{2,1,0:T(8,128)(2,1)S(1)}, bf16[4,80,768]{2,1,0:T(8,128)(2,1)S(1)}, u32[]{:S(2)}, u32[]{:S(2)}) collective-permute-start(bf16[4,80,768]{2,1,0:T(8,128)(2,1)S(1)} %order_four.1.refs_0_), channel_id=1, source_target_pairs={{0,4},{4,0},{1,5},{5,1},{2,6},{6,2},{3,7},{7,3},{8,12},{12,8},{9,1... | collective-permute-start | bytes 1474568 | tf_op jit(solution)/shard_map/ppermute | solution.py:336
  20.0 12.0 %collective-permute-start.5 = (bf16[4,80,768]{2,1,0:T(8,128)(2,1)S(1)}, bf16[4,80,768]{2,1,0:T(8,128)(2,1)S(1)}, u32[]{:S(2)}, u32[]{:S(2)}) collective-permute-start(bf16[4,80,768]{2,1,0:T(8,128)(2,1)S(1)} %order_four.1.refs_0_), channel_id=1, source_target_pairs={{0,2},{2,0},{1,3},{3,1},{4,6},{6,4},{5,7},{7,5},{8,10},{10,8},{9,1... | collective-permute-start | bytes 1474568 | tf_op jit(solution)/shard_map/ppermute | solution.py:336
  21.5 10.2 %collective-permute-start.7 = (bf16[128,768]{1,0:T(8,128)(2,1)S(1)}, bf16[128,768]{1,0:T(8,128)(2,1)S(1)}, u32[]{:S(2)}, u32[]{:S(2)}) collective-permute-start(bf16[128,768]{1,0:T(8,128)(2,1)S(1)} %concatenate.20.one), channel_id=1, source_target_pairs={{0,16},{8,24},{16,0},{24,8},{1,17},{9,25},{17,1},{25,9},{2,18},{10... | collective-permute-start | bytes 589832 | tf_op jit(solution)/shard_map/ppermute | solution.py:336
  32.0 7.5 %collective-permute-start.8 = (bf16[4,40,768]{2,1,0:T(8,128)(2,1)S(1)}, bf16[4,40,768]{2,1,0:T(8,128)(2,1)S(1)}, u32[]{:S(2)}, u32[]{:S(2)}) collective-permute-start(bf16[4,40,768]{2,1,0:T(8,128)(2,1)S(1)} %slice.98), channel_id=1, source_target_pairs={{0,4},{4,0},{1,5},{5,1},{2,6},{6,2},{3,7},{7,3},{8,12},{12,8},{9,1... | collective-permute-start | bytes 737288 | tf_op jit(solution)/shard_map/ppermute | solution.py:336
  32.8 15.2 %collective-permute-start.10 = (bf16[4,80,768]{2,1,0:T(8,128)(2,1)S(1)}, bf16[4,80,768]{2,1,0:T(8,128)(2,1)S(1)}, u32[]{:S(2)}, u32[]{:S(2)}) collective-permute-start(bf16[4,80,768]{2,1,0:T(8,128)(2,1)S(1)} %order_four.1.refs_0_), channel_id=1, source_target_pairs={{0,1},{1,0},{2,3},{3,2},{4,5},{5,4},{6,7},{7,6},{8,9},{9,8},{10,11... | collective-permute-start | bytes 1474568 | tf_op jit(solution)/shard_map/ppermute | solution.py:336
  33.4 11.6 %collective-permute-start.15 = (bf16[2,128,768]{2,1,0:T(8,128)(2,1)S(1)}, bf16[2,128,768]{2,1,0:T(8,128)(2,1)S(1)}, u32[]{:S(2)}, u32[]{:S(2)}) collective-permute-start(bf16[2,128,768]{2,1,0:T(8,128)(2,1)S(1)} %pair_z.2.pair), channel_id=1, source_target_pairs={{0,8},{8,0},{16,24},{24,16},{1,9},{9,1},{17,25},{25,17},{2,10},{10... | collective-permute-start | bytes 1179656 | tf_op jit(solution)/shard_map/ppermute | solution.py:336
  34.9 13.1 %collective-permute-start.11 = (bf16[4,80,768]{2,1,0:T(8,128)(2,1)S(1)}, bf16[4,80,768]{2,1,0:T(8,128)(2,1)S(1)}, u32[]{:S(2)}, u32[]{:S(2)}) collective-permute-start(bf16[4,80,768]{2,1,0:T(8,128)(2,1)S(1)} %collective-permute-done.5.refs_1_), channel_id=1, source_target_pairs={{0,1},{1,0},{2,3},{3,2},{4,5},{5,4},{6,7},{7,6},{8,9},{9,8},{10,11... | collective-permute-start | bytes 1474568 | tf_op jit(solution)/shard_map/ppermute | solution.py:336
  35.1 8.2 %collective-permute-start.9 = (bf16[4,40,768]{2,1,0:T(8,128)(2,1)S(1)}, bf16[4,40,768]{2,1,0:T(8,128)(2,1)S(1)}, u32[]{:S(2)}, u32[]{:S(2)}) collective-permute-start(bf16[4,40,768]{2,1,0:T(8,128)(2,1)S(1)} %slice.99), channel_id=1, source_target_pairs={{0,2},{2,0},{1,3},{3,1},{4,6},{6,4},{5,7},{7,5},{8,10},{10,8},{9,1... | collective-permute-start | bytes 737288 | tf_op jit(solution)/shard_map/ppermute | solution.py:336
  39.5 10.1 %collective-permute-start.12 = (bf16[4,80,768]{2,1,0:T(8,128)(2,1)S(1)}, bf16[4,80,768]{2,1,0:T(8,128)(2,1)S(1)}, u32[]{:S(2)}, u32[]{:S(2)}) collective-permute-start(bf16[4,80,768]{2,1,0:T(8,128)(2,1)S(1)} %collective-permute-done.6.refs_2_), channel_id=1, source_target_pairs={{0,1},{1,0},{2,3},{3,2},{4,5},{5,4},{6,7},{7,6},{8,9},{9,8},{10,11... | collective-permute-start | bytes 1474568 | tf_op jit(solution)/shard_map/ppermute | solution.py:336
  43.3 5.3 %collective-permute-start.14 = (bf16[4,40,768]{2,1,0:T(8,128)(2,1)S(1)}, bf16[4,40,768]{2,1,0:T(8,128)(2,1)S(1)}, u32[]{:S(2)}, u32[]{:S(2)}) collective-permute-start(bf16[4,40,768]{2,1,0:T(8,128)(2,1)S(1)} %collective-permute-done.9.refs_4_), channel_id=1, source_target_pairs={{0,1},{1,0},{2,3},{3,2},{4,5},{5,4},{6,7},{7,6},{8,9},{9,8},{10,11... | collective-permute-start | bytes 737288 | tf_op jit(solution)/shard_map/ppermute | solution.py:336
  45.6 15.9 %collective-permute-start.20 = (bf16[192,768]{1,0:T(8,128)(2,1)S(1)}, bf16[192,768]{1,0:T(8,128)(2,1)S(1)}, u32[]{:S(2)}, u32[]{:S(2)}) collective-permute-start(bf16[192,768]{1,0:T(8,128)(2,1)S(1)} %pad_maximum_fusion.one), channel_id=1, source_target_pairs={{0,16},{8,24},{16,0},{24,8},{1,17},{9,25},{17,1},{25,9},{2,18},{10... | collective-permute-start | bytes 884744 | tf_op jit(solution)/shard_map/ppermute | solution.py:336
  48.0 22.1 %collective-permute-start.22 = (bf16[4,128,768]{2,1,0:T(8,128)(2,1)S(1)}, bf16[4,128,768]{2,1,0:T(8,128)(2,1)S(1)}, u32[]{:S(2)}, u32[]{:S(2)}) collective-permute-start(bf16[4,128,768]{2,1,0:T(8,128)(2,1)S(1)} %order_z.1.refs_0_), channel_id=1, source_target_pairs={{0,4},{4,0},{1,5},{5,1},{2,6},{6,2},{3,7},{7,3},{8,12},{12,8},{9,1... | collective-permute-start | bytes 2359304 | tf_op jit(solution)/shard_map/ppermute | solution.py:336
  48.6 21.6 %collective-permute-start.21 = (bf16[4,128,768]{2,1,0:T(8,128)(2,1)S(1)}, bf16[4,128,768]{2,1,0:T(8,128)(2,1)S(1)}, u32[]{:S(2)}, u32[]{:S(2)}) collective-permute-start(bf16[4,128,768]{2,1,0:T(8,128)(2,1)S(1)} %order_z.1.refs_0_), channel_id=1, source_target_pairs={{0,2},{2,0},{1,3},{3,1},{4,6},{6,4},{5,7},{7,5},{8,10},{10,8},{9,1... | collective-permute-start | bytes 2359304 | tf_op jit(solution)/shard_map/ppermute | solution.py:336
  54.4 7.1 %collective-permute-start.16 = (bf16[128,768]{1,0:T(8,128)(2,1)S(1)}, bf16[128,768]{1,0:T(8,128)(2,1)S(1)}, u32[]{:S(2)}, u32[]{:S(2)}) collective-permute-start(bf16[128,768]{1,0:T(8,128)(2,1)S(1)} %get-tuple-element.170.refs_0_), channel_id=1, source_target_pairs={{0,1},{1,0},{2,3},{3,2},{4,5},{5,4},{6,7},{7,6},{8,9},{9,8},{10,11... | collective-permute-start | bytes 589832 | tf_op jit(solution)/shard_map/ppermute | solution.py:336
  54.5 7.6 %collective-permute-start.17 = (bf16[128,768]{1,0:T(8,128)(2,1)S(1)}, bf16[128,768]{1,0:T(8,128)(2,1)S(1)}, u32[]{:S(2)}, u32[]{:S(2)}) collective-permute-start(bf16[128,768]{1,0:T(8,128)(2,1)S(1)} %get-tuple-element.171.refs_1_), channel_id=1, source_target_pairs={{0,1},{1,0},{2,3},{3,2},{4,5},{5,4},{6,7},{7,6},{8,9},{9,8},{10,11... | collective-permute-start | bytes 589832 | tf_op jit(solution)/shard_map/ppermute | solution.py:336
  61.6 8.6 %collective-permute-start.23 = (bf16[256,768]{1,0:T(8,128)(2,1)S(1)}, bf16[256,768]{1,0:T(8,128)(2,1)S(1)}, u32[]{:S(2)}, u32[]{:S(2)}) collective-permute-start(bf16[256,768]{1,0:T(8,128)(2,1)S(1)} %get-tuple-element.176.refs_0_), channel_id=1, source_target_pairs={{0,1},{1,0},{2,3},{3,2},{4,5},{5,4},{6,7},{7,6},{8,9},{9,8},{10,11... | collective-permute-start | bytes 1179656 | tf_op jit(solution)/shard_map/ppermute | solution.py:336
  62.1 8.1 %collective-permute-start.24 = (bf16[256,768]{1,0:T(8,128)(2,1)S(1)}, bf16[256,768]{1,0:T(8,128)(2,1)S(1)}, u32[]{:S(2)}, u32[]{:S(2)}) collective-permute-start(bf16[256,768]{1,0:T(8,128)(2,1)S(1)} %get-tuple-element.177.refs_1_), channel_id=1, source_target_pairs={{0,1},{1,0},{2,3},{3,2},{4,5},{5,4},{6,7},{7,6},{8,9},{9,8},{10,11... | collective-permute-start | bytes 1179656 | tf_op jit(solution)/shard_map/ppermute | solution.py:336
  65.0 15.5 %collective-permute-start.27 = (bf16[2,192,768]{2,1,0:T(8,128)(2,1)S(1)}, bf16[2,192,768]{2,1,0:T(8,128)(2,1)S(1)}, u32[]{:S(2)}, u32[]{:S(2)}) collective-permute-start(bf16[2,192,768]{2,1,0:T(8,128)(2,1)S(1)} %pair_z.3.pair), channel_id=1, source_target_pairs={{0,8},{8,0},{16,24},{24,16},{1,9},{9,1},{17,25},{25,17},{2,10},{10... | collective-permute-start | bytes 1769480 | tf_op jit(solution)/shard_map/ppermute | solution.py:336
  70.2 11.0 %collective-permute-start.25 = (bf16[4,64,768]{2,1,0:T(8,128)(2,1)S(1)}, bf16[4,64,768]{2,1,0:T(8,128)(2,1)S(1)}, u32[]{:S(2)}, u32[]{:S(2)}) collective-permute-start(bf16[4,64,768]{2,1,0:T(8,128)(2,1)S(1)} %slice.100), channel_id=1, source_target_pairs={{0,4},{4,0},{1,5},{5,1},{2,6},{6,2},{3,7},{7,3},{8,12},{12,8},{9,1... | collective-permute-start | bytes 1179656 | tf_op jit(solution)/shard_map/ppermute | solution.py:336
  71.2 10.9 %collective-permute-start.26 = (bf16[4,64,768]{2,1,0:T(8,128)(2,1)S(1)}, bf16[4,64,768]{2,1,0:T(8,128)(2,1)S(1)}, u32[]{:S(2)}, u32[]{:S(2)}) collective-permute-start(bf16[4,64,768]{2,1,0:T(8,128)(2,1)S(1)} %slice.101), channel_id=1, source_target_pairs={{0,2},{2,0},{1,3},{3,1},{4,6},{6,4},{5,7},{7,5},{8,10},{10,8},{9,1... | collective-permute-start | bytes 1179656 | tf_op jit(solution)/shard_map/ppermute | solution.py:336
  82.2 2.6 %collective-permute-start.34 = (bf16[4,64,768]{2,1,0:T(8,128)(2,1)S(1)}, bf16[4,64,768]{2,1,0:T(8,128)(2,1)S(1)}, u32[]{:S(2)}, u32[]{:S(2)}) collective-permute-start(bf16[4,64,768]{2,1,0:T(8,128)(2,1)S(1)} %collective-permute-done.26.refs_7_), channel_id=1, source_target_pairs={{0,1},{1,0},{2,3},{3,2},{4,5},{5,4},{6,7},{7,6},{8,9},{9,8},{10,11... | collective-permute-start | bytes 1179656 | tf_op jit(solution)/shard_map/ppermute | solution.py:336
  82.7 3.2 %collective-permute-start.32 = (bf16[4,128,768]{2,1,0:T(8,128)(2,1)S(1)}, bf16[4,128,768]{2,1,0:T(8,128)(2,1)S(1)}, u32[]{:S(2)}, u32[]{:S(2)}) collective-permute-start(bf16[4,128,768]{2,1,0:T(8,128)(2,1)S(1)} %collective-permute-done.22.refs_2_), channel_id=1, source_target_pairs={{0,1},{1,0},{2,3},{3,2},{4,5},{5,4},{6,7},{7,6},{8,9},{9,8},{10,11... | collective-permute-start | bytes 2359304 | tf_op jit(solution)/shard_map/ppermute | solution.py:336
  82.7 4.0 %collective-permute-start.30 = (bf16[4,128,768]{2,1,0:T(8,128)(2,1)S(1)}, bf16[4,128,768]{2,1,0:T(8,128)(2,1)S(1)}, u32[]{:S(2)}, u32[]{:S(2)}) collective-permute-start(bf16[4,128,768]{2,1,0:T(8,128)(2,1)S(1)} %order_z.1.refs_0_), channel_id=1, source_target_pairs={{0,1},{1,0},{2,3},{3,2},{4,5},{5,4},{6,7},{7,6},{8,9},{9,8},{10,11... | collective-permute-start | bytes 2359304 | tf_op jit(solution)/shard_map/ppermute | solution.py:336
  83.2 4.6 %collective-permute-start.31 = (bf16[4,128,768]{2,1,0:T(8,128)(2,1)S(1)}, bf16[4,128,768]{2,1,0:T(8,128)(2,1)S(1)}, u32[]{:S(2)}, u32[]{:S(2)}) collective-permute-start(bf16[4,128,768]{2,1,0:T(8,128)(2,1)S(1)} %collective-permute-done.21.refs_1_), channel_id=1, source_target_pairs={{0,1},{1,0},{2,3},{3,2},{4,5},{5,4},{6,7},{7,6},{8,9},{9,8},{10,11... | collective-permute-start | bytes 2359304 | tf_op jit(solution)/shard_map/ppermute | solution.py:336
  83.9 15.8 %collective-permute-start.28 = (bf16[4,96,768]{2,1,0:T(8,128)(2,1)S(1)}, bf16[4,96,768]{2,1,0:T(8,128)(2,1)S(1)}, u32[]{:S(2)}, u32[]{:S(2)}) collective-permute-start(bf16[4,96,768]{2,1,0:T(8,128)(2,1)S(1)} %get-tuple-element.195.refs_0_), channel_id=1, source_target_pairs={{0,4},{4,0},{1,5},{5,1},{2,6},{6,2},{3,7},{7,3},{8,12},{12,8},{9,1... | collective-permute-start | bytes 1769480 | tf_op jit(solution)/shard_map/ppermute | solution.py:336
  84.7 15.5 %collective-permute-start.29 = (bf16[4,96,768]{2,1,0:T(8,128)(2,1)S(1)}, bf16[4,96,768]{2,1,0:T(8,128)(2,1)S(1)}, u32[]{:S(2)}, u32[]{:S(2)}) collective-permute-start(bf16[4,96,768]{2,1,0:T(8,128)(2,1)S(1)} %get-tuple-element.196.refs_2_), channel_id=1, source_target_pairs={{0,2},{2,0},{1,3},{3,1},{4,6},{6,4},{5,7},{7,5},{8,10},{10,8},{9,1... | collective-permute-start | bytes 1769480 | tf_op jit(solution)/shard_map/ppermute | solution.py:336
  85.9 14.8 %collective-permute-start.35 = (bf16[4,96,768]{2,1,0:T(8,128)(2,1)S(1)}, bf16[4,96,768]{2,1,0:T(8,128)(2,1)S(1)}, u32[]{:S(2)}, u32[]{:S(2)}) collective-permute-start(bf16[4,96,768]{2,1,0:T(8,128)(2,1)S(1)} %get-tuple-element.195.refs_0_), channel_id=1, source_target_pairs={{0,1},{1,0},{2,3},{3,2},{4,5},{5,4},{6,7},{7,6},{8,9},{9,8},{10,11... | collective-permute-start | bytes 1769480 | tf_op jit(solution)/shard_map/ppermute | solution.py:336
  86.7 14.0 %collective-permute-start.37 = (bf16[4,96,768]{2,1,0:T(8,128)(2,1)S(1)}, bf16[4,96,768]{2,1,0:T(8,128)(2,1)S(1)}, u32[]{:S(2)}, u32[]{:S(2)}) collective-permute-start(bf16[4,96,768]{2,1,0:T(8,128)(2,1)S(1)} %get-tuple-element.196.refs_2_), channel_id=1, source_target_pairs={{0,1},{1,0},{2,3},{3,2},{4,5},{5,4},{6,7},{7,6},{8,9},{9,8},{10,11... | collective-permute-start | bytes 1769480 | tf_op jit(solution)/shard_map/ppermute | solution.py:336
  100.2 2.0 collective-permute-start.36
  100.2 2.8 %collective-permute-start.38 = (bf16[4,96,768]{2,1,0:T(8,128)(2,1)S(1)}, bf16[4,96,768]{2,1,0:T(8,128)(2,1)S(1)}, u32[]{:S(2)}, u32[]{:S(2)}) collective-permute-start(bf16[4,96,768]{2,1,0:T(8,128)(2,1)S(1)} %collective-permute-done.29.refs_3_), channel_id=1, source_target_pairs={{0,1},{1,0},{2,3},{3,2},{4,5},{5,4},{6,7},{7,6},{8,9},{9,8},{10,11... | collective-permute-start | bytes 1769480 | tf_op jit(solution)/shard_map/ppermute | solution.py:336
  117.5 5.3 %collective-permute-start.39 = (bf16[16,96,768]{2,1,0:T(8,128)(2,1)S(1)}, bf16[16,96,768]{2,1,0:T(8,128)(2,1)S(1)}, u32[]{:S(2)}, u32[]{:S(2)}) collective-permute-start(bf16[16,96,768]{2,1,0:T(8,128)(2,1)S(1)} %get-tuple-element.210), channel_id=1, source_target_pairs={{0,1},{1,0},{2,3},{3,2},{4,5},{5,4},{6,7},{7,6},{8,9},{9,8},{10,11... | collective-permute-start | bytes 7077896 | tf_op jit(solution)/shard_map/ppermute | solution.py:336
  123.6 16.7 %collective-permute-start.42 = (bf16[16,96,768]{2,1,0:T(8,128)(2,1)S(1)}, bf16[16,96,768]{2,1,0:T(8,128)(2,1)S(1)}, u32[]{:S(2)}, u32[]{:S(2)}) collective-permute-start(bf16[16,96,768]{2,1,0:T(8,128)(2,1)S(1)} %get-tuple-element.222), channel_id=1, source_target_pairs={{0,1},{1,0},{2,3},{3,2},{4,5},{5,4},{6,7},{7,6},{8,9},{9,8},{10,11... | collective-permute-start | bytes 7077896 | tf_op jit(solution)/shard_map/ppermute | solution.py:336
  124.1 16.3 %collective-permute-start.40 = (bf16[4,96,768]{2,1,0:T(8,128)(2,1)S(1)}, bf16[4,96,768]{2,1,0:T(8,128)(2,1)S(1)}, u32[]{:S(2)}, u32[]{:S(2)}) collective-permute-start(bf16[4,96,768]{2,1,0:T(8,128)(2,1)S(1)} %get-tuple-element.213), channel_id=1, source_target_pairs={{0,4},{4,0},{1,5},{5,1},{2,6},{6,2},{3,7},{7,3},{8,12},{12,8},{9,1... | collective-permute-start | bytes 1769480 | tf_op jit(solution)/shard_map/ppermute | solution.py:336
  125.2 15.1 %collective-permute-start.41 = (bf16[4,96,768]{2,1,0:T(8,128)(2,1)S(1)}, bf16[4,96,768]{2,1,0:T(8,128)(2,1)S(1)}, u32[]{:S(2)}, u32[]{:S(2)}) collective-permute-start(bf16[4,96,768]{2,1,0:T(8,128)(2,1)S(1)} %get-tuple-element.221), channel_id=1, source_target_pairs={{0,2},{2,0},{1,3},{3,1},{4,6},{6,4},{5,7},{7,5},{8,10},{10,8},{9,1... | collective-permute-start | bytes 1769480 | tf_op jit(solution)/shard_map/ppermute | solution.py:336
  137.1 3.2 %collective-permute-start.43 = (bf16[16,24,768]{2,1,0:T(8,128)(2,1)S(1)}, bf16[16,24,768]{2,1,0:T(8,128)(2,1)S(1)}, u32[]{:S(2)}, u32[]{:S(2)}) collective-permute-start(bf16[16,24,768]{2,1,0:T(8,128)(2,1)S(1)} %get-tuple-element.229), channel_id=1, source_target_pairs={{0,1},{1,0},{2,3},{3,2},{4,5},{5,4},{6,7},{7,6},{8,9},{9,8},{10,11... | collective-permute-start | bytes 1769480 | tf_op jit(solution)/shard_map/ppermute | solution.py:336
  141.1 13.1 %collective-permute-start.44 = (bf16[4,64,768]{2,1,0:T(8,128)(2,1)S(1)}, bf16[4,64,768]{2,1,0:T(8,128)(2,1)S(1)}, u32[]{:S(2)}, u32[]{:S(2)}) collective-permute-start(bf16[4,64,768]{2,1,0:T(8,128)(2,1)S(1)} %get-tuple-element.230), channel_id=1, source_target_pairs={{0,2},{2,0},{1,3},{3,1},{4,6},{6,4},{5,7},{7,5},{8,10},{10,8},{9,1... | collective-permute-start | bytes 1179656 | tf_op jit(solution)/shard_map/ppermute | solution.py:336
  142.6 11.6 %collective-permute-start.45 = (bf16[4,56,768]{2,1,0:T(8,128)(2,1)S(1)}, bf16[4,56,768]{2,1,0:T(8,128)(2,1)S(1)}, u32[]{:S(2)}, u32[]{:S(2)}) collective-permute-start(bf16[4,56,768]{2,1,0:T(8,128)(2,1)S(1)} %get-tuple-element.231), channel_id=1, source_target_pairs={{0,4},{4,0},{1,5},{5,1},{2,6},{6,2},{3,7},{7,3},{8,12},{12,8},{9,1... | collective-permute-start | bytes 1032200 | tf_op jit(solution)/shard_map/ppermute | solution.py:336
  144.4 19.2 %collective-permute-start.51 = (bf16[2,96,768]{2,1,0:T(8,128)(2,1)S(1)}, bf16[2,96,768]{2,1,0:T(8,128)(2,1)S(1)}, u32[]{:S(2)}, u32[]{:S(2)}) collective-permute-start(bf16[2,96,768]{2,1,0:T(8,128)(2,1)S(1)} %get-tuple-element.254), channel_id=1, source_target_pairs={{0,16},{8,24},{16,0},{24,8},{1,17},{9,25},{17,1},{25,9},{2,18},{10... | collective-permute-start | bytes 884744 | tf_op jit(solution)/shard_map/ppermute | solution.py:336
  147.3 16.4 %collective-permute-start.50 = (bf16[2,96,768]{2,1,0:T(8,128)(2,1)S(1)}, bf16[2,96,768]{2,1,0:T(8,128)(2,1)S(1)}, u32[]{:S(2)}, u32[]{:S(2)}) collective-permute-start(bf16[2,96,768]{2,1,0:T(8,128)(2,1)S(1)} %get-tuple-element.225), channel_id=1, source_target_pairs={{0,8},{8,0},{16,24},{24,16},{1,9},{9,1},{17,25},{25,17},{2,10},{10... | collective-permute-start | bytes 884744 | tf_op jit(solution)/shard_map/ppermute | solution.py:336
  154.2 10.0 %collective-permute-start.46 = (bf16[256,768]{1,0:T(8,128)(2,1)S(1)}, bf16[256,768]{1,0:T(8,128)(2,1)S(1)}, u32[]{:S(2)}, u32[]{:S(2)}) collective-permute-start(bf16[256,768]{1,0:T(8,128)(2,1)S(1)} %get-tuple-element.245), channel_id=1, source_target_pairs={{0,1},{1,0},{2,3},{3,2},{4,5},{5,4},{6,7},{7,6},{8,9},{9,8},{10,11... | collective-permute-start | bytes 1179656 | tf_op jit(solution)/shard_map/ppermute | solution.py:336
  155.2 21.6 %collective-permute-start.52 = (bf16[4,120,768]{2,1,0:T(8,128)(2,1)S(1)}, bf16[4,120,768]{2,1,0:T(8,128)(2,1)S(1)}, u32[]{:S(2)}, u32[]{:S(2)}) collective-permute-start(bf16[4,120,768]{2,1,0:T(8,128)(2,1)S(1)} %get-tuple-element.236), channel_id=1, source_target_pairs={{0,4},{4,0},{1,5},{5,1},{2,6},{6,2},{3,7},{7,3},{8,12},{12,8},{9,1... | collective-permute-start | bytes 2211848 | tf_op jit(solution)/shard_map/ppermute | solution.py:336
  156.5 20.3 %collective-permute-start.53 = (bf16[4,120,768]{2,1,0:T(8,128)(2,1)S(1)}, bf16[4,120,768]{2,1,0:T(8,128)(2,1)S(1)}, u32[]{:S(2)}, u32[]{:S(2)}) collective-permute-start(bf16[4,120,768]{2,1,0:T(8,128)(2,1)S(1)} %get-tuple-element.237), channel_id=1, source_target_pairs={{0,2},{2,0},{1,3},{3,1},{4,6},{6,4},{5,7},{7,5},{8,10},{10,8},{9,1... | collective-permute-start | bytes 2211848 | tf_op jit(solution)/shard_map/ppermute | solution.py:336
  163.7 3.4 %collective-permute-start.48 = (bf16[256,768]{1,0:T(8,128)(2,1)S(1)}, bf16[256,768]{1,0:T(8,128)(2,1)S(1)}, u32[]{:S(2)}, u32[]{:S(2)}) collective-permute-start(bf16[256,768]{1,0:T(8,128)(2,1)S(1)} %get-tuple-element.250), channel_id=1, source_target_pairs={{0,1},{1,0},{2,3},{3,2},{4,5},{5,4},{6,7},{7,6},{8,9},{9,8},{10,11... | collective-permute-start | bytes 1179656 | tf_op jit(solution)/shard_map/ppermute | solution.py:336
  164.2 3.4 %collective-permute-start.49 = (bf16[256,768]{1,0:T(8,128)(2,1)S(1)}, bf16[256,768]{1,0:T(8,128)(2,1)S(1)}, u32[]{:S(2)}, u32[]{:S(2)}) collective-permute-start(bf16[256,768]{1,0:T(8,128)(2,1)S(1)} %get-tuple-element.251), channel_id=1, source_target_pairs={{0,1},{1,0},{2,3},{3,2},{4,5},{5,4},{6,7},{7,6},{8,9},{9,8},{10,11... | collective-permute-start | bytes 1179656 | tf_op jit(solution)/shard_map/ppermute | solution.py:336
  165.4 7.7 %collective-permute-start.55 = (bf16[96,768]{1,0:T(8,128)(2,1)S(1)}, bf16[96,768]{1,0:T(8,128)(2,1)S(1)}, u32[]{:S(2)}, u32[]{:S(2)}) collective-permute-start(bf16[96,768]{1,0:T(8,128)(2,1)S(1)} %get-tuple-element.268), channel_id=1, source_target_pairs={{0,8},{8,0},{16,24},{24,16},{1,9},{9,1},{17,25},{25,17},{2,10},{10... | collective-permute-start | bytes 442376 | tf_op jit(solution)/shard_map/ppermute | solution.py:336
  167.1 9.7 %collective-permute-start.54 = (bf16[96,768]{1,0:T(8,128)(2,1)S(1)}, bf16[96,768]{1,0:T(8,128)(2,1)S(1)}, u32[]{:S(2)}, u32[]{:S(2)}) collective-permute-start(bf16[96,768]{1,0:T(8,128)(2,1)S(1)} %get-tuple-element.257), channel_id=1, source_target_pairs={{0,16},{8,24},{16,0},{24,8},{1,17},{9,25},{17,1},{25,9},{2,18},{10... | collective-permute-start | bytes 442376 | tf_op jit(solution)/shard_map/ppermute | solution.py:336
  176.8 4.0 %collective-permute-start.56 = (bf16[16,80,768]{2,1,0:T(8,128)(2,1)S(1)}, bf16[16,80,768]{2,1,0:T(8,128)(2,1)S(1)}, u32[]{:S(2)}, u32[]{:S(2)}) collective-permute-start(bf16[16,80,768]{2,1,0:T(8,128)(2,1)S(1)} %get-tuple-element.271), channel_id=1, source_target_pairs={{0,1},{1,0},{2,3},{3,2},{4,5},{5,4},{6,7},{7,6},{8,9},{9,8},{10,11... | collective-permute-start | bytes 5898248 | tf_op jit(solution)/shard_map/ppermute | solution.py:336
  181.5 8.4 %collective-permute-start.57 = (bf16[4,40,768]{2,1,0:T(8,128)(2,1)S(1)}, bf16[4,40,768]{2,1,0:T(8,128)(2,1)S(1)}, u32[]{:S(2)}, u32[]{:S(2)}) collective-permute-start(bf16[4,40,768]{2,1,0:T(8,128)(2,1)S(1)} %get-tuple-element.272), channel_id=1, source_target_pairs={{0,2},{2,0},{1,3},{3,1},{4,6},{6,4},{5,7},{7,5},{8,10},{10,8},{9,1... | collective-permute-start | bytes 737288 | tf_op jit(solution)/shard_map/ppermute | solution.py:336
  182.8 7.7 %collective-permute-start.58 = (bf16[4,40,768]{2,1,0:T(8,128)(2,1)S(1)}, bf16[4,40,768]{2,1,0:T(8,128)(2,1)S(1)}, u32[]{:S(2)}, u32[]{:S(2)}) collective-permute-start(bf16[4,40,768]{2,1,0:T(8,128)(2,1)S(1)} %get-tuple-element.273), channel_id=1, source_target_pairs={{0,4},{4,0},{1,5},{5,1},{2,6},{6,2},{3,7},{7,3},{8,12},{12,8},{9,1... | collective-permute-start | bytes 737288 | tf_op jit(solution)/shard_map/ppermute | solution.py:336
  184.8 15.4 %collective-permute-start.63 = (bf16[120,768]{1,0:T(8,128)(2,1)S(1)}, bf16[120,768]{1,0:T(8,128)(2,1)S(1)}, u32[]{:S(2)}, u32[]{:S(2)}) collective-permute-start(bf16[120,768]{1,0:T(8,128)(2,1)S(1)} %get-tuple-element.275), channel_id=1, source_target_pairs={{0,8},{8,0},{16,24},{24,16},{1,9},{9,1},{17,25},{25,17},{2,10},{10... | collective-permute-start | bytes 552968 | tf_op jit(solution)/shard_map/ppermute | solution.py:336
  185.1 16.2 %collective-permute-start.64 = (bf16[120,768]{1,0:T(8,128)(2,1)S(1)}, bf16[120,768]{1,0:T(8,128)(2,1)S(1)}, u32[]{:S(2)}, u32[]{:S(2)}) collective-permute-start(bf16[120,768]{1,0:T(8,128)(2,1)S(1)} %get-tuple-element.276), channel_id=1, source_target_pairs={{0,16},{8,24},{16,0},{24,8},{1,17},{9,25},{17,1},{25,9},{2,18},{10... | collective-permute-start | bytes 552968 | tf_op jit(solution)/shard_map/ppermute | solution.py:336
  186.7 14.6 %collective-permute-start.65 = (bf16[120,768]{1,0:T(8,128)(2,1)S(1)}, bf16[120,768]{1,0:T(8,128)(2,1)S(1)}, u32[]{:S(2)}, u32[]{:S(2)}) collective-permute-start(bf16[120,768]{1,0:T(8,128)(2,1)S(1)} %get-tuple-element.277), channel_id=1, source_target_pairs={{0,24},{8,16},{16,8},{24,0},{1,25},{9,17},{17,9},{25,1},{2,26},{10... | collective-permute-start | bytes 552968 | tf_op jit(solution)/shard_map/ppermute | solution.py:336
  191.4 15.7 %collective-permute-start.59 = (bf16[4,80,768]{2,1,0:T(8,128)(2,1)S(1)}, bf16[4,80,768]{2,1,0:T(8,128)(2,1)S(1)}, u32[]{:S(2)}, u32[]{:S(2)}) collective-permute-start(bf16[4,80,768]{2,1,0:T(8,128)(2,1)S(1)} %get-tuple-element.280), channel_id=1, source_target_pairs={{0,4},{4,0},{1,5},{5,1},{2,6},{6,2},{3,7},{7,3},{8,12},{12,8},{9,1... | collective-permute-start | bytes 1474568 | tf_op jit(solution)/shard_map/ppermute | solution.py:336
  192.2 14.8 %collective-permute-start.60 = (bf16[4,80,768]{2,1,0:T(8,128)(2,1)S(1)}, bf16[4,80,768]{2,1,0:T(8,128)(2,1)S(1)}, u32[]{:S(2)}, u32[]{:S(2)}) collective-permute-start(bf16[4,80,768]{2,1,0:T(8,128)(2,1)S(1)} %get-tuple-element.281), channel_id=1, source_target_pairs={{0,2},{2,0},{1,3},{3,1},{4,6},{6,4},{5,7},{7,5},{8,10},{10,8},{9,1... | collective-permute-start | bytes 1474568 | tf_op jit(solution)/shard_map/ppermute | solution.py:336
  201.3 4.4 %collective-permute-start.61 = (bf16[48,768]{1,0:T(8,128)(2,1)S(1)}, bf16[48,768]{1,0:T(8,128)(2,1)S(1)}, u32[]{:S(2)}, u32[]{:S(2)}) collective-permute-start(bf16[48,768]{1,0:T(8,128)(2,1)S(1)} %get-tuple-element.286), channel_id=1, source_target_pairs={{0,2},{2,0},{1,3},{3,1},{4,6},{6,4},{5,7},{7,5},{8,10},{10,8},{9,1... | collective-permute-start | bytes 221192 | tf_op jit(solution)/shard_map/ppermute | solution.py:336
  202.7 4.4 %collective-permute-start.62 = (bf16[48,768]{1,0:T(8,128)(2,1)S(1)}, bf16[48,768]{1,0:T(8,128)(2,1)S(1)}, u32[]{:S(2)}, u32[]{:S(2)}) collective-permute-start(bf16[48,768]{1,0:T(8,128)(2,1)S(1)} %get-tuple-element.288), channel_id=1, source_target_pairs={{0,4},{4,0},{1,5},{5,1},{2,6},{6,2},{3,7},{7,3},{8,12},{12,8},{9,1... | collective-permute-start | bytes 221192 | tf_op jit(solution)/shard_map/ppermute | solution.py:336
  208.0 8.7 %collective-permute-start.66 = (bf16[80,768]{1,0:T(8,128)(2,1)S(1)}, bf16[80,768]{1,0:T(8,128)(2,1)S(1)}, u32[]{:S(2)}, u32[]{:S(2)}) collective-permute-start(bf16[80,768]{1,0:T(8,128)(2,1)S(1)} %get-tuple-element.296), channel_id=1, source_target_pairs={{0,8},{8,0},{16,24},{24,16},{1,9},{9,1},{17,25},{25,17},{2,10},{10... | collective-permute-start | bytes 368648 | tf_op jit(solution)/shard_map/ppermute | solution.py:336
  211.2 9.6 %collective-permute-start.67 = (bf16[80,768]{1,0:T(8,128)(2,1)S(1)}, bf16[80,768]{1,0:T(8,128)(2,1)S(1)}, u32[]{:S(2)}, u32[]{:S(2)}) collective-permute-start(bf16[80,768]{1,0:T(8,128)(2,1)S(1)} %get-tuple-element.297), channel_id=1, source_target_pairs={{0,16},{8,24},{16,0},{24,8},{1,17},{9,25},{17,1},{25,9},{2,18},{10... | collective-permute-start | bytes 368648 | tf_op jit(solution)/shard_map/ppermute | solution.py:336
  211.2 9.6 %collective-permute-start.68 = (bf16[80,768]{1,0:T(8,128)(2,1)S(1)}, bf16[80,768]{1,0:T(8,128)(2,1)S(1)}, u32[]{:S(2)}, u32[]{:S(2)}) collective-permute-start(bf16[80,768]{1,0:T(8,128)(2,1)S(1)} %get-tuple-element.298), channel_id=1, source_target_pairs={{0,24},{8,16},{16,8},{24,0},{1,25},{9,17},{17,9},{25,1},{2,26},{10... | collective-permute-start | bytes 368648 | tf_op jit(solution)/shard_map/ppermute | solution.py:336
  (32 other events, 429.4 us)

commit v3 on v2

--- a/solution.py
+++ b/solution.py
@@ -1512,7 +1512,6 @@
     mid_y, mid_x = hold((mid_y, mid_x), a_send)
     far_in, next_in = hold((far_in, next_in), a_send)
     core_sums = pp(after(a_send, mid_y, mid_x, far_in, next_in), "seq")
-    to_far_x, to_far_y, down_mine = reduce_fourth(ids, upper, lower, far_in, next_in)
     part = [unit(a_own), unit(core_sums)]
     corner = reduce_corner(ids, part, cut_a)
     low, high = pp(corner[0], "x"), pp(corner[1], "y")
@@ -1521,7 +1520,8 @@
     low, high = hold((low, high), *sends)
     to_y, to_x = reduce_sides(ids, part, low, high)
     side_y, side_x = pp(to_y, "y"), pp(to_x, "x")
-    received = [pp(after(to_far_x, to_x), "x"), pp(after(to_far_y, to_y), "y")]
+    to_far_x, to_far_y, down_mine = reduce_fourth(ids, upper, lower, after(far_in, to_y, to_x), next_in)
+    received = [pp(to_far_x, "x"), pp(to_far_y, "y")]
     grad_in = last(
         ids, weights_again, g_first, g_q, g_keys, after(g_values, to_y, to_x), tokens
     )

time: 224 us -> 224 us (level)
  transfers between devices with their start and end apart: 69 -> 69, of which waited for: 29 -> 30; matrix products, arithmetic and copies ran while one was open for 4% -> 4% of each run, Pallas kernels for 33% -> 33%
where the time goes in v3:
time: 224 us
  Pallas kernels  92.2 us (41%)
  waiting for transfers between devices  59.4 us (27%)
  starting transfers between devices  57.2 us (26%)
  local copies, waits for them, and re-layouts  11.3 us (5%)
  other arithmetic  2.42 us (1%)
    pallas_call x27, Pallas kernels, call(): pl.pallas_call(body, grid_spec=pltpu.PrefetchScalarGridSpec(num_scalar_pr...  92.2 us
    ppermute x69, waiting for transfers between devices, pp(): return lax.ppermute(value, axis, [(i, i ^ step) for i in range(size)])  59.4 us
    ppermute x69, starting transfers between devices, pp(): return lax.ppermute(value, axis, [(i, i ^ step) for i in range(size)])  57.2 us
    pad x8, local copies, waits for them, and re-layouts, local(): jnp.pad(part.reshape(1, -1), ((0, 0), (0, width - part.shape[0])))  5.29 us
  transfers between devices with their start and end apart: 69, of which 30 were waited for; matrix products, arithmetic and copies ran while one was open for 4% of the time, Pallas kernels for 33%

profile of v3, /device:TPU:0, one launch (start us, length us, event | category | flops | bytes accessed | tf_op | source)
XLA Modules:
  0.0 223.9 jit_solution(8191186077196229268)
XLA Ops:
  0.7 0.9 fusion.4
  2.3 5.1 %collective-permute-start.4 = (bf16[80,768]{1,0:T(8,128)(2,1)S(1)}, bf16[80,768]{1,0:T(8,128)(2,1)S(1)}, u32[]{:S(2)}, u32[]{:S(2)}) collective-permute-start(bf16[80,768]{1,0:T(8,128)(2,1)S(1)} %concatenate.19.refs_0_), channel_id=1, source_target_pairs={{0,24},{8,16},{16,8},{24,0},{1,25},{9,17},{17,9},{25,1},{2,26},{10... | collective-permute-start | bytes 368648 | tf_op jit(solution)/shard_map/ppermute | solution.py:336
  8.1 0.9 fusion.3
  9.0 1.7 collective-permute-start
  10.7 1.5 collective-permute-start.1
  20.0 1.5 collective-permute-start.5
  21.5 1.0 collective-permute-start.7
  22.5 3.1 %prepare.1 = (bf16[512,768]{1,0:T(8,128)(2,1)S(1)}, bf16[512,768]{1,0:T(8,128)(2,1)S(1)}, bf16[512,768]{1,0:T(8,128)(2,1)S(1)}) custom-call(s32[4]{0:T(128)S(1)} %pad_add_fusion.ids, bf16[512,768]{1,0:T(8,128)(2,1)S(1)} %bitcast.78, s32[2,1,192,256]{3,2,1,0:T(8,128)S(1)} %bitcast.93, s32[2,1,192,256]{3,2,1,0:T(8,128)S(1)} %bitcast.94), custom_call_target="tpu_custom_call" | custom-call | flops 1024 | bytes 393216 | tf_op jit(solution)/shard_map/prepare/pallas_call | solution.py:459
  25.6 6.0 %collective-permute-done.7.two = bf16[128,768]{1,0:T(8,128)(2,1)S(1)} collective-permute-done((bf16[128,768]{1,0:T(8,128)(2,1)S(1)}, bf16[128,768]{1,0:T(8,128)(2,1)S(1)}, u32[]{:S(2)}, u32[]{:S(2)}) %collective-permute-start.7) | collective-permute-done | bytes 196640 | tf_op jit(solution)/shard_map/ppermute | solution.py:336
  33.4 1.5 collective-permute-start.15
  35.7 3.8 %collective-permute-done.8.refs_3_ = bf16[4,40,768]{2,1,0:T(8,128)(2,1)S(1)} collective-permute-done((bf16[4,40,768]{2,1,0:T(8,128)(2,1)S(1)}, bf16[4,40,768]{2,1,0:T(8,128)(2,1)S(1)}, u32[]{:S(2)}, u32[]{:S(2)}) %collective-permute-start.8) | collective-permute-done | bytes 245792 | tf_op jit(solution)/shard_map/ppermute | solution.py:336
  39.5 3.8 %collective-permute-done.9.refs_4_ = bf16[4,40,768]{2,1,0:T(8,128)(2,1)S(1)} collective-permute-done((bf16[4,40,768]{2,1,0:T(8,128)(2,1)S(1)}, bf16[4,40,768]{2,1,0:T(8,128)(2,1)S(1)}, u32[]{:S(2)}, u32[]{:S(2)}) %collective-permute-start.9) | collective-permute-done | bytes 245792 | tf_op jit(solution)/shard_map/ppermute | solution.py:336
  43.4 1.7 collective-permute-done.15.received
  45.6 2.4 %collective-permute-start.20 = (bf16[192,768]{1,0:T(8,128)(2,1)S(1)}, bf16[192,768]{1,0:T(8,128)(2,1)S(1)}, u32[]{:S(2)}, u32[]{:S(2)}) collective-permute-start(bf16[192,768]{1,0:T(8,128)(2,1)S(1)} %pad_maximum_fusion.one), channel_id=1, source_target_pairs={{0,16},{8,24},{16,0},{24,8},{1,17},{9,25},{17,1},{25,9},{2,18},{10... | collective-permute-start | bytes 884744 | tf_op jit(solution)/shard_map/ppermute | solution.py:336
  48.6 1.1 collective-permute-start.21
  49.7 4.6 %project.1 = (bf16[2,256,768]{2,1,0:T(8,128)(2,1)S(1)}, bf16[128,768]{1,0:T(8,128)(2,1)S(1)}, bf16[128,768]{1,0:T(8,128)(2,1)S(1)}, bf16[128,768]{1,0:T(8,128)(2...) custom-call(s32[4]{0:T(128)S(1)} %pad_add_fusion.ids, ...), custom_call_target="tpu_custom_call" | custom-call | flops 1024 | bytes 655360 | tf_op jit(solution)/shard_map/project/pallas_call | solution.py:459
  55.0 6.6 %collective-permute-done.20.two = bf16[192,768]{1,0:T(8,128)(2,1)S(1)} collective-permute-done((bf16[192,768]{1,0:T(8,128)(2,1)S(1)}, bf16[192,768]{1,0:T(8,128)(2,1)S(1)}, u32[]{:S(2)}, u32[]{:S(2)}) %collective-permute-start.20) | collective-permute-done | bytes 294944 | tf_op jit(solution)/shard_map/ppermute | solution.py:336
  63.1 1.3 collective-permute-done.19.refs_7_
  65.5 4.6 %attention.2 = (bf16[2,256,768]{2,1,0:T(8,128)(2,1)S(1)}, bf16[2,6,4,512,128]{4,3,2,1,0:T(8,128)(2,1)S(1)}) custom-call(s32[4]{0:T(128)S(1)} %pad_add_fusion.ids, bf16[2,256,768]{2,1,0:T(8,128)(2,1)S(1)} %get-tuple-element.178.q, bf16[128,768]{1,0:T(8,128)(2,1)S(1)} %get-tuple-element.169.refs_0_, bf16[128,768]{1,0:T(8,128)(2,1)S(1)} %get-tuple-element.170.refs_1_, ...), custom_call_target="tpu_custom_call" | custom-call | flops 1024 | bytes 917504 | tf_op jit(solution)/shard_map/attention/pallas_call | solution.py:459
  70.2 1.0 collective-permute-start.25
  71.2 1.4 collective-permute-start.26
  72.6 4.5 %attention.3 = (bf16[2,256,768]{2,1,0:T(8,128)(2,1)S(1)}, bf16[2,6,4,512,128]{4,3,2,1,0:T(8,128)(2,1)S(1)}) custom-call(s32[4]{0:T(128)S(1)} %pad_add_fusion.ids, bf16[2,256,768]{2,1,0:T(8,128)(2,1)S(1)} %get-tuple-element.178.q, bf16[256,768]{1,0:T(8,128)(2,1)S(1)} %get-tuple-element.175.refs_0_, ...), custom_call_target="tpu_custom_call", output_to_operand_aliasing={{0}: (7, {}), {1}: (8, {})} | custom-call | flops 1024 | bytes 917504 | tf_op jit(solution)/shard_map/attention/pallas_call | solution.py:459
  77.2 3.3 %collective-permute-done.27.received = bf16[2,192,768]{2,1,0:T(8,128)(2,1)S(1)} collective-permute-done((bf16[2,192,768]{2,1,0:T(8,128)(2,1)S(1)}, bf16[2,192,768]{2,1,0:T(8,128)(2,1)S(1)}, u32[]{:S(2)}, u32[]{:S(2)}) %collective-permute-start.27) | collective-permute-done | bytes 589856 | tf_op jit(solution)/shard_map/ppermute | solution.py:336
  81.3 0.9 collective-permute-done.26.refs_7_
  84.7 1.1 collective-permute-start.29
  86.8 1.0 collective-permute-done.31.refs_4_
  87.8 10.1 %feed_up.1 = (f32[8,3072]{1,0:T(8,128)S(1)}, f32[512,768]{1,0:T(8,128)S(1)}, f32[512,128]{1,0:T(8,128)S(1)}, bf16[512,3072]{1,0:T(8,128)(2,1)S(1)}, bf16[512,3072]{1,0:T(8,128)(2,1)S(1)}) custom-call(s32[4]{0:T(128)S(1)} %pad_add_fusion.ids, bf16[4,128,768]{2,1,0:T(8,128)(2,1)S(1)} %order_z.1.refs_0_, ...), custom_call_target="tpu_custom_call" | custom-call | flops 1024 | bytes 1572864 | tf_op jit(solution)/shard_map/feed_up/pallas_call | solution.py:459
  98.0 1.7 collective-permute-done.28.refs_1_
  100.7 1.5 collective-permute-done.36.refs_5_
  103.1 14.4 %feed_down.1 = (bf16[512,768]{1,0:T(8,128)(2,1)}, f32[512,768]{1,0:T(8,128)S(1)}, bf16[512,3072]{1,0:T(8,128)(2,1)S(1)}, bf16[16,96,768]{2,1,0:T(8,128)(2,1)S(1)...) custom-call(s32[4]{0:T(128)S(1)} %pad_add_fusion.ids, bf16[4,96,768]{2,1,0:T(8,128)(2,1)S(1)} %get-tuple-element.194.refs_0_, ...), custom_call_target="tpu_custom_call" | custom-call | flops 1024 | bytes 2359296 | tf_op jit(solution)/shard_map/feed_down/pallas_call | solution.py:459
  117.7 5.1 %up_grads.1 = (bf16[16,96,768]{2,1,0:T(8,128)(2,1)S(1)}, bf16[16,96,768]{2,1,0:T(8,128)(2,1)S(1)}) custom-call(s32[4]{0:T(128)S(1)} %pad_add_fusion.ids, bf16[512,3072]{1,0:T(8,128)(2,1)S(1)} %get-tuple-element.213.g_inner.refs_10_, f32[512,768]{1,0:T(8,128)S(1)} %get-tuple-element.203.refs_10_.scaled.refs_12_, ...), custom_call_target="tpu_custom_call" | custom-call | flops 1024 | bytes 1310720 | tf_op jit(solution)/shard_map/up_grads/pallas_call | solution.py:459
  124.1 1.2 collective-permute-start.40
  125.2 1.4 collective-permute-start.41
  126.7 10.5 %middle.1 = (f32[512,768]{1,0:T(8,128)S(1)}, bf16[512,768]{1,0:T(8,128)(2,1)S(1)}, bf16[16,24,768]{2,1,0:T(8,128)(2,1)S(1)}, bf16[16,24,768]{2,1,0:T(8,128)(2,1)S(1)}, f32[32,8,768]{2,1,0:T(8,128)S(1)}) custom-call(s32[4]{0:T(128)S(1)} %pad_add_fusion.ids, bf16[4,128,768]{2,1,0:T(8,128)(2,1)} %copy-done.2, bf16[4,128,768]{2,1,0:T(8,128)(2,1)} %copy-done.4, ...), custom_call_target="tpu_custom_call" | custom-call | flops 1024 | bytes 1179648 | tf_op jit(solution)/shard_map/middle/pallas_call | solution.py:459
  137.2 3.1 %collective-permute-done.41.refs_7_ = bf16[4,96,768]{2,1,0:T(8,128)(2,1)S(1)} collective-permute-done((bf16[4,96,768]{2,1,0:T(8,128)(2,1)S(1)}, bf16[4,96,768]{2,1,0:T(8,128)(2,1)S(1)}, u32[]{:S(2)}, u32[]{:S(2)}) %collective-permute-start.41) | collective-permute-done | bytes 589856 | tf_op jit(solution)/shard_map/ppermute | solution.py:336
  141.1 1.5 collective-permute-start.44
  143.1 1.3 reduce_second.1
  144.4 2.8 %collective-permute-start.51 = (bf16[2,96,768]{2,1,0:T(8,128)(2,1)S(1)}, bf16[2,96,768]{2,1,0:T(8,128)(2,1)S(1)}, u32[]{:S(2)}, u32[]{:S(2)}) collective-permute-start(bf16[2,96,768]{2,1,0:T(8,128)(2,1)S(1)} %get-tuple-element.253), channel_id=1, source_target_pairs={{0,16},{8,24},{16,0},{24,8},{1,17},{9,25},{17,1},{25,9},{2,18},{10... | collective-permute-start | bytes 884744 | tf_op jit(solution)/shard_map/ppermute | solution.py:336
  147.6 6.6 %attention_back.2 = (bf16[256,768]{1,0:T(8,128)(2,1)S(1)}, f32[256,768]{1,0:T(8,128)S(1)}, f32[256,768]{1,0:T(8,128)S(1)}, bf16[256,768]{1,0:T(8,128)(2,1)S(1)}, bf16[256,768]{1,0:T(8,128)(2,1)S(1)}) custom-call(s32[4]{0:T(128)S(1)} %pad_add_fusion.ids, bf16[2,256,768]{2,1,0:T(8,128)(2,1)S(1)} %get-tuple-element.178.q, ...), custom_call_target="tpu_custom_call" | custom-call | flops 1024 | bytes 1310720 | tf_op jit(solution)/shard_map/attention_back/pallas_call | solution.py:459
  154.3 1.0 reduce_sides.2
  155.2 1.3 collective-permute-start.52
  157.3 6.3 %attention_back.3 = (bf16[256,768]{1,0:T(8,128)(2,1)S(1)}, f32[256,768]{1,0:T(8,128)S(1)}, f32[256,768]{1,0:T(8,128)S(1)}, bf16[256,768]{1,0:T(8,128)(2,1)S(1)}, bf16[256,768]{1,0:T(8,128)(2,1)S(1)}) custom-call(s32[4]{0:T(128)S(1)} %pad_add_fusion.ids, bf16[2,256,768]{2,1,0:T(8,128)(2,1)S(1)} %get-tuple-element.178.q, ...), custom_call_target="tpu_custom_call" | custom-call | flops 1024 | bytes 1310720 | tf_op jit(solution)/shard_map/attention_back/pallas_call | solution.py:459
  165.4 1.7 collective-permute-start.55
  167.6 4.3 %input_grads.1 = (bf16[16,80,768]{2,1,0:T(8,128)(2,1)S(1)}, bf16[16,80,768]{2,1,0:T(8,128)(2,1)S(1)}, bf16[512,768]{1,0:T(8,128)(2,1)S(1)}, bf16[512,768]{1,0:T(8,128)(2,1)S(1)}, bf16[512,768]{1,0:T(8,128)(2,1)S(1)}) custom-call(s32[4]{0:T(128)S(1)} %pad_add_fusion.ids, bf16[512,768]{1,0:T(8,128)(2,1)S(1)} %bitcast.81, ...), custom_call_target="tpu_custom_call" | custom-call | flops 1024 | bytes 786432 | tf_op jit(solution)/shard_map/input_grads/pallas_call | solution.py:459
  171.9 1.2 collective-permute-done.55.from_next
  173.1 3.7 %collective-permute-done.54.from_far = bf16[96,768]{1,0:T(8,128)(2,1)S(1)} collective-permute-done((bf16[96,768]{1,0:T(8,128)(2,1)S(1)}, bf16[96,768]{1,0:T(8,128)(2,1)S(1)}, u32[]{:S(2)}, u32[]{:S(2)}) %collective-permute-start.54) | collective-permute-done | bytes 147488 | tf_op jit(solution)/shard_map/ppermute | solution.py:336
  176.9 4.0 %collective-permute-done.56 = bf16[16,80,768]{2,1,0:T(8,128)(2,1)S(1)} collective-permute-done((bf16[16,80,768]{2,1,0:T(8,128)(2,1)S(1)}, bf16[16,80,768]{2,1,0:T(8,128)(2,1)S(1)}, u32[]{:S(2)}, u32[]{:S(2)}) %collective-permute-start.56) | collective-permute-done | bytes 1966112 | tf_op jit(solution)/shard_map/ppermute | solution.py:336
  181.5 1.3 collective-permute-start.57
  183.6 1.2 reduce_depth.2
  185.1 1.6 collective-permute-start.64
  186.7 2.5 %collective-permute-start.65 = (bf16[120,768]{1,0:T(8,128)(2,1)S(1)}, bf16[120,768]{1,0:T(8,128)(2,1)S(1)}, u32[]{:S(2)}, u32[]{:S(2)}) collective-permute-start(bf16[120,768]{1,0:T(8,128)(2,1)S(1)} %get-tuple-element.276), channel_id=1, source_target_pairs={{0,24},{8,16},{16,8},{24,0},{1,25},{9,17},{17,9},{25,1},{2,26},{10... | collective-permute-start | bytes 552968 | tf_op jit(solution)/shard_map/ppermute | solution.py:336
  189.5 1.0 collective-permute-done.58.refs_5_
  191.4 0.9 collective-permute-start.59
  192.2 1.4 collective-permute-start.60
  193.7 6.5 %input_back.1 = bf16[512,768]{1,0:T(8,128)(2,1)} custom-call(s32[4]{0:T(128)S(1)} %pad_add_fusion.ids, bf16[4,80,768]{2,1,0:T(8,128)(2,1)} %copy-done.5, bf16[4,80,768]{2,1,0:T(8,128)(2,1)} %copy-done.10, bf16[4,80,768]{2,1,0:T(8,128)(2,1)} %copy-done.9, bf16[4,40,768]{2,1,0:T(8,128)(2,1)} %copy-done.18, bf16[4,40,768]{2,1,0:T(8,128)(2,1)} %copy-done.19, ...), custom_call_target="tpu_custom_call" | custom-call | flops 1024 | bytes 655360 | tf_op jit(solution)/shard_map/input_back/pallas_call | solution.py:459
  200.2 1.2 collective-permute-done.64
  201.9 1.4 collective-permute-start.61
  205.4 1.0 collective-permute-done.61
  206.4 1.3 collective-permute-done.62
  207.7 0.9 reduce_depth.3
  208.6 3.3 %collective-permute-start.66 = (bf16[80,768]{1,0:T(8,128)(2,1)S(1)}, bf16[80,768]{1,0:T(8,128)(2,1)S(1)}, u32[]{:S(2)}, u32[]{:S(2)}) collective-permute-start(bf16[80,768]{1,0:T(8,128)(2,1)S(1)} %get-tuple-element.294), channel_id=1, source_target_pairs={{0,8},{8,0},{16,24},{24,16},{1,9},{9,1},{17,25},{25,17},{2,10},{10... | collective-permute-start | bytes 368648 | tf_op jit(solution)/shard_map/ppermute | solution.py:336
  211.9 2.4 %collective-permute-start.68 = (bf16[80,768]{1,0:T(8,128)(2,1)S(1)}, bf16[80,768]{1,0:T(8,128)(2,1)S(1)}, u32[]{:S(2)}, u32[]{:S(2)}) collective-permute-start(bf16[80,768]{1,0:T(8,128)(2,1)S(1)} %get-tuple-element.296), channel_id=1, source_target_pairs={{0,24},{8,16},{16,8},{24,0},{1,25},{9,17},{17,9},{25,1},{2,26},{10... | collective-permute-start | bytes 368648 | tf_op jit(solution)/shard_map/ppermute | solution.py:336
  215.1 2.2 collective-permute-done.66
  217.3 4.2 %collective-permute-done.67 = bf16[80,768]{1,0:T(8,128)(2,1)S(1)} collective-permute-done((bf16[80,768]{1,0:T(8,128)(2,1)S(1)}, bf16[80,768]{1,0:T(8,128)(2,1)S(1)}, u32[]{:S(2)}, u32[]{:S(2)}) %collective-permute-start.67) | collective-permute-done | bytes 122912 | tf_op jit(solution)/shard_map/ppermute | solution.py:336
  (186 shorter events, 37.3 us)
Async XLA Ops:
  2.3 16.3 %collective-permute-start.4 = (bf16[80,768]{1,0:T(8,128)(2,1)S(1)}, bf16[80,768]{1,0:T(8,128)(2,1)S(1)}, u32[]{:S(2)}, u32[]{:S(2)}) collective-permute-start(bf16[80,768]{1,0:T(8,128)(2,1)S(1)} %concatenate.19.refs_0_), channel_id=1, source_target_pairs={{0,24},{8,16},{16,8},{24,0},{1,25},{9,17},{17,9},{25,1},{2,26},{10... | collective-permute-start | bytes 368648 | tf_op jit(solution)/shard_map/ppermute | solution.py:336
  7.4 11.2 %collective-permute-start.3 = (bf16[80,768]{1,0:T(8,128)(2,1)S(1)}, bf16[80,768]{1,0:T(8,128)(2,1)S(1)}, u32[]{:S(2)}, u32[]{:S(2)}) collective-permute-start(bf16[80,768]{1,0:T(8,128)(2,1)S(1)} %concatenate.19.refs_0_), channel_id=1, source_target_pairs={{0,16},{8,24},{16,0},{24,8},{1,17},{9,25},{17,1},{25,9},{2,18},{10... | collective-permute-start | bytes 368648 | tf_op jit(solution)/shard_map/ppermute | solution.py:336
  7.4 11.2 %collective-permute-start.2 = (bf16[80,768]{1,0:T(8,128)(2,1)S(1)}, bf16[80,768]{1,0:T(8,128)(2,1)S(1)}, u32[]{:S(2)}, u32[]{:S(2)}) collective-permute-start(bf16[80,768]{1,0:T(8,128)(2,1)S(1)} %concatenate.19.refs_0_), channel_id=1, source_target_pairs={{0,8},{8,0},{16,24},{24,16},{1,9},{9,1},{17,25},{25,17},{2,10},{10... | collective-permute-start | bytes 368648 | tf_op jit(solution)/shard_map/ppermute | solution.py:336
  9.0 9.6 %collective-permute-start = (bf16[48,768]{1,0:T(8,128)(2,1)S(1)}, bf16[48,768]{1,0:T(8,128)(2,1)S(1)}, u32[]{:S(2)}, u32[]{:S(2)}) collective-permute-start(bf16[48,768]{1,0:T(8,128)(2,1)S(1)} %get-tuple-element.332), channel_id=1, source_target_pairs={{0,2},{2,0},{1,3},{3,1},{4,6},{6,4},{5,7},{7,5},{8,10},{10,8},{9,1... | collective-permute-start | bytes 221192 | tf_op jit(solution)/shard_map/ppermute | solution.py:336
  10.7 7.9 %collective-permute-start.1 = (bf16[48,768]{1,0:T(8,128)(2,1)S(1)}, bf16[48,768]{1,0:T(8,128)(2,1)S(1)}, u32[]{:S(2)}, u32[]{:S(2)}) collective-permute-start(bf16[48,768]{1,0:T(8,128)(2,1)S(1)} %get-tuple-element.333), channel_id=1, source_target_pairs={{0,4},{4,0},{1,5},{5,1},{2,6},{6,2},{3,7},{7,3},{8,12},{12,8},{9,1... | collective-permute-start | bytes 221192 | tf_op jit(solution)/shard_map/ppermute | solution.py:336
  19.2 12.4 %collective-permute-start.6 = (bf16[4,80,768]{2,1,0:T(8,128)(2,1)S(1)}, bf16[4,80,768]{2,1,0:T(8,128)(2,1)S(1)}, u32[]{:S(2)}, u32[]{:S(2)}) collective-permute-start(bf16[4,80,768]{2,1,0:T(8,128)(2,1)S(1)} %order_four.1.refs_0_), channel_id=1, source_target_pairs={{0,4},{4,0},{1,5},{5,1},{2,6},{6,2},{3,7},{7,3},{8,12},{12,8},{9,1... | collective-permute-start | bytes 1474568 | tf_op jit(solution)/shard_map/ppermute | solution.py:336
  20.0 12.0 %collective-permute-start.5 = (bf16[4,80,768]{2,1,0:T(8,128)(2,1)S(1)}, bf16[4,80,768]{2,1,0:T(8,128)(2,1)S(1)}, u32[]{:S(2)}, u32[]{:S(2)}) collective-permute-start(bf16[4,80,768]{2,1,0:T(8,128)(2,1)S(1)} %order_four.1.refs_0_), channel_id=1, source_target_pairs={{0,2},{2,0},{1,3},{3,1},{4,6},{6,4},{5,7},{7,5},{8,10},{10,8},{9,1... | collective-permute-start | bytes 1474568 | tf_op jit(solution)/shard_map/ppermute | solution.py:336
  21.5 10.2 %collective-permute-start.7 = (bf16[128,768]{1,0:T(8,128)(2,1)S(1)}, bf16[128,768]{1,0:T(8,128)(2,1)S(1)}, u32[]{:S(2)}, u32[]{:S(2)}) collective-permute-start(bf16[128,768]{1,0:T(8,128)(2,1)S(1)} %concatenate.20.one), channel_id=1, source_target_pairs={{0,16},{8,24},{16,0},{24,8},{1,17},{9,25},{17,1},{25,9},{2,18},{10... | collective-permute-start | bytes 589832 | tf_op jit(solution)/shard_map/ppermute | solution.py:336
  32.0 7.5 %collective-permute-start.8 = (bf16[4,40,768]{2,1,0:T(8,128)(2,1)S(1)}, bf16[4,40,768]{2,1,0:T(8,128)(2,1)S(1)}, u32[]{:S(2)}, u32[]{:S(2)}) collective-permute-start(bf16[4,40,768]{2,1,0:T(8,128)(2,1)S(1)} %slice.98), channel_id=1, source_target_pairs={{0,4},{4,0},{1,5},{5,1},{2,6},{6,2},{3,7},{7,3},{8,12},{12,8},{9,1... | collective-permute-start | bytes 737288 | tf_op jit(solution)/shard_map/ppermute | solution.py:336
  32.8 15.2 %collective-permute-start.10 = (bf16[4,80,768]{2,1,0:T(8,128)(2,1)S(1)}, bf16[4,80,768]{2,1,0:T(8,128)(2,1)S(1)}, u32[]{:S(2)}, u32[]{:S(2)}) collective-permute-start(bf16[4,80,768]{2,1,0:T(8,128)(2,1)S(1)} %order_four.1.refs_0_), channel_id=1, source_target_pairs={{0,1},{1,0},{2,3},{3,2},{4,5},{5,4},{6,7},{7,6},{8,9},{9,8},{10,11... | collective-permute-start | bytes 1474568 | tf_op jit(solution)/shard_map/ppermute | solution.py:336
  33.4 11.6 %collective-permute-start.15 = (bf16[2,128,768]{2,1,0:T(8,128)(2,1)S(1)}, bf16[2,128,768]{2,1,0:T(8,128)(2,1)S(1)}, u32[]{:S(2)}, u32[]{:S(2)}) collective-permute-start(bf16[2,128,768]{2,1,0:T(8,128)(2,1)S(1)} %pair_z.2.pair), channel_id=1, source_target_pairs={{0,8},{8,0},{16,24},{24,16},{1,9},{9,1},{17,25},{25,17},{2,10},{10... | collective-permute-start | bytes 1179656 | tf_op jit(solution)/shard_map/ppermute | solution.py:336
  34.9 13.1 %collective-permute-start.11 = (bf16[4,80,768]{2,1,0:T(8,128)(2,1)S(1)}, bf16[4,80,768]{2,1,0:T(8,128)(2,1)S(1)}, u32[]{:S(2)}, u32[]{:S(2)}) collective-permute-start(bf16[4,80,768]{2,1,0:T(8,128)(2,1)S(1)} %collective-permute-done.5.refs_1_), channel_id=1, source_target_pairs={{0,1},{1,0},{2,3},{3,2},{4,5},{5,4},{6,7},{7,6},{8,9},{9,8},{10,11... | collective-permute-start | bytes 1474568 | tf_op jit(solution)/shard_map/ppermute | solution.py:336
  35.1 8.2 %collective-permute-start.9 = (bf16[4,40,768]{2,1,0:T(8,128)(2,1)S(1)}, bf16[4,40,768]{2,1,0:T(8,128)(2,1)S(1)}, u32[]{:S(2)}, u32[]{:S(2)}) collective-permute-start(bf16[4,40,768]{2,1,0:T(8,128)(2,1)S(1)} %slice.99), channel_id=1, source_target_pairs={{0,2},{2,0},{1,3},{3,1},{4,6},{6,4},{5,7},{7,5},{8,10},{10,8},{9,1... | collective-permute-start | bytes 737288 | tf_op jit(solution)/shard_map/ppermute | solution.py:336
  39.5 10.1 %collective-permute-start.12 = (bf16[4,80,768]{2,1,0:T(8,128)(2,1)S(1)}, bf16[4,80,768]{2,1,0:T(8,128)(2,1)S(1)}, u32[]{:S(2)}, u32[]{:S(2)}) collective-permute-start(bf16[4,80,768]{2,1,0:T(8,128)(2,1)S(1)} %collective-permute-done.6.refs_2_), channel_id=1, source_target_pairs={{0,1},{1,0},{2,3},{3,2},{4,5},{5,4},{6,7},{7,6},{8,9},{9,8},{10,11... | collective-permute-start | bytes 1474568 | tf_op jit(solution)/shard_map/ppermute | solution.py:336
  43.3 5.3 %collective-permute-start.14 = (bf16[4,40,768]{2,1,0:T(8,128)(2,1)S(1)}, bf16[4,40,768]{2,1,0:T(8,128)(2,1)S(1)}, u32[]{:S(2)}, u32[]{:S(2)}) collective-permute-start(bf16[4,40,768]{2,1,0:T(8,128)(2,1)S(1)} %collective-permute-done.9.refs_4_), channel_id=1, source_target_pairs={{0,1},{1,0},{2,3},{3,2},{4,5},{5,4},{6,7},{7,6},{8,9},{9,8},{10,11... | collective-permute-start | bytes 737288 | tf_op jit(solution)/shard_map/ppermute | solution.py:336
  45.6 15.9 %collective-permute-start.20 = (bf16[192,768]{1,0:T(8,128)(2,1)S(1)}, bf16[192,768]{1,0:T(8,128)(2,1)S(1)}, u32[]{:S(2)}, u32[]{:S(2)}) collective-permute-start(bf16[192,768]{1,0:T(8,128)(2,1)S(1)} %pad_maximum_fusion.one), channel_id=1, source_target_pairs={{0,16},{8,24},{16,0},{24,8},{1,17},{9,25},{17,1},{25,9},{2,18},{10... | collective-permute-start | bytes 884744 | tf_op jit(solution)/shard_map/ppermute | solution.py:336
  48.0 22.1 %collective-permute-start.22 = (bf16[4,128,768]{2,1,0:T(8,128)(2,1)S(1)}, bf16[4,128,768]{2,1,0:T(8,128)(2,1)S(1)}, u32[]{:S(2)}, u32[]{:S(2)}) collective-permute-start(bf16[4,128,768]{2,1,0:T(8,128)(2,1)S(1)} %order_z.1.refs_0_), channel_id=1, source_target_pairs={{0,4},{4,0},{1,5},{5,1},{2,6},{6,2},{3,7},{7,3},{8,12},{12,8},{9,1... | collective-permute-start | bytes 2359304 | tf_op jit(solution)/shard_map/ppermute | solution.py:336
  48.6 21.6 %collective-permute-start.21 = (bf16[4,128,768]{2,1,0:T(8,128)(2,1)S(1)}, bf16[4,128,768]{2,1,0:T(8,128)(2,1)S(1)}, u32[]{:S(2)}, u32[]{:S(2)}) collective-permute-start(bf16[4,128,768]{2,1,0:T(8,128)(2,1)S(1)} %order_z.1.refs_0_), channel_id=1, source_target_pairs={{0,2},{2,0},{1,3},{3,1},{4,6},{6,4},{5,7},{7,5},{8,10},{10,8},{9,1... | collective-permute-start | bytes 2359304 | tf_op jit(solution)/shard_map/ppermute | solution.py:336
  54.4 7.1 %collective-permute-start.16 = (bf16[128,768]{1,0:T(8,128)(2,1)S(1)}, bf16[128,768]{1,0:T(8,128)(2,1)S(1)}, u32[]{:S(2)}, u32[]{:S(2)}) collective-permute-start(bf16[128,768]{1,0:T(8,128)(2,1)S(1)} %get-tuple-element.169.refs_0_), channel_id=1, source_target_pairs={{0,1},{1,0},{2,3},{3,2},{4,5},{5,4},{6,7},{7,6},{8,9},{9,8},{10,11... | collective-permute-start | bytes 589832 | tf_op jit(solution)/shard_map/ppermute | solution.py:336
  54.5 7.6 %collective-permute-start.17 = (bf16[128,768]{1,0:T(8,128)(2,1)S(1)}, bf16[128,768]{1,0:T(8,128)(2,1)S(1)}, u32[]{:S(2)}, u32[]{:S(2)}) collective-permute-start(bf16[128,768]{1,0:T(8,128)(2,1)S(1)} %get-tuple-element.170.refs_1_), channel_id=1, source_target_pairs={{0,1},{1,0},{2,3},{3,2},{4,5},{5,4},{6,7},{7,6},{8,9},{9,8},{10,11... | collective-permute-start | bytes 589832 | tf_op jit(solution)/shard_map/ppermute | solution.py:336
  61.6 8.6 %collective-permute-start.23 = (bf16[256,768]{1,0:T(8,128)(2,1)S(1)}, bf16[256,768]{1,0:T(8,128)(2,1)S(1)}, u32[]{:S(2)}, u32[]{:S(2)}) collective-permute-start(bf16[256,768]{1,0:T(8,128)(2,1)S(1)} %get-tuple-element.175.refs_0_), channel_id=1, source_target_pairs={{0,1},{1,0},{2,3},{3,2},{4,5},{5,4},{6,7},{7,6},{8,9},{9,8},{10,11... | collective-permute-start | bytes 1179656 | tf_op jit(solution)/shard_map/ppermute | solution.py:336
  62.1 8.1 %collective-permute-start.24 = (bf16[256,768]{1,0:T(8,128)(2,1)S(1)}, bf16[256,768]{1,0:T(8,128)(2,1)S(1)}, u32[]{:S(2)}, u32[]{:S(2)}) collective-permute-start(bf16[256,768]{1,0:T(8,128)(2,1)S(1)} %get-tuple-element.176.refs_1_), channel_id=1, source_target_pairs={{0,1},{1,0},{2,3},{3,2},{4,5},{5,4},{6,7},{7,6},{8,9},{9,8},{10,11... | collective-permute-start | bytes 1179656 | tf_op jit(solution)/shard_map/ppermute | solution.py:336
  65.0 15.5 %collective-permute-start.27 = (bf16[2,192,768]{2,1,0:T(8,128)(2,1)S(1)}, bf16[2,192,768]{2,1,0:T(8,128)(2,1)S(1)}, u32[]{:S(2)}, u32[]{:S(2)}) collective-permute-start(bf16[2,192,768]{2,1,0:T(8,128)(2,1)S(1)} %pair_z.3.pair), channel_id=1, source_target_pairs={{0,8},{8,0},{16,24},{24,16},{1,9},{9,1},{17,25},{25,17},{2,10},{10... | collective-permute-start | bytes 1769480 | tf_op jit(solution)/shard_map/ppermute | solution.py:336
  70.2 11.0 %collective-permute-start.25 = (bf16[4,64,768]{2,1,0:T(8,128)(2,1)S(1)}, bf16[4,64,768]{2,1,0:T(8,128)(2,1)S(1)}, u32[]{:S(2)}, u32[]{:S(2)}) collective-permute-start(bf16[4,64,768]{2,1,0:T(8,128)(2,1)S(1)} %slice.100), channel_id=1, source_target_pairs={{0,4},{4,0},{1,5},{5,1},{2,6},{6,2},{3,7},{7,3},{8,12},{12,8},{9,1... | collective-permute-start | bytes 1179656 | tf_op jit(solution)/shard_map/ppermute | solution.py:336
  71.2 10.9 %collective-permute-start.26 = (bf16[4,64,768]{2,1,0:T(8,128)(2,1)S(1)}, bf16[4,64,768]{2,1,0:T(8,128)(2,1)S(1)}, u32[]{:S(2)}, u32[]{:S(2)}) collective-permute-start(bf16[4,64,768]{2,1,0:T(8,128)(2,1)S(1)} %slice.101), channel_id=1, source_target_pairs={{0,2},{2,0},{1,3},{3,1},{4,6},{6,4},{5,7},{7,5},{8,10},{10,8},{9,1... | collective-permute-start | bytes 1179656 | tf_op jit(solution)/shard_map/ppermute | solution.py:336
  82.2 2.6 %collective-permute-start.34 = (bf16[4,64,768]{2,1,0:T(8,128)(2,1)S(1)}, bf16[4,64,768]{2,1,0:T(8,128)(2,1)S(1)}, u32[]{:S(2)}, u32[]{:S(2)}) collective-permute-start(bf16[4,64,768]{2,1,0:T(8,128)(2,1)S(1)} %collective-permute-done.26.refs_7_), channel_id=1, source_target_pairs={{0,1},{1,0},{2,3},{3,2},{4,5},{5,4},{6,7},{7,6},{8,9},{9,8},{10,11... | collective-permute-start | bytes 1179656 | tf_op jit(solution)/shard_map/ppermute | solution.py:336
  82.7 3.2 %collective-permute-start.32 = (bf16[4,128,768]{2,1,0:T(8,128)(2,1)S(1)}, bf16[4,128,768]{2,1,0:T(8,128)(2,1)S(1)}, u32[]{:S(2)}, u32[]{:S(2)}) collective-permute-start(bf16[4,128,768]{2,1,0:T(8,128)(2,1)S(1)} %collective-permute-done.22.refs_2_), channel_id=1, source_target_pairs={{0,1},{1,0},{2,3},{3,2},{4,5},{5,4},{6,7},{7,6},{8,9},{9,8},{10,11... | collective-permute-start | bytes 2359304 | tf_op jit(solution)/shard_map/ppermute | solution.py:336
  82.7 4.0 %collective-permute-start.30 = (bf16[4,128,768]{2,1,0:T(8,128)(2,1)S(1)}, bf16[4,128,768]{2,1,0:T(8,128)(2,1)S(1)}, u32[]{:S(2)}, u32[]{:S(2)}) collective-permute-start(bf16[4,128,768]{2,1,0:T(8,128)(2,1)S(1)} %order_z.1.refs_0_), channel_id=1, source_target_pairs={{0,1},{1,0},{2,3},{3,2},{4,5},{5,4},{6,7},{7,6},{8,9},{9,8},{10,11... | collective-permute-start | bytes 2359304 | tf_op jit(solution)/shard_map/ppermute | solution.py:336
  83.2 4.6 %collective-permute-start.31 = (bf16[4,128,768]{2,1,0:T(8,128)(2,1)S(1)}, bf16[4,128,768]{2,1,0:T(8,128)(2,1)S(1)}, u32[]{:S(2)}, u32[]{:S(2)}) collective-permute-start(bf16[4,128,768]{2,1,0:T(8,128)(2,1)S(1)} %collective-permute-done.21.refs_1_), channel_id=1, source_target_pairs={{0,1},{1,0},{2,3},{3,2},{4,5},{5,4},{6,7},{7,6},{8,9},{9,8},{10,11... | collective-permute-start | bytes 2359304 | tf_op jit(solution)/shard_map/ppermute | solution.py:336
  83.9 15.8 %collective-permute-start.28 = (bf16[4,96,768]{2,1,0:T(8,128)(2,1)S(1)}, bf16[4,96,768]{2,1,0:T(8,128)(2,1)S(1)}, u32[]{:S(2)}, u32[]{:S(2)}) collective-permute-start(bf16[4,96,768]{2,1,0:T(8,128)(2,1)S(1)} %get-tuple-element.194.refs_0_), channel_id=1, source_target_pairs={{0,4},{4,0},{1,5},{5,1},{2,6},{6,2},{3,7},{7,3},{8,12},{12,8},{9,1... | collective-permute-start | bytes 1769480 | tf_op jit(solution)/shard_map/ppermute | solution.py:336
  84.7 15.5 %collective-permute-start.29 = (bf16[4,96,768]{2,1,0:T(8,128)(2,1)S(1)}, bf16[4,96,768]{2,1,0:T(8,128)(2,1)S(1)}, u32[]{:S(2)}, u32[]{:S(2)}) collective-permute-start(bf16[4,96,768]{2,1,0:T(8,128)(2,1)S(1)} %get-tuple-element.195.refs_2_), channel_id=1, source_target_pairs={{0,2},{2,0},{1,3},{3,1},{4,6},{6,4},{5,7},{7,5},{8,10},{10,8},{9,1... | collective-permute-start | bytes 1769480 | tf_op jit(solution)/shard_map/ppermute | solution.py:336
  85.9 14.8 %collective-permute-start.35 = (bf16[4,96,768]{2,1,0:T(8,128)(2,1)S(1)}, bf16[4,96,768]{2,1,0:T(8,128)(2,1)S(1)}, u32[]{:S(2)}, u32[]{:S(2)}) collective-permute-start(bf16[4,96,768]{2,1,0:T(8,128)(2,1)S(1)} %get-tuple-element.194.refs_0_), channel_id=1, source_target_pairs={{0,1},{1,0},{2,3},{3,2},{4,5},{5,4},{6,7},{7,6},{8,9},{9,8},{10,11... | collective-permute-start | bytes 1769480 | tf_op jit(solution)/shard_map/ppermute | solution.py:336
  86.7 14.0 %collective-permute-start.37 = (bf16[4,96,768]{2,1,0:T(8,128)(2,1)S(1)}, bf16[4,96,768]{2,1,0:T(8,128)(2,1)S(1)}, u32[]{:S(2)}, u32[]{:S(2)}) collective-permute-start(bf16[4,96,768]{2,1,0:T(8,128)(2,1)S(1)} %get-tuple-element.195.refs_2_), channel_id=1, source_target_pairs={{0,1},{1,0},{2,3},{3,2},{4,5},{5,4},{6,7},{7,6},{8,9},{9,8},{10,11... | collective-permute-start | bytes 1769480 | tf_op jit(solution)/shard_map/ppermute | solution.py:336
  100.2 2.0 collective-permute-start.36
  100.2 2.8 %collective-permute-start.38 = (bf16[4,96,768]{2,1,0:T(8,128)(2,1)S(1)}, bf16[4,96,768]{2,1,0:T(8,128)(2,1)S(1)}, u32[]{:S(2)}, u32[]{:S(2)}) collective-permute-start(bf16[4,96,768]{2,1,0:T(8,128)(2,1)S(1)} %collective-permute-done.29.refs_3_), channel_id=1, source_target_pairs={{0,1},{1,0},{2,3},{3,2},{4,5},{5,4},{6,7},{7,6},{8,9},{9,8},{10,11... | collective-permute-start | bytes 1769480 | tf_op jit(solution)/shard_map/ppermute | solution.py:336
  117.5 5.3 %collective-permute-start.39 = (bf16[16,96,768]{2,1,0:T(8,128)(2,1)S(1)}, bf16[16,96,768]{2,1,0:T(8,128)(2,1)S(1)}, u32[]{:S(2)}, u32[]{:S(2)}) collective-permute-start(bf16[16,96,768]{2,1,0:T(8,128)(2,1)S(1)} %get-tuple-element.209), channel_id=1, source_target_pairs={{0,1},{1,0},{2,3},{3,2},{4,5},{5,4},{6,7},{7,6},{8,9},{9,8},{10,11... | collective-permute-start | bytes 7077896 | tf_op jit(solution)/shard_map/ppermute | solution.py:336
  123.6 16.7 %collective-permute-start.42 = (bf16[16,96,768]{2,1,0:T(8,128)(2,1)S(1)}, bf16[16,96,768]{2,1,0:T(8,128)(2,1)S(1)}, u32[]{:S(2)}, u32[]{:S(2)}) collective-permute-start(bf16[16,96,768]{2,1,0:T(8,128)(2,1)S(1)} %get-tuple-element.221), channel_id=1, source_target_pairs={{0,1},{1,0},{2,3},{3,2},{4,5},{5,4},{6,7},{7,6},{8,9},{9,8},{10,11... | collective-permute-start | bytes 7077896 | tf_op jit(solution)/shard_map/ppermute | solution.py:336
  124.1 16.3 %collective-permute-start.40 = (bf16[4,96,768]{2,1,0:T(8,128)(2,1)S(1)}, bf16[4,96,768]{2,1,0:T(8,128)(2,1)S(1)}, u32[]{:S(2)}, u32[]{:S(2)}) collective-permute-start(bf16[4,96,768]{2,1,0:T(8,128)(2,1)S(1)} %get-tuple-element.212), channel_id=1, source_target_pairs={{0,4},{4,0},{1,5},{5,1},{2,6},{6,2},{3,7},{7,3},{8,12},{12,8},{9,1... | collective-permute-start | bytes 1769480 | tf_op jit(solution)/shard_map/ppermute | solution.py:336
  125.2 15.1 %collective-permute-start.41 = (bf16[4,96,768]{2,1,0:T(8,128)(2,1)S(1)}, bf16[4,96,768]{2,1,0:T(8,128)(2,1)S(1)}, u32[]{:S(2)}, u32[]{:S(2)}) collective-permute-start(bf16[4,96,768]{2,1,0:T(8,128)(2,1)S(1)} %get-tuple-element.220), channel_id=1, source_target_pairs={{0,2},{2,0},{1,3},{3,1},{4,6},{6,4},{5,7},{7,5},{8,10},{10,8},{9,1... | collective-permute-start | bytes 1769480 | tf_op jit(solution)/shard_map/ppermute | solution.py:336
  137.1 3.2 %collective-permute-start.43 = (bf16[16,24,768]{2,1,0:T(8,128)(2,1)S(1)}, bf16[16,24,768]{2,1,0:T(8,128)(2,1)S(1)}, u32[]{:S(2)}, u32[]{:S(2)}) collective-permute-start(bf16[16,24,768]{2,1,0:T(8,128)(2,1)S(1)} %get-tuple-element.228), channel_id=1, source_target_pairs={{0,1},{1,0},{2,3},{3,2},{4,5},{5,4},{6,7},{7,6},{8,9},{9,8},{10,11... | collective-permute-start | bytes 1769480 | tf_op jit(solution)/shard_map/ppermute | solution.py:336
  141.1 13.1 %collective-permute-start.44 = (bf16[4,64,768]{2,1,0:T(8,128)(2,1)S(1)}, bf16[4,64,768]{2,1,0:T(8,128)(2,1)S(1)}, u32[]{:S(2)}, u32[]{:S(2)}) collective-permute-start(bf16[4,64,768]{2,1,0:T(8,128)(2,1)S(1)} %get-tuple-element.229), channel_id=1, source_target_pairs={{0,2},{2,0},{1,3},{3,1},{4,6},{6,4},{5,7},{7,5},{8,10},{10,8},{9,1... | collective-permute-start | bytes 1179656 | tf_op jit(solution)/shard_map/ppermute | solution.py:336
  142.6 11.6 %collective-permute-start.45 = (bf16[4,56,768]{2,1,0:T(8,128)(2,1)S(1)}, bf16[4,56,768]{2,1,0:T(8,128)(2,1)S(1)}, u32[]{:S(2)}, u32[]{:S(2)}) collective-permute-start(bf16[4,56,768]{2,1,0:T(8,128)(2,1)S(1)} %get-tuple-element.230), channel_id=1, source_target_pairs={{0,4},{4,0},{1,5},{5,1},{2,6},{6,2},{3,7},{7,3},{8,12},{12,8},{9,1... | collective-permute-start | bytes 1032200 | tf_op jit(solution)/shard_map/ppermute | solution.py:336
  144.4 19.2 %collective-permute-start.51 = (bf16[2,96,768]{2,1,0:T(8,128)(2,1)S(1)}, bf16[2,96,768]{2,1,0:T(8,128)(2,1)S(1)}, u32[]{:S(2)}, u32[]{:S(2)}) collective-permute-start(bf16[2,96,768]{2,1,0:T(8,128)(2,1)S(1)} %get-tuple-element.253), channel_id=1, source_target_pairs={{0,16},{8,24},{16,0},{24,8},{1,17},{9,25},{17,1},{25,9},{2,18},{10... | collective-permute-start | bytes 884744 | tf_op jit(solution)/shard_map/ppermute | solution.py:336
  147.3 16.4 %collective-permute-start.50 = (bf16[2,96,768]{2,1,0:T(8,128)(2,1)S(1)}, bf16[2,96,768]{2,1,0:T(8,128)(2,1)S(1)}, u32[]{:S(2)}, u32[]{:S(2)}) collective-permute-start(bf16[2,96,768]{2,1,0:T(8,128)(2,1)S(1)} %get-tuple-element.224), channel_id=1, source_target_pairs={{0,8},{8,0},{16,24},{24,16},{1,9},{9,1},{17,25},{25,17},{2,10},{10... | collective-permute-start | bytes 884744 | tf_op jit(solution)/shard_map/ppermute | solution.py:336
  154.2 10.0 %collective-permute-start.46 = (bf16[256,768]{1,0:T(8,128)(2,1)S(1)}, bf16[256,768]{1,0:T(8,128)(2,1)S(1)}, u32[]{:S(2)}, u32[]{:S(2)}) collective-permute-start(bf16[256,768]{1,0:T(8,128)(2,1)S(1)} %get-tuple-element.244), channel_id=1, source_target_pairs={{0,1},{1,0},{2,3},{3,2},{4,5},{5,4},{6,7},{7,6},{8,9},{9,8},{10,11... | collective-permute-start | bytes 1179656 | tf_op jit(solution)/shard_map/ppermute | solution.py:336
  155.2 21.6 %collective-permute-start.52 = (bf16[4,120,768]{2,1,0:T(8,128)(2,1)S(1)}, bf16[4,120,768]{2,1,0:T(8,128)(2,1)S(1)}, u32[]{:S(2)}, u32[]{:S(2)}) collective-permute-start(bf16[4,120,768]{2,1,0:T(8,128)(2,1)S(1)} %get-tuple-element.235), channel_id=1, source_target_pairs={{0,4},{4,0},{1,5},{5,1},{2,6},{6,2},{3,7},{7,3},{8,12},{12,8},{9,1... | collective-permute-start | bytes 2211848 | tf_op jit(solution)/shard_map/ppermute | solution.py:336
  156.5 20.3 %collective-permute-start.53 = (bf16[4,120,768]{2,1,0:T(8,128)(2,1)S(1)}, bf16[4,120,768]{2,1,0:T(8,128)(2,1)S(1)}, u32[]{:S(2)}, u32[]{:S(2)}) collective-permute-start(bf16[4,120,768]{2,1,0:T(8,128)(2,1)S(1)} %get-tuple-element.236), channel_id=1, source_target_pairs={{0,2},{2,0},{1,3},{3,1},{4,6},{6,4},{5,7},{7,5},{8,10},{10,8},{9,1... | collective-permute-start | bytes 2211848 | tf_op jit(solution)/shard_map/ppermute | solution.py:336
  163.7 3.4 %collective-permute-start.48 = (bf16[256,768]{1,0:T(8,128)(2,1)S(1)}, bf16[256,768]{1,0:T(8,128)(2,1)S(1)}, u32[]{:S(2)}, u32[]{:S(2)}) collective-permute-start(bf16[256,768]{1,0:T(8,128)(2,1)S(1)} %get-tuple-element.249), channel_id=1, source_target_pairs={{0,1},{1,0},{2,3},{3,2},{4,5},{5,4},{6,7},{7,6},{8,9},{9,8},{10,11... | collective-permute-start | bytes 1179656 | tf_op jit(solution)/shard_map/ppermute | solution.py:336
  164.2 3.4 %collective-permute-start.49 = (bf16[256,768]{1,0:T(8,128)(2,1)S(1)}, bf16[256,768]{1,0:T(8,128)(2,1)S(1)}, u32[]{:S(2)}, u32[]{:S(2)}) collective-permute-start(bf16[256,768]{1,0:T(8,128)(2,1)S(1)} %get-tuple-element.250), channel_id=1, source_target_pairs={{0,1},{1,0},{2,3},{3,2},{4,5},{5,4},{6,7},{7,6},{8,9},{9,8},{10,11... | collective-permute-start | bytes 1179656 | tf_op jit(solution)/shard_map/ppermute | solution.py:336
  165.4 7.7 %collective-permute-start.55 = (bf16[96,768]{1,0:T(8,128)(2,1)S(1)}, bf16[96,768]{1,0:T(8,128)(2,1)S(1)}, u32[]{:S(2)}, u32[]{:S(2)}) collective-permute-start(bf16[96,768]{1,0:T(8,128)(2,1)S(1)} %get-tuple-element.267), channel_id=1, source_target_pairs={{0,8},{8,0},{16,24},{24,16},{1,9},{9,1},{17,25},{25,17},{2,10},{10... | collective-permute-start | bytes 442376 | tf_op jit(solution)/shard_map/ppermute | solution.py:336
  167.1 9.7 %collective-permute-start.54 = (bf16[96,768]{1,0:T(8,128)(2,1)S(1)}, bf16[96,768]{1,0:T(8,128)(2,1)S(1)}, u32[]{:S(2)}, u32[]{:S(2)}) collective-permute-start(bf16[96,768]{1,0:T(8,128)(2,1)S(1)} %get-tuple-element.256), channel_id=1, source_target_pairs={{0,16},{8,24},{16,0},{24,8},{1,17},{9,25},{17,1},{25,9},{2,18},{10... | collective-permute-start | bytes 442376 | tf_op jit(solution)/shard_map/ppermute | solution.py:336
  176.8 4.0 %collective-permute-start.56 = (bf16[16,80,768]{2,1,0:T(8,128)(2,1)S(1)}, bf16[16,80,768]{2,1,0:T(8,128)(2,1)S(1)}, u32[]{:S(2)}, u32[]{:S(2)}) collective-permute-start(bf16[16,80,768]{2,1,0:T(8,128)(2,1)S(1)} %get-tuple-element.270), channel_id=1, source_target_pairs={{0,1},{1,0},{2,3},{3,2},{4,5},{5,4},{6,7},{7,6},{8,9},{9,8},{10,11... | collective-permute-start | bytes 5898248 | tf_op jit(solution)/shard_map/ppermute | solution.py:336
  181.5 8.1 %collective-permute-start.57 = (bf16[4,40,768]{2,1,0:T(8,128)(2,1)S(1)}, bf16[4,40,768]{2,1,0:T(8,128)(2,1)S(1)}, u32[]{:S(2)}, u32[]{:S(2)}) collective-permute-start(bf16[4,40,768]{2,1,0:T(8,128)(2,1)S(1)} %get-tuple-element.271), channel_id=1, source_target_pairs={{0,2},{2,0},{1,3},{3,1},{4,6},{6,4},{5,7},{7,5},{8,10},{10,8},{9,1... | collective-permute-start | bytes 737288 | tf_op jit(solution)/shard_map/ppermute | solution.py:336
  182.8 7.7 %collective-permute-start.58 = (bf16[4,40,768]{2,1,0:T(8,128)(2,1)S(1)}, bf16[4,40,768]{2,1,0:T(8,128)(2,1)S(1)}, u32[]{:S(2)}, u32[]{:S(2)}) collective-permute-start(bf16[4,40,768]{2,1,0:T(8,128)(2,1)S(1)} %get-tuple-element.272), channel_id=1, source_target_pairs={{0,4},{4,0},{1,5},{5,1},{2,6},{6,2},{3,7},{7,3},{8,12},{12,8},{9,1... | collective-permute-start | bytes 737288 | tf_op jit(solution)/shard_map/ppermute | solution.py:336
  184.8 15.4 %collective-permute-start.63 = (bf16[120,768]{1,0:T(8,128)(2,1)S(1)}, bf16[120,768]{1,0:T(8,128)(2,1)S(1)}, u32[]{:S(2)}, u32[]{:S(2)}) collective-permute-start(bf16[120,768]{1,0:T(8,128)(2,1)S(1)} %get-tuple-element.274), channel_id=1, source_target_pairs={{0,8},{8,0},{16,24},{24,16},{1,9},{9,1},{17,25},{25,17},{2,10},{10... | collective-permute-start | bytes 552968 | tf_op jit(solution)/shard_map/ppermute | solution.py:336
  185.1 16.2 %collective-permute-start.64 = (bf16[120,768]{1,0:T(8,128)(2,1)S(1)}, bf16[120,768]{1,0:T(8,128)(2,1)S(1)}, u32[]{:S(2)}, u32[]{:S(2)}) collective-permute-start(bf16[120,768]{1,0:T(8,128)(2,1)S(1)} %get-tuple-element.275), channel_id=1, source_target_pairs={{0,16},{8,24},{16,0},{24,8},{1,17},{9,25},{17,1},{25,9},{2,18},{10... | collective-permute-start | bytes 552968 | tf_op jit(solution)/shard_map/ppermute | solution.py:336
  186.7 14.6 %collective-permute-start.65 = (bf16[120,768]{1,0:T(8,128)(2,1)S(1)}, bf16[120,768]{1,0:T(8,128)(2,1)S(1)}, u32[]{:S(2)}, u32[]{:S(2)}) collective-permute-start(bf16[120,768]{1,0:T(8,128)(2,1)S(1)} %get-tuple-element.276), channel_id=1, source_target_pairs={{0,24},{8,16},{16,8},{24,0},{1,25},{9,17},{17,9},{25,1},{2,26},{10... | collective-permute-start | bytes 552968 | tf_op jit(solution)/shard_map/ppermute | solution.py:336
  191.4 16.3 %collective-permute-start.59 = (bf16[4,80,768]{2,1,0:T(8,128)(2,1)S(1)}, bf16[4,80,768]{2,1,0:T(8,128)(2,1)S(1)}, u32[]{:S(2)}, u32[]{:S(2)}) collective-permute-start(bf16[4,80,768]{2,1,0:T(8,128)(2,1)S(1)} %get-tuple-element.279), channel_id=1, source_target_pairs={{0,4},{4,0},{1,5},{5,1},{2,6},{6,2},{3,7},{7,3},{8,12},{12,8},{9,1... | collective-permute-start | bytes 1474568 | tf_op jit(solution)/shard_map/ppermute | solution.py:336
  192.2 15.5 %collective-permute-start.60 = (bf16[4,80,768]{2,1,0:T(8,128)(2,1)S(1)}, bf16[4,80,768]{2,1,0:T(8,128)(2,1)S(1)}, u32[]{:S(2)}, u32[]{:S(2)}) collective-permute-start(bf16[4,80,768]{2,1,0:T(8,128)(2,1)S(1)} %get-tuple-element.280), channel_id=1, source_target_pairs={{0,2},{2,0},{1,3},{3,1},{4,6},{6,4},{5,7},{7,5},{8,10},{10,8},{9,1... | collective-permute-start | bytes 1474568 | tf_op jit(solution)/shard_map/ppermute | solution.py:336
  201.9 4.4 %collective-permute-start.61 = (bf16[48,768]{1,0:T(8,128)(2,1)S(1)}, bf16[48,768]{1,0:T(8,128)(2,1)S(1)}, u32[]{:S(2)}, u32[]{:S(2)}) collective-permute-start(bf16[48,768]{1,0:T(8,128)(2,1)S(1)} %get-tuple-element.285), channel_id=1, source_target_pairs={{0,2},{2,0},{1,3},{3,1},{4,6},{6,4},{5,7},{7,5},{8,10},{10,8},{9,1... | collective-permute-start | bytes 221192 | tf_op jit(solution)/shard_map/ppermute | solution.py:336
  203.3 4.4 %collective-permute-start.62 = (bf16[48,768]{1,0:T(8,128)(2,1)S(1)}, bf16[48,768]{1,0:T(8,128)(2,1)S(1)}, u32[]{:S(2)}, u32[]{:S(2)}) collective-permute-start(bf16[48,768]{1,0:T(8,128)(2,1)S(1)} %get-tuple-element.286), channel_id=1, source_target_pairs={{0,4},{4,0},{1,5},{5,1},{2,6},{6,2},{3,7},{7,3},{8,12},{12,8},{9,1... | collective-permute-start | bytes 221192 | tf_op jit(solution)/shard_map/ppermute | solution.py:336
  208.6 8.7 %collective-permute-start.66 = (bf16[80,768]{1,0:T(8,128)(2,1)S(1)}, bf16[80,768]{1,0:T(8,128)(2,1)S(1)}, u32[]{:S(2)}, u32[]{:S(2)}) collective-permute-start(bf16[80,768]{1,0:T(8,128)(2,1)S(1)} %get-tuple-element.294), channel_id=1, source_target_pairs={{0,8},{8,0},{16,24},{24,16},{1,9},{9,1},{17,25},{25,17},{2,10},{10... | collective-permute-start | bytes 368648 | tf_op jit(solution)/shard_map/ppermute | solution.py:336
  211.9 9.6 %collective-permute-start.67 = (bf16[80,768]{1,0:T(8,128)(2,1)S(1)}, bf16[80,768]{1,0:T(8,128)(2,1)S(1)}, u32[]{:S(2)}, u32[]{:S(2)}) collective-permute-start(bf16[80,768]{1,0:T(8,128)(2,1)S(1)} %get-tuple-element.295), channel_id=1, source_target_pairs={{0,16},{8,24},{16,0},{24,8},{1,17},{9,25},{17,1},{25,9},{2,18},{10... | collective-permute-start | bytes 368648 | tf_op jit(solution)/shard_map/ppermute | solution.py:336
  211.9 9.6 %collective-permute-start.68 = (bf16[80,768]{1,0:T(8,128)(2,1)S(1)}, bf16[80,768]{1,0:T(8,128)(2,1)S(1)}, u32[]{:S(2)}, u32[]{:S(2)}) collective-permute-start(bf16[80,768]{1,0:T(8,128)(2,1)S(1)} %get-tuple-element.296), channel_id=1, source_target_pairs={{0,24},{8,16},{16,8},{24,0},{1,25},{9,17},{17,9},{25,1},{2,26},{10... | collective-permute-start | bytes 368648 | tf_op jit(solution)/shard_map/ppermute | solution.py:336
  (32 other events, 429.4 us)
